TPU v7x, 256 devices: a whole 4x4x8 slice. The times are simulated.
256 devices in a mesh: dp: 16 (over y, z_hi, core), mp: 16 (over x, z_lo).
Axes of the slice: x: 4, y: 4, z: 8 (z_hi: 2, z_lo: 4; z = z_hi * 4 + z_lo), core: 2. Of those that a mesh axis runs over, the one named last changes fastest.
Arguments:
- skip_stream_arriving: float32 [4096, 2304], P('dp', 'mp'), may hold values from -170 to 170
- chosen_specialists: int32 [4096, 2], P('dp'), may hold values from 0 to 3, all different within a row; in each aligned block of 256 rows (0 to 255, 256 to 511, ...) at most 160 rows name the same one
- sequence_piece_tallies: int32 [16, 4], P('dp'), may hold values from 1 to 128, 256 in all within a row
- premix_rmsnorm_gain: float32 [2304], P('mp'), may hold values from 0.1 to 1.9
- dispatcher_weights: bfloat16 [2304, 4], replicated, may hold values from -0.125 to 0.125
- specialist_switch_weights: bfloat16 [4, 2304, 5760], P(None, 'dp', 'mp'), may hold values from -0.125 to 0.125
- specialist_expand_weights: bfloat16 [4, 2304, 5760], P(None, 'dp', 'mp'), may hold values from -0.125 to 0.125
- specialist_contract_weights: bfloat16 [4, 5760, 2304], P(None, 'mp', 'dp'), may hold values from -0.109375 to 0.109375
- terminal_rmsnorm_gain: float32 [2304], replicated, may hold values from 0.1 to 1.9
- lexicon_projector_weights: bfloat16 [2304, 131072], P(None, ('dp', 'mp')), may hold values from -12 to 12
- softness_per_sequence: float32 [64], replicated, may hold values from 0.02 to 1.5
Outputs:
- new_hidden: float32 [4096, 2304], P('dp', 'mp')
- logprobs: float32 [64, 131072], P(None, ('dp', 'mp'))
Inputs may be any that keep to these rules, and one draw needn't show every extreme that they name: `chosen_specialists`: in the 256 rows of each data group no expert is named by more than 160 rows, a bound that some block reaches. `sequence_piece_tallies`: each row sums to 256; its largest entry is 128.
All inputs are finite; a program needn't handle non-finite values.
Results may differ from a plain program's by a relative error of at most 0.0014.
Values may be sent and summed in bfloat16 or wider, within the bound.
A program may use at most 128 MiB of HBM per device.

v0:
```python
import math

import jax
import jax.numpy as jnp
from jax import lax
from jax.experimental import pallas as pl
from jax.experimental.pallas import tpu as pltpu
from jax.sharding import PartitionSpec as P

EMBED_DIMENSION = 2304


branch_scale = 1.4 / math.sqrt(40.0)
epsilon = 1e-05


def axis_gather(block, axis, count, tag):
    def kernel(x_ref, out_ref, send_sem, recv_sem):
        me = lax.axis_index(axis)
        barrier = pltpu.get_barrier_semaphore()
        for step in range(1, count):
            peer = lax.rem(me + step, count)
            pl.semaphore_signal(barrier, 1, device_id={axis: peer},
                                device_id_type=pl.DeviceIdType.MESH)
        pl.semaphore_wait(barrier, count - 1)
        copies = []
        for step in range(1, count):
            peer = lax.rem(me + step, count)
            copy = pltpu.make_async_remote_copy(
                src_ref=x_ref, dst_ref=out_ref.at[me],
                send_sem=send_sem.at[step], recv_sem=recv_sem.at[step],
                device_id={axis: peer}, device_id_type=pl.DeviceIdType.MESH)
            copy.start()
            copies.append(copy)
        out_ref[me] = x_ref[...]
        for copy in copies:
            copy.wait_send()
            copy.wait_recv()
    return pl.pallas_call(
        kernel,
        out_shape=jax.ShapeDtypeStruct((count,) + block.shape, block.dtype),
        in_specs=[pl.BlockSpec(memory_space=pltpu.VMEM)],
        out_specs=pl.BlockSpec(memory_space=pltpu.VMEM),
        scratch_shapes=[pltpu.SemaphoreType.DMA((count,)), pltpu.SemaphoreType.DMA((count,))],
        compiler_params=pltpu.CompilerParams(collective_id=tag, has_side_effects=True),
    )(block)


def body(
    skip_stream_arriving,
    chosen_specialists,
    sequence_piece_tallies,
    premix_rmsnorm_gain,
    dispatcher_weights,
    specialist_switch_weights,
    specialist_expand_weights,
    specialist_contract_weights,
    terminal_rmsnorm_gain,
    lexicon_projector_weights,
    softness_per_sequence,
):
    tok_rows = skip_stream_arriving.shape[0]
    experts = specialist_switch_weights.shape[0]
    columns_count = lax.axis_size("mp")
    groups = lax.axis_size("dp")
    local_squares = jnp.sum(skip_stream_arriving * skip_stream_arriving, axis=1)
    squares = jnp.sum(axis_gather(local_squares[None], "mp", columns_count, 0), axis=(0, 1))
    normed_local = (
        skip_stream_arriving
        * lax.rsqrt(squares / EMBED_DIMENSION + epsilon)[:, None]
        * premix_rmsnorm_gain
    ).astype(jnp.bfloat16)
    features = (
        axis_gather(normed_local, "mp", columns_count, 5)
        .transpose(1, 0, 2)
        .reshape(tok_rows, EMBED_DIMENSION)
    )
    router = jnp.dot(features, dispatcher_weights, preferred_element_type=jnp.float32)
    mixing = jax.nn.softmax(jnp.take_along_axis(router, chosen_specialists, axis=1), axis=1)
    all_weights = lax.all_gather(
        jnp.stack(
            [
                specialist_switch_weights,
                specialist_expand_weights,
                jnp.swapaxes(specialist_contract_weights, 1, 2),
            ],
            axis=1,
        ),
        "dp", axis=2, tiled=True,
    )
    combined = jnp.zeros((tok_rows, EMBED_DIMENSION), jnp.float32)
    for expert in range(experts):
        weight = jnp.where(chosen_specialists[:, 0] == expert, mixing[:, 0], 0.0) + jnp.where(
            chosen_specialists[:, 1] == expert, mixing[:, 1], 0.0
        )
        gate = jnp.dot(features, all_weights[expert, 0], preferred_element_type=jnp.float32)
        up_part = jnp.dot(features, all_weights[expert, 1], preferred_element_type=jnp.float32)
        act = (jax.nn.silu(gate) * up_part).astype(jnp.bfloat16)
        down = lax.dot_general(
            act, all_weights[expert, 2], (((1,), (1,)), ((), ())),
            preferred_element_type=jnp.float32,
        )
        combined = combined + down * weight[:, None]
    ends_index = jnp.cumsum(sequence_piece_tallies[0], dtype=jnp.int32) - 1
    partial_rows = combined.astype(jnp.bfloat16)
    branch = lax.psum_scatter(partial_rows, "mp", scatter_dimension=1, tiled=True).astype(jnp.float32)
    new_hidden = skip_stream_arriving + branch_scale * branch
    skip_ends = (
        axis_gather(skip_stream_arriving[ends_index], "mp", columns_count, 6)
        .transpose(1, 0, 2)
        .reshape(ends_index.shape[0], EMBED_DIMENSION)
    )
    end_partials = axis_gather(partial_rows[ends_index], "mp", columns_count, 1)
    end_rows = skip_ends + branch_scale * jnp.sum(end_partials.astype(jnp.float32), axis=0)
    end_squares = jnp.sum(end_rows * end_rows, axis=1)
    end_normed = (
        end_rows * lax.rsqrt(end_squares / EMBED_DIMENSION + epsilon)[:, None] * terminal_rmsnorm_gain
    ).astype(jnp.bfloat16)
    lexicon_projector_feed = axis_gather(end_normed, "dp", groups, 2).reshape(
        groups * end_normed.shape[0], EMBED_DIMENSION
    )
    lexicon_logit_values = jnp.dot(
        lexicon_projector_feed, lexicon_projector_weights, preferred_element_type=jnp.float32
    ) / (EMBED_DIMENSION / 256.0 * softness_per_sequence[:, None])
    local_max = jnp.max(lexicon_logit_values, axis=1)
    local_sum = jnp.sum(jnp.exp(lexicon_logit_values - local_max[:, None]), axis=1)
    stats = jnp.stack([local_max, local_sum])
    for axis, count, tag in (("mp", columns_count, 3), ("dp", groups, 4)):
        held = axis_gather(stats, axis, count, tag)
        top = jnp.max(held[:, 0], axis=0)
        stats = jnp.stack([top, jnp.sum(held[:, 1] * jnp.exp(held[:, 0] - top[None]), axis=0)])
    largest, total_exp = stats[0], stats[1]
    logprobs = lexicon_logit_values - largest[:, None] - jnp.log(total_exp)[:, None]
    return (new_hidden, logprobs)


def solution(mesh):
    return jax.shard_map(
        body,
        mesh=mesh,
        in_specs=(
            P("dp", "mp"),
            P("dp", None),
            P("dp", None),
            P("mp"),
            P(),
            P(None, "dp", "mp"),
            P(None, "dp", "mp"),
            P(None, "mp", "dp"),
            P(),
            P(None, ("dp", "mp")),
            P(),
        ),
        out_specs=(P("dp", "mp"), P(None, ("dp", "mp"))),
        check_vma=False,
    )
```

profile of v0, /device:TPU:8, one launch (start us, length us, event | category | flops | bytes accessed | tf_op | source)
XLA Modules:
  0.0 400.3 jit_solution(18230711120667831225)
XLA Ops:
  7.2 0.0 copy-start
  7.2 0.0 all-gather.2.cloned.1.call-start
  7.2 0.0 copy-start.3
  7.2 0.0 copy-start.9
  7.2 2.8 pad_maximum_fusion
  10.0 0.0 all-gather.2.cloned.1.call-update
  10.0 0.0 reduce-scatter.4.cloned.1.call-start
  10.1 0.0 copy-done.3
  10.1 0.1 copy.116
  10.2 0.0 copy-start.1
  10.2 0.6 multiply_reduce_fusion
  10.9 11.5 %shard_map.122 = f32[16,1,256]{2,1,0:T(1,128)} custom-call(f32[1,256]{1,0:T(1,128)} %bitcast.131), custom_call_target="tpu_custom_call" | custom-call | tf_op jit(solution)/shard_map/pallas_call | solution.py:39
  22.4 0.8 reduce_sum.73
  23.2 0.0 copy-done.9
  23.2 0.8 multiply_convert_fusion.x_ref
  23.9 78.4 %shard_map.123 = bf16[16,256,144]{2,1,0:T(8,128)(2,1)} custom-call(bf16[256,144]{1,0:T(8,128)(2,1)} %multiply_convert_fusion.x_ref), custom_call_target="tpu_custom_call" | custom-call | tf_op jit(solution)/shard_map/pallas_call | solution.py:39
  102.4 0.0 copy-start.6
  102.4 3.1 copy.113
  105.5 0.8 copy.114
  106.3 1.1 reshape.92
  107.4 1.0 fusion.61
  108.4 5.1 %gather_fusion.2 = f32[512]{0:T(512)S(1)} fusion(f32[256,4]{0,1:T(4,128)S(1)} %fusion.61, s32[512]{0:T(512)S(1)} %reshape.92), kind=kCustom, calls=%fused_computation.2 | custom fusion | bytes 8192 | tf_op jit(solution)/shard_map/jit(take_along_axis)/gather | solution.py:79
  113.4 0.8 reshape.95
  114.2 1.0 copy.115
  115.2 0.8 reduce-window.4
  116.0 2.1 gather_fusion
  118.1 109.1 %shard_map.124 = f32[16,4,144]{2,1,0:T(4,128)} custom-call(f32[4,144]{1,0:T(4,128)} %gather_fusion), custom_call_target="tpu_custom_call" | custom-call | tf_op jit(solution)/shard_map/pallas_call | solution.py:39
  227.3 1.5 copy.118
  228.8 1.6 reshape.74
  230.4 1.2 broadcast_multiply_fusion.1
  231.6 0.6 fusion.51
  232.1 16.1 %all-gather.2.cloned.1.call-done = bf16[4,3,2304,360]{3,2,0,1:T(8,128)(2,1)} async-done(((bf16[4,3,144,360]{3,2,0,1:T(8,128)(2,1)}), bf16[4,3,2304,360]{3,2,0,1:T(8,128)(2,1)}) %all-gather.2.cloned.1.call-update) | async-done | bytes 19906576 | tf_op jit(solution)/shard_map/all_gather | solution.py:80
  248.2 3.0 fusion.11
  251.2 3.0 fusion.9
  254.2 3.0 fusion.7
  257.2 3.0 fusion.5
  260.3 5.8 %convolution_multiply_fusion.3 = f32[256,2304]{1,0:T(8,128)} fusion(bf16[4,3,2304,360]{3,2,0,1:T(8,128)(2,1)} %all-gather.2.cloned.1.call-done, f32[256]{0:T(256)S(1)} %bitcast.137, bf16[256,2304]{0,1:T(8,128)(2,1)S(1)} %bitcast.112, f32[256,360]{0,1:T(8,128)} %fusion.11), kind=kOutput, calls=%fused_computation.9 | convolution fusion | flops 850489344 | bytes 7447552 | tf_op jit(solution)/shard_map/dot_general | solution.py:99
  266.1 6.6 %fusion.2 = f32[256,2304]{1,0:T(8,128)} fusion(f32[256,2304]{1,0:T(8,128)} %convolution_multiply_fusion.3, bf16[4,3,2304,360]{3,2,0,1:T(8,128)(2,1)} %all-gather.2.cloned.1.call-done, f32[256]{0:T(256)S(1)} %bitcast.133, bf16[256,2304]{0,1:T(8,128)(2,1)S(1)} %bitcast.113, f32[256,360]{0,1:T(8,128)} %fusion.9), kind=kOutput, calls=%fused_computation.8 | convolution fusion | flops 851079168 | bytes 9806848 | tf_op jit(solution)/shard_map/dot_general | solution.py:99
  272.7 6.6 %fusion.1 = f32[256,2304]{1,0:T(8,128)} fusion(f32[256,2304]{1,0:T(8,128)} %fusion.2, bf16[4,3,2304,360]{3,2,0,1:T(8,128)(2,1)} %all-gather.2.cloned.1.call-done, f32[256]{0:T(256)S(1)} %bitcast.132, bf16[256,2304]{0,1:T(8,128)(2,1)S(1)} %bitcast.114, f32[256,360]{0,1:T(8,128)} %fusion.7), kind=kOutput, calls=%fused_computation.6 | convolution fusion | flops 851079168 | bytes 9806848 | tf_op jit(solution)/shard_map/dot_general | solution.py:99
  279.3 0.0 copy-done.10
  279.3 6.1 %fusion.3 = bf16[256,2304]{1,0:T(8,128)(2,1)} fusion(f32[256,2304]{1,0:T(8,128)} %fusion.1, bf16[4,3,2304,360]{3,2,0,1:T(8,128)(2,1)} %all-gather.2.cloned.1.call-done, f32[256]{0:T(256)S(1)} %bitcast.136, bf16[256,2304]{0,1:T(8,128)(2,1)S(1)} %bitcast.115, f32[256,360]{0,1:T(8,128)} %fusion.5), kind=kOutput, calls=%fused_computation.10 | convolution fusion | flops 851668992 | bytes 8627200 | tf_op jit(solution)/shard_map/dot_general | solution.py:99
  285.4 2.6 gather_fusion.1
  288.0 2.4 copy.123
  290.4 14.1 %shard_map.125 = bf16[16,4,2304]{2,1,0:T(4,128)(2,1)} custom-call(bf16[4,2304]{1,0:T(4,128)(2,1)} %gather_fusion.1), custom_call_target="tpu_custom_call" | custom-call | tf_op jit(solution)/shard_map/pallas_call | solution.py:39
  304.5 1.1 convert_reduce_fusion
  305.6 0.1 mul.162
  305.7 0.2 fusion.45
  305.9 0.0 reduce-scatter.4.cloned.1.call-update
  306.0 0.7 multiply_convert_fusion.1.x_ref
  306.7 15.1 %shard_map.126 = bf16[16,4,2304]{2,1,0:T(4,128)(2,1)} custom-call(bf16[4,2304]{1,0:T(4,128)(2,1)} %multiply_convert_fusion.1.x_ref), custom_call_target="tpu_custom_call" | custom-call | tf_op jit(solution)/shard_map/pallas_call | solution.py:39
  321.8 1.0 reshape.75
  322.8 0.6 fusion.60
  323.5 0.2 exponential_reduce_fusion
  323.7 0.6 pad_maximum_fusion.1.x_ref
  324.2 10.2 %shard_map.127 = f32[16,2,64]{2,1,0:T(2,128)} custom-call(f32[2,64]{1,0:T(2,128)} %pad_maximum_fusion.1.x_ref), custom_call_target="tpu_custom_call" | custom-call | tf_op jit(solution)/shard_map/pallas_call | solution.py:39
  334.4 0.8 fusion.59
  335.3 0.6 pad_maximum_fusion.2.x_ref
  335.9 11.7 %shard_map.128 = f32[16,2,64]{2,1,0:T(2,128)} custom-call(f32[2,64]{1,0:T(2,128)} %pad_maximum_fusion.2.x_ref), custom_call_target="tpu_custom_call" | custom-call | tf_op jit(solution)/shard_map/pallas_call | solution.py:39
  347.6 0.8 fusion.58
  348.4 0.8 subtract_subtract_fusion
  349.2 42.5 %reduce-scatter.4.cloned.1.call-done = bf16[144,256]{1,0:T(8,128)(2,1)} async-done(((bf16[2304,256]{1,0:T(8,128)(2,1)}), bf16[144,256]{1,0:T(8,128)(2,1)}) %reduce-scatter.4.cloned.1.call-update) | async-done | bytes 73744
  391.6 1.0 copy.124
  392.6 0.0 copy-done.2
  392.7 0.8 copy.122
  (32 shorter events, 0.3 us)
Async XLA Ops:
  7.2 315.6 %copy-start = (bf16[2304,512]{1,0:T(8,128)(2,1)S(1)}, bf16[2304,512]{1,0:T(8,128)(2,1)}, u32[]{:S(2)}) copy-start(bf16[2304,512]{1,0:T(8,128)(2,1)} %param.20) | copy-start | bytes 7077892
  7.2 241.1 %all-gather.2.cloned.1.call-start = ((), (), s32[]{:S(2)}) async-start(), calls=%async_computation.1 | async-start | bytes 22560768 | tf_op jit(solution)/shard_map/all_gather | solution.py:80
  7.2 2.9 copy-start.3
  7.2 15.9 %copy-start.9 = (f32[144]{0:T(256)S(1)}, f32[144]{0:T(256)}, u32[]{:S(2)}) copy-start(f32[144]{0:T(256)} %param.14) | copy-start | bytes 1732
  10.0 381.6 %reduce-scatter.4.cloned.1.call-start = ((), (), s32[]{:S(2)}) async-start(), calls=%async_computation.2 | async-start | bytes 1253376
  10.2 92.1 %copy-start.1 = (f32[256,144]{1,0:T(8,128)}, f32[256,144]{1,0:T(8,128)S(1)}, u32[]{:S(2)}) copy-start(f32[256,144]{1,0:T(8,128)S(1)} %copy.116) | copy-start | bytes 442372
  102.4 3.1 copy-start.6
  257.2 3.0 copy-start.11
  260.3 5.8 %copy-start.8 = (f32[256,1]{0,1:T(1,128)S(1)}, f32[256,1]{0,1:T(1,128)}, u32[]{:S(2)}) copy-start(f32[256,1]{0,1:T(1,128)} %get-tuple-element.21) | copy-start | bytes 3076
  272.7 6.6 %copy-start.10 = (f32[256,1]{0,1:T(1,128)S(1)}, f32[256,1]{0,1:T(1,128)}, u32[]{:S(2)}) copy-start(f32[256,1]{0,1:T(1,128)} %get-tuple-element.18) | copy-start | bytes 3076
  285.4 20.3 %copy-start.4 = (f32[16,4,144]{2,1,0:T(4,128)S(1)}, f32[16,4,144]{2,1,0:T(4,128)}, u32[]{:S(2)}) copy-start(f32[16,4,144]{2,1,0:T(4,128)} %shard_map.124) | copy-start | bytes 110596
  288.0 17.9 %copy-start.5 = (f32[4,2304]{1,0:T(4,128)S(1)}, f32[4,2304]{1,0:T(4,128)}, u32[]{:S(2)}) copy-start(f32[4,2304]{1,0:T(4,128)} %reshape.74) | copy-start | bytes 110596
  288.0 17.9 %copy-start.7 = (f32[2304]{0:T(1024)S(1)}, f32[2304]{0:T(1024)}, u32[]{:S(2)}) copy-start(f32[2304]{0:T(1024)} %param.19) | copy-start | bytes 27652
  290.4 32.4 %copy-start.12 = (f32[64]{0:T(128)S(1)}, f32[64]{0:T(128)}, u32[]{:S(2)}) copy-start(f32[64]{0:T(128)} %broadcast_multiply_fusion.1) | copy-start | bytes 772
  322.8 69.8 %copy-start.2 = (f32[256,144]{1,0:T(8,128)S(1)}, f32[256,144]{1,0:T(8,128)}, u32[]{:S(2)}) copy-start(f32[256,144]{1,0:T(8,128)} %copy-done.1) | copy-start | bytes 442372
Sparse Core Ops, SparseCore 0:
  10.7 237.5 all-gather.1
  306.1 85.5 reduce-scatter.3
where the time goes:
time: 401 us; the launch traced here: 400 us
  Pallas kernels  250 us (62%)
  waiting for transfers between devices  58.6 us (15%)
  matrix products  38.7 us (10%)
  local copies, waits for them, and re-layouts  26.7 us (7%)
  between operations  14.3 us (4%)
  other arithmetic  11.8 us (3%)
    pallas_call x7, Pallas kernels, axis_gather(): pl.pallas_call(kernel, out_shape=jax.ShapeDtypeStruct((count,) + block.sh...  250 us
    unnamed x3, waiting for transfers between devices  42.5 us
    dot_general x4, matrix products, body(): lax.dot_general(act, all_weights[expert, 2], (((1,), (1,)), ((), ())), pr...  25.1 us
    all_gather x1, waiting for transfers between devices, body(): lax.all_gather(jnp.stack([specialist_switch_weights, specialist_expand_we...  16.1 us
    dot_general x4, matrix products, body(): jnp.dot(features, all_weights[expert, 0], preferred_element_type=jnp.floa...  12 us
    gather x5, local copies, waits for them, and re-layouts, body(): jnp.take_along_axis(router, chosen_specialists, axis=1)  8.73 us
  transfers between devices with their start and end apart: 2, of which 2 were waited for; matrix products, arithmetic and copies ran while one was open for 7% of the time, Pallas kernels for 59%

commit v1 on v0

--- a/solution.py
+++ b/solution.py
@@ -44,6 +44,38 @@
         scratch_shapes=[pltpu.SemaphoreType.DMA((count,)), pltpu.SemaphoreType.DMA((count,))],
         compiler_params=pltpu.CompilerParams(collective_id=tag, has_side_effects=True),
     )(block)
+
+
+def axis_exchange(blocks, axis, count, tag):
+    def kernel(x_ref, out_ref, send_sem, recv_sem):
+        me = lax.axis_index(axis)
+        barrier = pltpu.get_barrier_semaphore()
+        for step in range(1, count):
+            peer = lax.rem(me + step, count)
+            pl.semaphore_signal(barrier, 1, device_id={axis: peer},
+                                device_id_type=pl.DeviceIdType.MESH)
+        pl.semaphore_wait(barrier, count - 1)
+        copies = []
+        for step in range(1, count):
+            peer = lax.rem(me + step, count)
+            copy = pltpu.make_async_remote_copy(
+                src_ref=x_ref.at[peer], dst_ref=out_ref.at[me],
+                send_sem=send_sem.at[step], recv_sem=recv_sem.at[step],
+                device_id={axis: peer}, device_id_type=pl.DeviceIdType.MESH)
+            copy.start()
+            copies.append(copy)
+        out_ref[me] = x_ref[me]
+        for copy in copies:
+            copy.wait_send()
+            copy.wait_recv()
+    return pl.pallas_call(
+        kernel,
+        out_shape=jax.ShapeDtypeStruct(blocks.shape, blocks.dtype),
+        in_specs=[pl.BlockSpec(memory_space=pltpu.VMEM)],
+        out_specs=pl.BlockSpec(memory_space=pltpu.VMEM),
+        scratch_shapes=[pltpu.SemaphoreType.DMA((count,)), pltpu.SemaphoreType.DMA((count,))],
+        compiler_params=pltpu.CompilerParams(collective_id=tag, has_side_effects=True),
+    )(blocks)
 
 
 def body(
@@ -103,7 +135,10 @@
         combined = combined + down * weight[:, None]
     ends_index = jnp.cumsum(sequence_piece_tallies[0], dtype=jnp.int32) - 1
     partial_rows = combined.astype(jnp.bfloat16)
-    branch = lax.psum_scatter(partial_rows, "mp", scatter_dimension=1, tiled=True).astype(jnp.float32)
+    column_blocks = partial_rows.reshape(tok_rows, columns_count, -1).transpose(1, 0, 2)
+    branch = jnp.sum(
+        axis_exchange(column_blocks, "mp", columns_count, 7).astype(jnp.float32), axis=0
+    )
     new_hidden = skip_stream_arriving + branch_scale * branch
     skip_ends = (
         axis_gather(skip_stream_arriving[ends_index], "mp", columns_count, 6)

time: 401 us -> 425 us (1.060)
  Pallas kernels: 250 us -> 301 us
  waiting for transfers between devices: 58.6 us -> 16 us
  other arithmetic: 11.8 us -> 20.1 us
  local copies, waits for them, and re-layouts: 26.7 us -> 31.1 us
    pallas_call x0 -> x1, Pallas kernels: none -> 50.5 us  [axis_exchange(): pl.pallas_call(kernel, out_shape=jax.ShapeDtypeStruct(blocks.shape, block...]
    unnamed x3 -> x1, waiting for transfers between devices: 42.5 us -> 0.02 us
  transfers between devices with their start and end apart: 2 -> 1, of which waited for: 2 -> 1; matrix products, arithmetic and copies ran while one was open for 7% -> 5% of each run, Pallas kernels for 59% -> 47%
where the time goes in v1:
time: 425 us; the launch traced here: 422 us
  Pallas kernels  301 us (71%)
  matrix products  39.7 us (9%)
  local copies, waits for them, and re-layouts  31.1 us (7%)
  other arithmetic  20.1 us (5%)
  waiting for transfers between devices  16 us (4%)
  between operations  14.3 us (3%)
    pallas_call x7, Pallas kernels, axis_gather(): pl.pallas_call(kernel, out_shape=jax.ShapeDtypeStruct((count,) + block.sh...  250 us
    pallas_call x1, Pallas kernels, axis_exchange(): pl.pallas_call(kernel, out_shape=jax.ShapeDtypeStruct(blocks.shape, block...  50.5 us
    dot_general x4, matrix products, body(): lax.dot_general(act, all_weights[expert, 2], (((1,), (1,)), ((), ())), pr...  25.1 us
    all_gather x1, waiting for transfers between devices, body(): lax.all_gather(jnp.stack([specialist_switch_weights, specialist_expand_we...  16 us
    dot_general x4, matrix products, body(): jnp.dot(features, all_weights[expert, 0], preferred_element_type=jnp.floa...  12 us
    gather x5, local copies, waits for them, and re-layouts, body(): jnp.take_along_axis(router, chosen_specialists, axis=1)  8.73 us
  transfers between devices with their start and end apart: 1, of which 1 were waited for; matrix products, arithmetic and copies ran while one was open for 5% of the time, Pallas kernels for 47%

profile of v1, /device:TPU:8, one launch (start us, length us, event | category | flops | bytes accessed | tf_op | source)
XLA Modules:
  0.0 422.0 jit_solution(13636091019876746006)
XLA Ops:
  7.2 0.0 copy-start
  7.2 0.0 all-gather.2.cloned.1.call-start
  7.2 2.8 pad_maximum_fusion
  10.0 0.0 all-gather.2.cloned.1.call-update
  10.1 0.1 copy.118
  10.2 0.6 multiply_reduce_fusion
  10.8 11.5 %shard_map.122 = f32[16,1,256]{2,1,0:T(1,128)} custom-call(f32[1,256]{1,0:T(1,128)} %bitcast.131), custom_call_target="tpu_custom_call" | custom-call | tf_op jit(solution)/shard_map/pallas_call | solution.py:39
  22.3 0.8 reduce_sum.82
  23.1 0.8 multiply_convert_fusion.x_ref
  23.9 78.4 %shard_map.123 = bf16[16,256,144]{2,1,0:T(8,128)(2,1)} custom-call(bf16[256,144]{1,0:T(8,128)(2,1)} %multiply_convert_fusion.x_ref), custom_call_target="tpu_custom_call" | custom-call | tf_op jit(solution)/shard_map/pallas_call | solution.py:39
  102.3 0.0 copy-start.6
  102.3 3.1 copy.113
  105.4 0.8 copy.114
  106.2 1.1 reshape.96
  107.3 1.0 fusion.61
  108.3 5.1 %gather_fusion.2 = f32[512]{0:T(512)S(1)} fusion(f32[256,4]{0,1:T(4,128)S(1)} %fusion.61, s32[512]{0:T(512)S(1)} %reshape.96), kind=kCustom, calls=%fused_computation.2 | custom fusion | bytes 8192 | tf_op jit(solution)/shard_map/jit(take_along_axis)/gather | solution.py:111
  113.4 0.8 reshape.99
  114.2 1.0 copy.115
  115.1 0.8 reduce-window.4
  116.0 2.1 gather_fusion
  118.1 109.1 %shard_map.125 = f32[16,4,144]{2,1,0:T(4,128)} custom-call(f32[4,144]{1,0:T(4,128)} %gather_fusion), custom_call_target="tpu_custom_call" | custom-call | tf_op jit(solution)/shard_map/pallas_call | solution.py:39
  227.2 1.5 copy.120
  228.7 1.6 reshape.78
  230.3 1.2 broadcast_multiply_fusion.1
  231.6 0.6 fusion.51
  232.2 16.0 %all-gather.2.cloned.1.call-done = bf16[4,3,2304,360]{3,2,0,1:T(8,128)(2,1)} async-done(((bf16[4,3,144,360]{3,2,0,1:T(8,128)(2,1)}), bf16[4,3,2304,360]{3,2,0,1:T(8,128)(2,1)}) %all-gather.2.cloned.1.call-update) | async-done | bytes 19906576 | tf_op jit(solution)/shard_map/all_gather | solution.py:112
  248.1 3.0 fusion.11
  251.1 3.0 fusion.9
  254.1 3.0 fusion.7
  257.1 3.0 fusion.5
  260.1 5.8 %convolution_multiply_fusion.3 = f32[256,2304]{1,0:T(8,128)} fusion(bf16[4,3,2304,360]{3,2,0,1:T(8,128)(2,1)} %all-gather.2.cloned.1.call-done, f32[256]{0:T(256)S(1)} %bitcast.137, bf16[256,2304]{0,1:T(8,128)(2,1)S(1)} %bitcast.112, f32[256,360]{0,1:T(8,128)} %fusion.11), kind=kOutput, calls=%fused_computation.9 | convolution fusion | flops 850489344 | bytes 7447552 | tf_op jit(solution)/shard_map/dot_general | solution.py:131
  266.0 6.6 %fusion.2 = f32[256,2304]{1,0:T(8,128)} fusion(f32[256,2304]{1,0:T(8,128)} %convolution_multiply_fusion.3, bf16[4,3,2304,360]{3,2,0,1:T(8,128)(2,1)} %all-gather.2.cloned.1.call-done, f32[256]{0:T(256)S(1)} %bitcast.133, bf16[256,2304]{0,1:T(8,128)(2,1)S(1)} %bitcast.113, f32[256,360]{0,1:T(8,128)} %fusion.9), kind=kOutput, calls=%fused_computation.8 | convolution fusion | flops 851079168 | bytes 9806848 | tf_op jit(solution)/shard_map/dot_general | solution.py:131
  272.6 6.6 %fusion.1 = f32[256,2304]{1,0:T(8,128)} fusion(f32[256,2304]{1,0:T(8,128)} %fusion.2, bf16[4,3,2304,360]{3,2,0,1:T(8,128)(2,1)} %all-gather.2.cloned.1.call-done, f32[256]{0:T(256)S(1)} %bitcast.132, bf16[256,2304]{0,1:T(8,128)(2,1)S(1)} %bitcast.114, f32[256,360]{0,1:T(8,128)} %fusion.7), kind=kOutput, calls=%fused_computation.6 | convolution fusion | flops 851079168 | bytes 9806848 | tf_op jit(solution)/shard_map/dot_general | solution.py:131
  279.1 6.1 %fusion.3 = bf16[256,2304]{1,0:T(8,128)(2,1)} fusion(f32[256,2304]{1,0:T(8,128)} %fusion.1, bf16[4,3,2304,360]{3,2,0,1:T(8,128)(2,1)} %all-gather.2.cloned.1.call-done, f32[256]{0:T(256)S(1)} %bitcast.136, bf16[256,2304]{0,1:T(8,128)(2,1)S(1)} %bitcast.115, f32[256,360]{0,1:T(8,128)} %fusion.5), kind=kOutput, calls=%fused_computation.11 | convolution fusion | flops 851668992 | bytes 8627200 | tf_op jit(solution)/shard_map/dot_general | solution.py:131
  285.3 2.7 gather_fusion.1
  288.0 1.6 copy.116
  289.6 14.3 %shard_map.126 = bf16[16,4,2304]{2,1,0:T(4,128)(2,1)} custom-call(bf16[4,2304]{1,0:T(4,128)(2,1)} %gather_fusion.1), custom_call_target="tpu_custom_call" | custom-call | tf_op jit(solution)/shard_map/pallas_call | solution.py:39
  303.9 1.1 convert_reduce_fusion.1
  305.0 0.6 copy-done.5
  305.6 0.6 broadcast_multiply_fusion
  306.2 1.5 mul.162
  307.7 1.0 fusion.45
  308.8 1.5 multiply_convert_fusion.1.x_ref
  310.2 16.0 %shard_map.127 = bf16[16,4,2304]{2,1,0:T(4,128)(2,1)} custom-call(bf16[4,2304]{1,0:T(4,128)(2,1)} %multiply_convert_fusion.1.x_ref), custom_call_target="tpu_custom_call" | custom-call | tf_op jit(solution)/shard_map/pallas_call | solution.py:39
  326.2 1.7 reshape.79
  328.0 1.6 fusion.60
  329.6 0.0 copy-start.3
  329.6 0.7 copy-done.3
  330.2 0.2 exponential_reduce_fusion
  330.4 0.6 pad_maximum_fusion.1.x_ref
  331.0 9.4 %shard_map.128 = f32[16,2,64]{2,1,0:T(2,128)} custom-call(f32[2,64]{1,0:T(2,128)} %pad_maximum_fusion.1.x_ref), custom_call_target="tpu_custom_call" | custom-call | tf_op jit(solution)/shard_map/pallas_call | solution.py:39
  340.4 0.8 fusion.59
  341.2 0.6 reduce_max.38
  341.8 0.7 multiply_reduce_fusion.2
  342.5 1.3 pad_maximum_fusion.2.x_ref
  343.8 11.5 %shard_map.129 = f32[16,2,64]{2,1,0:T(2,128)} custom-call(f32[2,64]{1,0:T(2,128)} %pad_maximum_fusion.2.x_ref), custom_call_target="tpu_custom_call" | custom-call | tf_op jit(solution)/shard_map/pallas_call | solution.py:39
  355.3 0.8 fusion.58
  356.1 0.5 reduce_max.39
  356.6 0.7 multiply_reduce_fusion.1
  357.3 1.7 subtract_subtract_fusion
  359.0 2.8 copy.117
  361.7 50.5 %shard_map.124 = bf16[16,256,144]{2,1,0:T(8,128)(2,1)} custom-call(bf16[16,256,144]{2,1,0:T(8,128)(2,1)} %bitcast.117), custom_call_target="tpu_custom_call" | custom-call | tf_op jit(solution)/shard_map/pallas_call | solution.py:71
  412.3 2.0 convert_reduce_fusion
  414.4 0.8 copy.124
  (31 shorter events, 0.2 us)
Async XLA Ops:
  7.2 320.8 %copy-start = (bf16[2304,512]{1,0:T(8,128)(2,1)S(1)}, bf16[2304,512]{1,0:T(8,128)(2,1)}, u32[]{:S(2)}) copy-start(bf16[2304,512]{1,0:T(8,128)(2,1)} %param.20) | copy-start | bytes 7077892
  7.2 240.9 %all-gather.2.cloned.1.call-start = ((), (), s32[]{:S(2)}) async-start(), calls=%async_computation | async-start | bytes 22560768 | tf_op jit(solution)/shard_map/all_gather | solution.py:112
  7.2 2.8 copy-start.4
  7.2 15.9 %copy-start.9 = (f32[144]{0:T(256)S(1)}, f32[144]{0:T(256)}, u32[]{:S(2)}) copy-start(f32[144]{0:T(256)} %param.14) | copy-start | bytes 1732
  10.2 92.1 %copy-start.1 = (f32[256,144]{1,0:T(8,128)}, f32[256,144]{1,0:T(8,128)S(1)}, u32[]{:S(2)}) copy-start(f32[256,144]{1,0:T(8,128)S(1)} %copy.118) | copy-start | bytes 442372
  102.3 3.1 copy-start.6
  116.0 112.7 %copy-start.8 = (s32[1024]{0:T(1024)}, s32[1024]{0:T(1024)S(1)}, u32[]{:S(2)}) copy-start(s32[1024]{0:T(1024)S(1)} %pad_clamp_fusion) | copy-start | bytes 12292
  257.1 3.0 copy-start.11
  272.5 6.6 %copy-start.10 = (f32[256,1]{0,1:T(1,128)S(1)}, f32[256,1]{0,1:T(1,128)}, u32[]{:S(2)}) copy-start(f32[256,1]{0,1:T(1,128)} %get-tuple-element.12) | copy-start | bytes 3076
  285.3 23.5 %copy-start.7 = (f32[2304]{0:T(1024)S(1)}, f32[2304]{0:T(1024)}, u32[]{:S(2)}) copy-start(f32[2304]{0:T(1024)} %param.19) | copy-start | bytes 27652
  288.0 40.0 %copy-start.12 = (f32[64]{0:T(128)S(1)}, f32[64]{0:T(128)}, u32[]{:S(2)}) copy-start(f32[64]{0:T(128)} %broadcast_multiply_fusion.1) | copy-start | bytes 772
  305.0 0.6 copy-start.5
  329.6 0.7 copy-start.3
  412.3 2.0 copy-start.2
Sparse Core Ops, SparseCore 0:
  10.7 237.3 all-gather.1

commit v2 on v0

--- a/solution.py
+++ b/solution.py
@@ -14,8 +14,14 @@
 epsilon = 1e-05
 
 
-def axis_gather(block, axis, count, tag):
-    def kernel(x_ref, out_ref, send_sem, recv_sem):
+def axis_share(parts, axis, count, tag):
+    arrays = [array for array, _ in parts]
+    splits = [split for _, split in parts]
+    width = len(arrays)
+
+    def kernel(*refs):
+        sources, targets = refs[:width], refs[width:2 * width]
+        send_sem, recv_sem = refs[2 * width:]
         me = lax.axis_index(axis)
         barrier = pltpu.get_barrier_semaphore()
         for step in range(1, count):
@@ -26,24 +32,41 @@
         copies = []
         for step in range(1, count):
             peer = lax.rem(me + step, count)
-            copy = pltpu.make_async_remote_copy(
-                src_ref=x_ref, dst_ref=out_ref.at[me],
-                send_sem=send_sem.at[step], recv_sem=recv_sem.at[step],
-                device_id={axis: peer}, device_id_type=pl.DeviceIdType.MESH)
-            copy.start()
-            copies.append(copy)
-        out_ref[me] = x_ref[...]
+            for index in range(width):
+                source = sources[index].at[peer] if splits[index] else sources[index]
+                copy = pltpu.make_async_remote_copy(
+                    src_ref=source, dst_ref=targets[index].at[me],
+                    send_sem=send_sem.at[index, step], recv_sem=recv_sem.at[index, step],
+                    device_id={axis: peer}, device_id_type=pl.DeviceIdType.MESH)
+                copy.start()
+                copies.append(copy)
+        for index in range(width):
+            if splits[index]:
+                targets[index][me] = sources[index][me]
+            else:
+                targets[index][me] = sources[index][...]
         for copy in copies:
             copy.wait_send()
             copy.wait_recv()
+
     return pl.pallas_call(
         kernel,
-        out_shape=jax.ShapeDtypeStruct((count,) + block.shape, block.dtype),
-        in_specs=[pl.BlockSpec(memory_space=pltpu.VMEM)],
-        out_specs=pl.BlockSpec(memory_space=pltpu.VMEM),
-        scratch_shapes=[pltpu.SemaphoreType.DMA((count,)), pltpu.SemaphoreType.DMA((count,))],
+        out_shape=[
+            jax.ShapeDtypeStruct(array.shape if split else (count,) + array.shape, array.dtype)
+            for array, split in parts
+        ],
+        in_specs=[pl.BlockSpec(memory_space=pltpu.VMEM)] * width,
+        out_specs=[pl.BlockSpec(memory_space=pltpu.VMEM)] * width,
+        scratch_shapes=[
+            pltpu.SemaphoreType.DMA((width, count)),
+            pltpu.SemaphoreType.DMA((width, count)),
+        ],
         compiler_params=pltpu.CompilerParams(collective_id=tag, has_side_effects=True),
-    )(block)
+    )(*arrays)
+
+
+def axis_gather(block, axis, count, tag):
+    return axis_share([(block, False)], axis, count, tag)[0]
 
 
 def body(
@@ -71,9 +94,9 @@
         * premix_rmsnorm_gain
     ).astype(jnp.bfloat16)
     features = (
-        axis_gather(normed_local, "mp", columns_count, 5)
-        .transpose(1, 0, 2)
-        .reshape(tok_rows, EMBED_DIMENSION)
+        axis_gather(normed_local.T, "mp", columns_count, 5)
+        .reshape(EMBED_DIMENSION, tok_rows)
+        .T
     )
     router = jnp.dot(features, dispatcher_weights, preferred_element_type=jnp.float32)
     mixing = jax.nn.softmax(jnp.take_along_axis(router, chosen_specialists, axis=1), axis=1)
@@ -103,14 +126,17 @@
         combined = combined + down * weight[:, None]
     ends_index = jnp.cumsum(sequence_piece_tallies[0], dtype=jnp.int32) - 1
     partial_rows = combined.astype(jnp.bfloat16)
-    branch = lax.psum_scatter(partial_rows, "mp", scatter_dimension=1, tiled=True).astype(jnp.float32)
-    new_hidden = skip_stream_arriving + branch_scale * branch
+    column_blocks = partial_rows.T.reshape(columns_count, -1, tok_rows)
     skip_ends = (
         axis_gather(skip_stream_arriving[ends_index], "mp", columns_count, 6)
         .transpose(1, 0, 2)
         .reshape(ends_index.shape[0], EMBED_DIMENSION)
     )
-    end_partials = axis_gather(partial_rows[ends_index], "mp", columns_count, 1)
+    swapped, end_partials = axis_share(
+        [(column_blocks, True), (partial_rows[ends_index], False)], "mp", columns_count, 7
+    )
+    branch = jnp.sum(swapped.astype(jnp.float32), axis=0).T
+    new_hidden = skip_stream_arriving + branch_scale * branch
     end_rows = skip_ends + branch_scale * jnp.sum(end_partials.astype(jnp.float32), axis=0)
     end_squares = jnp.sum(end_rows * end_rows, axis=1)
     end_normed = (

time: 401 us -> 376 us (0.938)
  waiting for transfers between devices: 58.6 us -> 16 us
  Pallas kernels: 250 us -> 269 us
  local copies, waits for them, and re-layouts: 26.7 us -> 21.2 us
    unnamed x3 -> x1, waiting for transfers between devices: 42.5 us -> 0.02 us
    pallas_call x7, Pallas kernels: 250 us -> 269 us  [axis_share(): pl.pallas_call(kernel, out_shape=[jax.ShapeDtypeStruct(array.shape if spl...]
  transfers between devices with their start and end apart: 2 -> 1, of which waited for: 2 -> 1; matrix products, arithmetic and copies ran while one was open for 7% -> 5% of each run, Pallas kernels for 59% -> 51%
where the time goes in v2:
time: 376 us; the launch traced here: 373 us
  Pallas kernels  269 us (72%)
  matrix products  39.3 us (10%)
  local copies, waits for them, and re-layouts  21.2 us (6%)
  waiting for transfers between devices  16 us (4%)
  between operations  14.3 us (4%)
  other arithmetic  13.9 us (4%)
    pallas_call x7, Pallas kernels, axis_share(): pl.pallas_call(kernel, out_shape=[jax.ShapeDtypeStruct(array.shape if spl...  269 us
    dot_general x4, matrix products, body(): lax.dot_general(act, all_weights[expert, 2], (((1,), (1,)), ((), ())), pr...  25.1 us
    all_gather x1, waiting for transfers between devices, body(): lax.all_gather(jnp.stack([specialist_switch_weights, specialist_expand_we...  16 us
    dot_general x4, matrix products, body(): jnp.dot(features, all_weights[expert, 0], preferred_element_type=jnp.floa...  12 us
  transfers between devices with their start and end apart: 1, of which 1 were waited for; matrix products, arithmetic and copies ran while one was open for 5% of the time, Pallas kernels for 51%

profile of v2, /device:TPU:8, one launch (start us, length us, event | category | flops | bytes accessed | tf_op | source)
XLA Modules:
  0.0 373.4 jit_solution(10630637557797427856)
XLA Ops:
  7.2 0.0 copy-start
  7.2 0.0 all-gather.2.cloned.1.call-start
  7.2 0.0 copy-start.2
  7.2 0.0 copy-start.10
  7.2 2.8 pad_maximum_fusion
  10.1 0.0 all-gather.2.cloned.1.call-update
  10.1 0.0 copy-done.2
  10.1 0.8 copy.76
  10.9 0.6 multiply_reduce_fusion
  11.5 11.5 %shard_map.122 = f32[16,1,256]{2,1,0:T(1,128)} custom-call(f32[1,256]{1,0:T(1,128)} %bitcast.133), custom_call_target="tpu_custom_call" | custom-call | tf_op jit(solution)/shard_map/pallas_call | solution.py:52
  23.0 0.8 reduce_sum.82
  23.8 0.0 copy-done.10
  23.8 0.7 fusion.44.refs_0_
  24.5 59.8 %shard_map.123 = bf16[16,144,256]{2,1,0:T(8,128)(2,1)} custom-call(bf16[144,256]{1,0:T(8,128)(2,1)} %fusion.44.refs_0_), custom_call_target="tpu_custom_call" | custom-call | tf_op jit(solution)/shard_map/pallas_call | solution.py:52
  84.3 0.0 copy-done.6
  84.4 0.1 copy.73
  84.5 0.1 reshape.96
  84.7 0.0 copy-done.7
  84.7 1.5 fusion.62
  86.2 5.1 %gather_fusion.2 = f32[512]{0:T(512)S(1)} fusion(f32[256,4]{0,1:T(4,128)S(1)} %fusion.62, s32[512]{0:T(512)S(1)} %reshape.96), kind=kCustom, calls=%fused_computation.2 | custom fusion | bytes 8192 | tf_op jit(solution)/shard_map/jit(take_along_axis)/gather | solution.py:102
  91.2 0.8 reshape.99
  92.0 1.0 copy.74
  93.0 0.8 reduce-window.4
  93.9 2.2 gather_fusion.1
  96.1 120.2 %shard_map.125 = f32[16,4,144]{2,1,0:T(4,128)} custom-call(f32[4,144]{1,0:T(4,128)} %gather_fusion.1), custom_call_target="tpu_custom_call" | custom-call | tf_op jit(solution)/shard_map/pallas_call | solution.py:52
  216.2 1.5 copy.77
  217.7 1.6 reshape.78
  219.3 1.2 broadcast_multiply_fusion.1
  220.5 0.6 fusion.52
  221.1 16.0 %all-gather.2.cloned.1.call-done = bf16[4,3,2304,360]{3,2,0,1:T(8,128)(2,1)} async-done(((bf16[4,3,144,360]{3,2,0,1:T(8,128)(2,1)}), bf16[4,3,2304,360]{3,2,0,1:T(8,128)(2,1)}) %all-gather.2.cloned.1.call-update) | async-done | bytes 19906576 | tf_op jit(solution)/shard_map/all_gather | solution.py:103
  237.1 0.0 copy-done.1
  237.1 3.0 fusion.11
  240.1 3.0 fusion.9
  243.1 3.0 fusion.7
  246.1 3.0 fusion.5
  249.1 0.0 copy-done.12
  249.1 5.8 %convolution_multiply_fusion.3 = f32[256,2304]{1,0:T(8,128)} fusion(bf16[4,3,2304,360]{3,2,0,1:T(8,128)(2,1)} %all-gather.2.cloned.1.call-done, f32[256]{0:T(256)S(1)} %bitcast.139, bf16[2304,256]{1,0:T(8,128)(2,1)S(1)} %bitcast.115, f32[256,360]{0,1:T(8,128)} %fusion.11), kind=kOutput, calls=%fused_computation.9 | convolution fusion | flops 850489344 | bytes 7447552 | tf_op jit(solution)/shard_map/dot_general | solution.py:122
  255.0 0.0 copy-done.9
  255.0 6.6 %fusion.2 = f32[256,2304]{1,0:T(8,128)} fusion(f32[256,2304]{1,0:T(8,128)} %convolution_multiply_fusion.3, bf16[4,3,2304,360]{3,2,0,1:T(8,128)(2,1)} %all-gather.2.cloned.1.call-done, f32[256]{0:T(256)S(1)} %bitcast.135, bf16[2304,256]{1,0:T(8,128)(2,1)S(1)} %bitcast.116, f32[256,360]{0,1:T(8,128)} %fusion.9), kind=kOutput, calls=%fused_computation.8 | convolution fusion | flops 851079168 | bytes 9806848 | tf_op jit(solution)/shard_map/dot_general | solution.py:122
  261.5 6.6 %fusion.1 = f32[256,2304]{1,0:T(8,128)} fusion(f32[256,2304]{1,0:T(8,128)} %fusion.2, bf16[4,3,2304,360]{3,2,0,1:T(8,128)(2,1)} %all-gather.2.cloned.1.call-done, f32[256]{0:T(256)S(1)} %bitcast.134, bf16[2304,256]{1,0:T(8,128)(2,1)S(1)} %bitcast.117, f32[256,360]{0,1:T(8,128)} %fusion.7), kind=kOutput, calls=%fused_computation.6 | convolution fusion | flops 851079168 | bytes 9806848 | tf_op jit(solution)/shard_map/dot_general | solution.py:122
  268.1 0.0 copy-done.11
  268.1 6.1 %fusion.3 = bf16[256,2304]{1,0:T(8,128)(2,1)} fusion(f32[256,2304]{1,0:T(8,128)} %fusion.1, bf16[4,3,2304,360]{3,2,0,1:T(8,128)(2,1)} %all-gather.2.cloned.1.call-done, f32[256]{0:T(256)S(1)} %bitcast.138, bf16[2304,256]{1,0:T(8,128)(2,1)S(1)} %bitcast.118, f32[256,360]{0,1:T(8,128)} %fusion.5), kind=kOutput, calls=%fused_computation.10 | convolution fusion | flops 851668992 | bytes 8627200 | tf_op jit(solution)/shard_map/dot_general | solution.py:122
  274.2 2.6 gather_fusion
  276.9 2.6 copy.75
  279.5 39.5 %shard_map.124 = (bf16[16,144,256]{2,1,0:T(8,128)(2,1)}, bf16[16,4,2304]{2,1,0:T(4,128)(2,1)}) custom-call(bf16[16,144,256]{2,1,0:T(8,128)(2,1)} %bitcast.119, bf16[4,2304]{1,0:T(4,128)(2,1)} %gather_fusion), custom_call_target="tpu_custom_call" | custom-call | tf_op jit(solution)/shard_map/pallas_call | solution.py:52
  319.0 1.1 convert_reduce_fusion.1
  320.1 0.1 mul.174
  320.2 0.0 copy-done.4
  320.2 0.2 fusion.46
  320.4 0.7 multiply_convert_fusion.1.refs_0_
  321.1 16.0 %shard_map.126 = bf16[16,4,2304]{2,1,0:T(4,128)(2,1)} custom-call(bf16[4,2304]{1,0:T(4,128)(2,1)} %multiply_convert_fusion.1.refs_0_), custom_call_target="tpu_custom_call" | custom-call | tf_op jit(solution)/shard_map/pallas_call | solution.py:52
  337.1 1.0 reshape.79
  338.2 0.0 copy-start.3
  338.2 0.6 fusion.61
  338.8 0.2 exponential_reduce_fusion
  339.0 0.6 pad_maximum_fusion.1.refs_0_
  339.6 10.3 %shard_map.127 = f32[16,2,64]{2,1,0:T(2,128)} custom-call(f32[2,64]{1,0:T(2,128)} %pad_maximum_fusion.1.refs_0_), custom_call_target="tpu_custom_call" | custom-call | tf_op jit(solution)/shard_map/pallas_call | solution.py:52
  349.9 0.8 fusion.60
  350.7 0.6 pad_maximum_fusion.2.refs_0_
  351.3 11.5 %shard_map.128 = f32[16,2,64]{2,1,0:T(2,128)} custom-call(f32[2,64]{1,0:T(2,128)} %pad_maximum_fusion.2.refs_0_), custom_call_target="tpu_custom_call" | custom-call | tf_op jit(solution)/shard_map/pallas_call | solution.py:52
  362.8 0.8 fusion.59
  363.7 0.8 subtract_subtract_fusion
  364.4 1.4 convert_reduce_fusion
  365.9 0.7 bitcast_add_fusion
  (29 shorter events, 0.2 us)
Async XLA Ops:
  7.2 331.0 %copy-start = (bf16[2304,512]{1,0:T(8,128)(2,1)S(1)}, bf16[2304,512]{1,0:T(8,128)(2,1)}, u32[]{:S(2)}) copy-start(bf16[2304,512]{1,0:T(8,128)(2,1)} %param.20) | copy-start | bytes 7077892
  7.2 229.9 %all-gather.2.cloned.1.call-start = ((), (), s32[]{:S(2)}) async-start(), calls=%async_computation | async-start | bytes 22560768 | tf_op jit(solution)/shard_map/all_gather | solution.py:103
  7.2 2.9 copy-start.2
  7.2 16.6 %copy-start.10 = (f32[144]{0:T(256)S(1)}, f32[144]{0:T(256)}, u32[]{:S(2)}) copy-start(f32[144]{0:T(256)} %param.14) | copy-start | bytes 1732
  10.1 74.3 %copy-start.6 = (s32[256,2]{0,1:T(2,128)S(1)}, s32[256,2]{0,1:T(2,128)}, u32[]{:S(2)}) copy-start(s32[256,2]{0,1:T(2,128)} %param.12) | copy-start | bytes 6148
  10.1 74.6 %copy-start.7 = (bf16[2304,4]{0,1:T(4,128)(2,1)S(1)}, bf16[2304,4]{0,1:T(4,128)(2,1)}, u32[]{:S(2)}) copy-start(bf16[2304,4]{0,1:T(4,128)(2,1)} %param.15) | copy-start | bytes 55300
  86.2 150.9 %copy-start.1 = (bf16[16,144,256]{2,1,0:T(8,128)(2,1)S(1)}, bf16[16,144,256]{2,1,0:T(8,128)(2,1)}, u32[]{:S(2)}) copy-start(bf16[16,144,256]{2,1,0:T(8,128)(2,1)} %shard_map.123) | copy-start | bytes 3538948
  246.1 3.0 copy-start.12
  249.1 5.8 %copy-start.9 = (f32[256,1]{0,1:T(1,128)S(1)}, f32[256,1]{0,1:T(1,128)}, u32[]{:S(2)}) copy-start(f32[256,1]{0,1:T(1,128)} %get-tuple-element.15) | copy-start | bytes 3076
  261.5 6.6 %copy-start.11 = (f32[256,1]{0,1:T(1,128)S(1)}, f32[256,1]{0,1:T(1,128)}, u32[]{:S(2)}) copy-start(f32[256,1]{0,1:T(1,128)} %get-tuple-element.12) | copy-start | bytes 3076
  276.9 43.4 %copy-start.4 = (f32[16,4,144]{2,1,0:T(4,128)S(1)}, f32[16,4,144]{2,1,0:T(4,128)}, u32[]{:S(2)}) copy-start(f32[16,4,144]{2,1,0:T(4,128)} %shard_map.125) | copy-start | bytes 110596
  276.9 43.6 %copy-start.5 = (f32[4,2304]{1,0:T(4,128)S(1)}, f32[4,2304]{1,0:T(4,128)}, u32[]{:S(2)}) copy-start(f32[4,2304]{1,0:T(4,128)} %reshape.78) | copy-start | bytes 110596
  276.9 43.6 %copy-start.8 = (f32[2304]{0:T(1024)S(1)}, f32[2304]{0:T(1024)}, u32[]{:S(2)}) copy-start(f32[2304]{0:T(1024)} %param.19) | copy-start | bytes 27652
  279.5 58.7 %copy-start.13 = (f32[64]{0:T(128)S(1)}, f32[64]{0:T(128)}, u32[]{:S(2)}) copy-start(f32[64]{0:T(128)} %broadcast_multiply_fusion.1) | copy-start | bytes 772
  338.2 27.7 %copy-start.3 = (f32[256,144]{0,1:T(8,128)S(1)}, f32[256,144]{0,1:T(8,128)}, u32[]{:S(2)}) copy-start(f32[256,144]{0,1:T(8,128)} %param.11) | copy-start | bytes 442372
Sparse Core Ops, SparseCore 0:
  10.7 226.3 all-gather.1

commit v3 on v2

--- a/solution.py
+++ b/solution.py
@@ -93,12 +93,13 @@
         * lax.rsqrt(squares / EMBED_DIMENSION + epsilon)[:, None]
         * premix_rmsnorm_gain
     ).astype(jnp.bfloat16)
-    features = (
-        axis_gather(normed_local.T, "mp", columns_count, 5)
-        .reshape(EMBED_DIMENSION, tok_rows)
-        .T
+    features_t = axis_gather(normed_local.T, "mp", columns_count, 5).reshape(
+        EMBED_DIMENSION, tok_rows
     )
-    router = jnp.dot(features, dispatcher_weights, preferred_element_type=jnp.float32)
+    by_rows = (((0,), (0,)), ((), ()))
+    router = lax.dot_general(
+        features_t, dispatcher_weights, by_rows, preferred_element_type=jnp.float32
+    )
     mixing = jax.nn.softmax(jnp.take_along_axis(router, chosen_specialists, axis=1), axis=1)
     all_weights = lax.all_gather(
         jnp.stack(
@@ -111,29 +112,30 @@
         ),
         "dp", axis=2, tiled=True,
     )
-    combined = jnp.zeros((tok_rows, EMBED_DIMENSION), jnp.float32)
+    combined_t = jnp.zeros((EMBED_DIMENSION, tok_rows), jnp.float32)
     for expert in range(experts):
         weight = jnp.where(chosen_specialists[:, 0] == expert, mixing[:, 0], 0.0) + jnp.where(
             chosen_specialists[:, 1] == expert, mixing[:, 1], 0.0
         )
-        gate = jnp.dot(features, all_weights[expert, 0], preferred_element_type=jnp.float32)
-        up_part = jnp.dot(features, all_weights[expert, 1], preferred_element_type=jnp.float32)
-        act = (jax.nn.silu(gate) * up_part).astype(jnp.bfloat16)
-        down = lax.dot_general(
-            act, all_weights[expert, 2], (((1,), (1,)), ((), ())),
-            preferred_element_type=jnp.float32,
+        gate_t = lax.dot_general(
+            all_weights[expert, 0], features_t, by_rows, preferred_element_type=jnp.float32
         )
-        combined = combined + down * weight[:, None]
+        up_t = lax.dot_general(
+            all_weights[expert, 1], features_t, by_rows, preferred_element_type=jnp.float32
+        )
+        act_t = (jax.nn.silu(gate_t) * up_t).astype(jnp.bfloat16)
+        down_t = jnp.dot(all_weights[expert, 2], act_t, preferred_element_type=jnp.float32)
+        combined_t = combined_t + down_t * weight[None, :]
     ends_index = jnp.cumsum(sequence_piece_tallies[0], dtype=jnp.int32) - 1
-    partial_rows = combined.astype(jnp.bfloat16)
-    column_blocks = partial_rows.T.reshape(columns_count, -1, tok_rows)
+    partial_t = combined_t.astype(jnp.bfloat16)
+    column_blocks = partial_t.reshape(columns_count, -1, tok_rows)
     skip_ends = (
         axis_gather(skip_stream_arriving[ends_index], "mp", columns_count, 6)
         .transpose(1, 0, 2)
         .reshape(ends_index.shape[0], EMBED_DIMENSION)
     )
     swapped, end_partials = axis_share(
-        [(column_blocks, True), (partial_rows[ends_index], False)], "mp", columns_count, 7
+        [(column_blocks, True), (partial_t[:, ends_index].T, False)], "mp", columns_count, 7
     )
     branch = jnp.sum(swapped.astype(jnp.float32), axis=0).T
     new_hidden = skip_stream_arriving + branch_scale * branch

time: 376 us -> 374 us (level)
  transfers between devices with their start and end apart: 1 -> 1, of which waited for: 1 -> 1; matrix products, arithmetic and copies ran while one was open for 5% -> 5% of each run, Pallas kernels for 51% -> 52%
where the time goes in v3:
time: 374 us; the launch traced here: 371 us
  Pallas kernels  269 us (72%)
  matrix products  38.2 us (10%)
  local copies, waits for them, and re-layouts  18.7 us (5%)
  waiting for transfers between devices  16 us (4%)
  other arithmetic  14.7 us (4%)
  between operations  14.3 us (4%)
    pallas_call x7, Pallas kernels, axis_share(): pl.pallas_call(kernel, out_shape=[jax.ShapeDtypeStruct(array.shape if spl...  269 us
    dot_general x4, matrix products, body(): jnp.dot(all_weights[expert, 2], act_t, preferred_element_type=jnp.float32)  24.6 us
    all_gather x1, waiting for transfers between devices, body(): lax.all_gather(jnp.stack([specialist_switch_weights, specialist_expand_we...  16 us
    dot_general x4, matrix products, body(): lax.dot_general(all_weights[expert, 0], features_t, by_rows, preferred_el...  11.5 us
  transfers between devices with their start and end apart: 1, of which 1 were waited for; matrix products, arithmetic and copies ran while one was open for 5% of the time, Pallas kernels for 52%

profile of v3, /device:TPU:8, one launch (start us, length us, event | category | flops | bytes accessed | tf_op | source)
XLA Modules:
  0.0 371.0 jit_solution(1003423016034686020)
XLA Ops:
  7.2 0.0 copy-start
  7.2 0.0 all-gather.2.cloned.1.call-start
  7.2 0.0 copy-start.2
  7.2 0.0 copy-start.8
  7.2 2.8 pad_maximum_fusion
  10.1 0.0 all-gather.2.cloned.1.call-update
  10.1 0.0 copy-done.2
  10.1 0.8 copy.76
  10.9 0.6 multiply_reduce_fusion
  11.5 11.5 %shard_map.122 = f32[16,1,256]{2,1,0:T(1,128)} custom-call(f32[1,256]{1,0:T(1,128)} %bitcast.131), custom_call_target="tpu_custom_call" | custom-call | tf_op jit(solution)/shard_map/pallas_call | solution.py:52
  23.0 0.8 reduce_sum.82
  23.8 0.0 copy-done.8
  23.8 0.7 fusion.44.refs_0_
  24.5 59.8 %shard_map.123 = bf16[16,144,256]{2,1,0:T(8,128)(2,1)} custom-call(bf16[144,256]{1,0:T(8,128)(2,1)} %fusion.44.refs_0_), custom_call_target="tpu_custom_call" | custom-call | tf_op jit(solution)/shard_map/pallas_call | solution.py:52
  84.3 0.0 copy-done.5
  84.4 0.1 copy.73
  84.5 0.1 reshape.216
  84.7 0.0 copy-done.6
  84.7 1.5 fusion.62
  86.2 4.9 %gather_fusion.2 = f32[512]{0:T(512)S(1)} fusion(f32[256,4]{0,1:T(4,128)S(1)} %fusion.62, s32[512]{0:T(512)S(1)} %reshape.216), kind=kCustom, calls=%fused_computation.2 | custom fusion | bytes 8192 | tf_op jit(solution)/shard_map/jit(take_along_axis)/gather | solution.py:103
  91.1 0.8 reshape.219
  91.9 1.0 copy.74
  92.8 0.8 reduce-window.4
  93.7 2.2 gather_fusion.1
  95.9 120.4 %shard_map.125 = f32[16,4,144]{2,1,0:T(4,128)} custom-call(f32[4,144]{1,0:T(4,128)} %gather_fusion.1), custom_call_target="tpu_custom_call" | custom-call | tf_op jit(solution)/shard_map/pallas_call | solution.py:52
  216.2 1.5 copy.77
  217.7 1.6 reshape.198
  219.3 1.2 broadcast_multiply_fusion.1
  220.5 0.6 fusion.52
  221.1 16.0 %all-gather.2.cloned.1.call-done = bf16[4,3,2304,360]{3,2,0,1:T(8,128)(2,1)} async-done(((bf16[4,3,144,360]{3,2,0,1:T(8,128)(2,1)}), bf16[4,3,2304,360]{3,2,0,1:T(8,128)(2,1)}) %all-gather.2.cloned.1.call-update) | async-done | bytes 19906576 | tf_op jit(solution)/shard_map/all_gather | solution.py:104
  237.1 0.0 copy-done.1
  237.1 2.9 fusion.11
  239.9 2.9 fusion.9
  242.8 2.9 fusion.7
  245.7 2.9 fusion.5
  248.6 0.0 copy-done.11
  248.6 5.7 %convolution_multiply_fusion.3 = f32[2304,256]{1,0:T(8,128)} fusion(bf16[4,3,2304,360]{3,2,0,1:T(8,128)(2,1)} %all-gather.2.cloned.1.call-done, f32[256]{0:T(256)S(1)} %bitcast.137, bf16[2304,256]{1,0:T(8,128)(2,1)S(1)} %bitcast.114, f32[360,256]{1,0:T(8,128)} %fusion.11), kind=kOutput, calls=%fused_computation.9 | convolution fusion | flops 850489344 | bytes 7447552 | tf_op jit(solution)/shard_map/dot_general | solution.py:127
  254.3 0.0 copy-done.10
  254.3 6.5 %fusion.2 = f32[2304,256]{1,0:T(8,128)} fusion(f32[2304,256]{1,0:T(8,128)} %convolution_multiply_fusion.3, bf16[4,3,2304,360]{3,2,0,1:T(8,128)(2,1)} %all-gather.2.cloned.1.call-done, f32[256]{0:T(256)S(1)} %bitcast.136, bf16[2304,256]{1,0:T(8,128)(2,1)S(1)} %bitcast.115, f32[360,256]{1,0:T(8,128)} %fusion.9), kind=kOutput, calls=%fused_computation.8 | convolution fusion | flops 851079168 | bytes 9806848 | tf_op jit(solution)/shard_map/dot_general | solution.py:127
  260.7 0.0 copy-done.9
  260.7 6.5 %fusion.1 = f32[2304,256]{1,0:T(8,128)} fusion(f32[2304,256]{1,0:T(8,128)} %fusion.2, bf16[4,3,2304,360]{3,2,0,1:T(8,128)(2,1)} %all-gather.2.cloned.1.call-done, f32[256]{0:T(256)S(1)} %bitcast.135, bf16[2304,256]{1,0:T(8,128)(2,1)S(1)} %bitcast.116, f32[360,256]{1,0:T(8,128)} %fusion.7), kind=kOutput, calls=%fused_computation.6 | convolution fusion | flops 851079168 | bytes 9806848 | tf_op jit(solution)/shard_map/dot_general | solution.py:127
  267.2 6.0 %fusion.3 = bf16[2304,256]{1,0:T(8,128)(2,1)} fusion(f32[2304,256]{1,0:T(8,128)} %fusion.1, bf16[4,3,2304,360]{3,2,0,1:T(8,128)(2,1)} %all-gather.2.cloned.1.call-done, f32[256]{0:T(256)S(1)} %bitcast.134, bf16[2304,256]{1,0:T(8,128)(2,1)S(1)} %bitcast.117, f32[360,256]{1,0:T(8,128)} %fusion.5), kind=kOutput, calls=%fused_computation.10 | convolution fusion | flops 851668992 | bytes 8627200 | tf_op jit(solution)/shard_map/dot_general | solution.py:127
  273.2 1.7 copy.75
  275.0 1.2 gather_fusion
  276.2 39.6 %shard_map.124 = (bf16[16,144,256]{2,1,0:T(8,128)(2,1)}, bf16[16,4,2304]{2,1,0:T(4,128)(2,1)}) custom-call(bf16[16,144,256]{2,1,0:T(8,128)(2,1)} %bitcast.118, bf16[4,2304]{1,0:T(4,128)(2,1)} %gather_fusion), custom_call_target="tpu_custom_call" | custom-call | tf_op jit(solution)/shard_map/pallas_call | solution.py:52
  315.7 1.1 convert_reduce_fusion.1
  316.8 0.1 mul.154
  316.9 1.0 fusion.46
  318.0 0.0 copy-done.4
  318.0 0.7 multiply_convert_fusion.1.refs_0_
  318.7 16.0 %shard_map.126 = bf16[16,4,2304]{2,1,0:T(4,128)(2,1)} custom-call(bf16[4,2304]{1,0:T(4,128)(2,1)} %multiply_convert_fusion.1.refs_0_), custom_call_target="tpu_custom_call" | custom-call | tf_op jit(solution)/shard_map/pallas_call | solution.py:52
  334.6 1.0 reshape.199
  335.7 0.0 copy-start.3
  335.7 0.6 fusion.61
  336.3 0.2 exponential_reduce_fusion
  336.5 0.6 pad_maximum_fusion.1.refs_0_
  337.1 10.3 %shard_map.127 = f32[16,2,64]{2,1,0:T(2,128)} custom-call(f32[2,64]{1,0:T(2,128)} %pad_maximum_fusion.1.refs_0_), custom_call_target="tpu_custom_call" | custom-call | tf_op jit(solution)/shard_map/pallas_call | solution.py:52
  347.4 0.8 fusion.60
  348.3 0.6 pad_maximum_fusion.2.refs_0_
  348.9 11.5 %shard_map.128 = f32[16,2,64]{2,1,0:T(2,128)} custom-call(f32[2,64]{1,0:T(2,128)} %pad_maximum_fusion.2.refs_0_), custom_call_target="tpu_custom_call" | custom-call | tf_op jit(solution)/shard_map/pallas_call | solution.py:52
  360.4 0.8 fusion.59
  361.2 0.8 subtract_subtract_fusion
  362.0 1.4 convert_reduce_fusion
  363.4 0.7 bitcast_add_fusion
  (27 shorter events, 0.2 us)
Async XLA Ops:
  7.2 328.5 %copy-start = (bf16[2304,512]{1,0:T(8,128)(2,1)S(1)}, bf16[2304,512]{1,0:T(8,128)(2,1)}, u32[]{:S(2)}) copy-start(bf16[2304,512]{1,0:T(8,128)(2,1)} %param.20) | copy-start | bytes 7077892
  7.2 229.9 %all-gather.2.cloned.1.call-start = ((), (), s32[]{:S(2)}) async-start(), calls=%async_computation | async-start | bytes 22560768 | tf_op jit(solution)/shard_map/all_gather | solution.py:104
  7.2 2.9 copy-start.2
  7.2 16.6 %copy-start.8 = (f32[144]{0:T(256)S(1)}, f32[144]{0:T(256)}, u32[]{:S(2)}) copy-start(f32[144]{0:T(256)} %param.14) | copy-start | bytes 1732
  10.1 74.3 %copy-start.5 = (s32[256,2]{0,1:T(2,128)S(1)}, s32[256,2]{0,1:T(2,128)}, u32[]{:S(2)}) copy-start(s32[256,2]{0,1:T(2,128)} %param.12) | copy-start | bytes 6148
  10.1 74.6 %copy-start.6 = (bf16[2304,4]{0,1:T(4,128)(2,1)S(1)}, bf16[2304,4]{0,1:T(4,128)(2,1)}, u32[]{:S(2)}) copy-start(bf16[2304,4]{0,1:T(4,128)(2,1)} %param.15) | copy-start | bytes 55300
  86.2 150.9 %copy-start.1 = (bf16[16,144,256]{2,1,0:T(8,128)(2,1)S(1)}, bf16[16,144,256]{2,1,0:T(8,128)(2,1)}, u32[]{:S(2)}) copy-start(bf16[16,144,256]{2,1,0:T(8,128)(2,1)} %shard_map.123) | copy-start | bytes 3538948
  245.7 2.9 copy-start.11
  248.6 5.7 %copy-start.10 = (f32[256,1]{0,1:T(1,128)S(1)}, f32[256,1]{0,1:T(1,128)}, u32[]{:S(2)}) copy-start(f32[256,1]{0,1:T(1,128)} %get-tuple-element.15) | copy-start | bytes 3076
  254.3 6.5 %copy-start.9 = (f32[256,1]{0,1:T(1,128)S(1)}, f32[256,1]{0,1:T(1,128)}, u32[]{:S(2)}) copy-start(f32[256,1]{0,1:T(1,128)} %get-tuple-element.13) | copy-start | bytes 3076
  276.2 41.8 %copy-start.4 = (f32[4,2304]{1,0:T(4,128)S(1)}, f32[4,2304]{1,0:T(4,128)}, u32[]{:S(2)}) copy-start(f32[4,2304]{1,0:T(4,128)} %reshape.198) | copy-start | bytes 110596
  276.2 41.8 %copy-start.7 = (f32[2304]{0:T(1024)S(1)}, f32[2304]{0:T(1024)}, u32[]{:S(2)}) copy-start(f32[2304]{0:T(1024)} %param.19) | copy-start | bytes 27652
  276.2 59.5 %copy-start.12 = (f32[64]{0:T(128)S(1)}, f32[64]{0:T(128)}, u32[]{:S(2)}) copy-start(f32[64]{0:T(128)} %broadcast_multiply_fusion.1) | copy-start | bytes 772
  335.7 27.7 %copy-start.3 = (f32[256,144]{0,1:T(8,128)S(1)}, f32[256,144]{0,1:T(8,128)}, u32[]{:S(2)}) copy-start(f32[256,144]{0,1:T(8,128)} %param.11) | copy-start | bytes 442372
Sparse Core Ops, SparseCore 0:
  10.7 226.3 all-gather.1

commit v4 on v3

--- a/solution.py
+++ b/solution.py
@@ -14,34 +14,37 @@
 epsilon = 1e-05
 
 
-def axis_share(parts, axis, count, tag):
-    arrays = [array for array, _ in parts]
-    splits = [split for _, split in parts]
+def mesh_share(parts, counts, tag):
+    arrays = [array for array, _, _ in parts]
     width = len(arrays)
+    axes = sorted({axis for _, axis, _ in parts})
 
     def kernel(*refs):
         sources, targets = refs[:width], refs[width:2 * width]
         send_sem, recv_sem = refs[2 * width:]
-        me = lax.axis_index(axis)
         barrier = pltpu.get_barrier_semaphore()
-        for step in range(1, count):
-            peer = lax.rem(me + step, count)
-            pl.semaphore_signal(barrier, 1, device_id={axis: peer},
-                                device_id_type=pl.DeviceIdType.MESH)
-        pl.semaphore_wait(barrier, count - 1)
+        for axis in axes:
+            me = lax.axis_index(axis)
+            for step in range(1, counts[axis]):
+                peer = lax.rem(me + step, counts[axis])
+                pl.semaphore_signal(barrier, 1, device_id={axis: peer},
+                                    device_id_type=pl.DeviceIdType.MESH)
+        pl.semaphore_wait(barrier, sum(counts[axis] - 1 for axis in axes))
         copies = []
-        for step in range(1, count):
-            peer = lax.rem(me + step, count)
-            for index in range(width):
-                source = sources[index].at[peer] if splits[index] else sources[index]
+        for index, (_, axis, split) in enumerate(parts):
+            me = lax.axis_index(axis)
+            for step in range(1, counts[axis]):
+                peer = lax.rem(me + step, counts[axis])
+                source = sources[index].at[peer] if split else sources[index]
                 copy = pltpu.make_async_remote_copy(
                     src_ref=source, dst_ref=targets[index].at[me],
                     send_sem=send_sem.at[index, step], recv_sem=recv_sem.at[index, step],
                     device_id={axis: peer}, device_id_type=pl.DeviceIdType.MESH)
                 copy.start()
                 copies.append(copy)
-        for index in range(width):
-            if splits[index]:
+        for index, (_, axis, split) in enumerate(parts):
+            me = lax.axis_index(axis)
+            if split:
                 targets[index][me] = sources[index][me]
             else:
                 targets[index][me] = sources[index][...]
@@ -52,21 +55,23 @@
     return pl.pallas_call(
         kernel,
         out_shape=[
-            jax.ShapeDtypeStruct(array.shape if split else (count,) + array.shape, array.dtype)
-            for array, split in parts
+            jax.ShapeDtypeStruct(
+                array.shape if split else (counts[axis],) + array.shape, array.dtype
+            )
+            for array, axis, split in parts
         ],
         in_specs=[pl.BlockSpec(memory_space=pltpu.VMEM)] * width,
         out_specs=[pl.BlockSpec(memory_space=pltpu.VMEM)] * width,
         scratch_shapes=[
-            pltpu.SemaphoreType.DMA((width, count)),
-            pltpu.SemaphoreType.DMA((width, count)),
+            pltpu.SemaphoreType.DMA((width, max(counts.values()))),
+            pltpu.SemaphoreType.DMA((width, max(counts.values()))),
         ],
         compiler_params=pltpu.CompilerParams(collective_id=tag, has_side_effects=True),
     )(*arrays)
 
 
 def axis_gather(block, axis, count, tag):
-    return axis_share([(block, False)], axis, count, tag)[0]
+    return mesh_share([(block, axis, False)], {axis: count}, tag)[0]
 
 
 def body(
@@ -129,24 +134,28 @@
     ends_index = jnp.cumsum(sequence_piece_tallies[0], dtype=jnp.int32) - 1
     partial_t = combined_t.astype(jnp.bfloat16)
     column_blocks = partial_t.reshape(columns_count, -1, tok_rows)
-    skip_ends = (
-        axis_gather(skip_stream_arriving[ends_index], "mp", columns_count, 6)
-        .transpose(1, 0, 2)
-        .reshape(ends_index.shape[0], EMBED_DIMENSION)
+    end_partials, skip_ends = mesh_share(
+        [
+            (partial_t[:, ends_index].T, "mp", False),
+            (skip_stream_arriving[ends_index], "mp", False),
+        ],
+        {"mp": columns_count},
+        6,
     )
-    swapped, end_partials = axis_share(
-        [(column_blocks, True), (partial_t[:, ends_index].T, False)], "mp", columns_count, 7
-    )
-    branch = jnp.sum(swapped.astype(jnp.float32), axis=0).T
-    new_hidden = skip_stream_arriving + branch_scale * branch
+    skip_ends = skip_ends.transpose(1, 0, 2).reshape(ends_index.shape[0], EMBED_DIMENSION)
     end_rows = skip_ends + branch_scale * jnp.sum(end_partials.astype(jnp.float32), axis=0)
     end_squares = jnp.sum(end_rows * end_rows, axis=1)
     end_normed = (
         end_rows * lax.rsqrt(end_squares / EMBED_DIMENSION + epsilon)[:, None] * terminal_rmsnorm_gain
     ).astype(jnp.bfloat16)
-    lexicon_projector_feed = axis_gather(end_normed, "dp", groups, 2).reshape(
-        groups * end_normed.shape[0], EMBED_DIMENSION
+    swapped, head_rows = mesh_share(
+        [(column_blocks, "mp", True), (end_normed, "dp", False)],
+        {"mp": columns_count, "dp": groups},
+        7,
     )
+    branch = jnp.sum(swapped.astype(jnp.float32), axis=0).T
+    new_hidden = skip_stream_arriving + branch_scale * branch
+    lexicon_projector_feed = head_rows.reshape(groups * end_normed.shape[0], EMBED_DIMENSION)
     lexicon_logit_values = jnp.dot(
         lexicon_projector_feed, lexicon_projector_weights, preferred_element_type=jnp.float32
     ) / (EMBED_DIMENSION / 256.0 * softness_per_sequence[:, None])

time: 374 us -> 374 us (level)
  waiting for transfers between devices: 16 us -> 139 us
  Pallas kernels: 269 us -> 148 us
    all_gather x1, waiting for transfers between devices: 16 us -> 139 us  [body(): lax.all_gather(jnp.stack([specialist_switch_weights, specialist_expand_we...]
    pallas_call x7 -> x6, Pallas kernels: 269 us -> 148 us  [mesh_share(): pl.pallas_call(kernel, out_shape=[jax.ShapeDtypeStruct(array.shape if spl...]
  transfers between devices with their start and end apart: 1 -> 1, of which waited for: 1 -> 1; matrix products, arithmetic and copies ran while one was open for 5% -> 4% of each run, Pallas kernels for 52% -> 19%
where the time goes in v4:
time: 374 us; the launch traced here: 371 us
  Pallas kernels  148 us (40%)
  waiting for transfers between devices  139 us (37%)
  matrix products  38.2 us (10%)
  local copies, waits for them, and re-layouts  17.5 us (5%)
  other arithmetic  14.7 us (4%)
  between operations  14.3 us (4%)
    pallas_call x6, Pallas kernels, mesh_share(): pl.pallas_call(kernel, out_shape=[jax.ShapeDtypeStruct(array.shape if spl...  148 us
    all_gather x1, waiting for transfers between devices, body(): lax.all_gather(jnp.stack([specialist_switch_weights, specialist_expand_we...  139 us
    dot_general x4, matrix products, body(): jnp.dot(all_weights[expert, 2], act_t, preferred_element_type=jnp.float32)  24.6 us
    dot_general x4, matrix products, body(): lax.dot_general(all_weights[expert, 0], features_t, by_rows, preferred_el...  11.5 us
  transfers between devices with their start and end apart: 1, of which 1 were waited for; matrix products, arithmetic and copies ran while one was open for 4% of the time, Pallas kernels for 19%

profile of v4, /device:TPU:8, one launch (start us, length us, event | category | flops | bytes accessed | tf_op | source)
XLA Modules:
  0.0 371.3 jit_solution(10894504129968952496)
XLA Ops:
  7.2 0.0 copy-start
  7.2 0.0 all-gather.2.cloned.1.call-start
  7.2 0.0 copy-start.2
  7.2 0.0 copy-start.8
  7.2 2.8 pad_maximum_fusion
  10.1 0.0 all-gather.2.cloned.1.call-update
  10.1 0.0 copy-done.2
  10.1 0.8 copy.76
  10.9 0.6 multiply_reduce_fusion
  11.5 11.5 %shard_map.122 = f32[16,1,256]{2,1,0:T(1,128)} custom-call(f32[1,256]{1,0:T(1,128)} %bitcast.131), custom_call_target="tpu_custom_call" | custom-call | tf_op jit(solution)/shard_map/pallas_call | solution.py:55
  23.0 0.8 reduce_sum.82
  23.8 0.0 copy-done.8
  23.8 0.7 fusion.44.refs_0_
  24.5 59.8 %shard_map.123 = bf16[16,144,256]{2,1,0:T(8,128)(2,1)} custom-call(bf16[144,256]{1,0:T(8,128)(2,1)} %fusion.44.refs_0_), custom_call_target="tpu_custom_call" | custom-call | tf_op jit(solution)/shard_map/pallas_call | solution.py:55
  84.3 0.0 copy-done.4
  84.4 0.1 copy.73
  84.5 0.1 reshape.216
  84.7 0.0 copy-done.5
  84.7 1.5 fusion.62
  86.2 4.9 %gather_fusion.2 = f32[512]{0:T(512)S(1)} fusion(f32[256,4]{0,1:T(4,128)S(1)} %fusion.62, s32[512]{0:T(512)S(1)} %reshape.216), kind=kCustom, calls=%fused_computation.2 | custom fusion | bytes 8192 | tf_op jit(solution)/shard_map/jit(take_along_axis)/gather | solution.py:108
  91.1 0.8 reshape.219
  91.9 1.0 copy.74
  92.8 0.8 reduce-window.4
  93.7 0.6 copy-done.7
  94.3 2.2 gather_fusion.1
  96.5 1.2 broadcast_multiply_fusion.1
  97.7 0.6 fusion.52
  98.3 139.0 %all-gather.2.cloned.1.call-done = bf16[4,3,2304,360]{3,2,0,1:T(8,128)(2,1)} async-done(((bf16[4,3,144,360]{3,2,0,1:T(8,128)(2,1)}), bf16[4,3,2304,360]{3,2,0,1:T(8,128)(2,1)}) %all-gather.2.cloned.1.call-update) | async-done | bytes 19906576 | tf_op jit(solution)/shard_map/all_gather | solution.py:109
  237.3 0.0 copy-done.1
  237.3 2.9 fusion.11
  240.2 2.9 fusion.9
  243.0 2.9 fusion.7
  245.9 2.9 fusion.5
  248.8 0.0 copy-done.10
  248.8 5.7 %convolution_multiply_fusion.3 = f32[2304,256]{1,0:T(8,128)} fusion(bf16[4,3,2304,360]{3,2,0,1:T(8,128)(2,1)} %all-gather.2.cloned.1.call-done, f32[256]{0:T(256)S(1)} %bitcast.137, bf16[2304,256]{1,0:T(8,128)(2,1)S(1)} %bitcast.114, f32[360,256]{1,0:T(8,128)} %fusion.11), kind=kOutput, calls=%fused_computation.9 | convolution fusion | flops 850489344 | bytes 7447552 | tf_op jit(solution)/shard_map/dot_general | solution.py:132
  254.5 6.5 %fusion.2 = f32[2304,256]{1,0:T(8,128)} fusion(f32[2304,256]{1,0:T(8,128)} %convolution_multiply_fusion.3, bf16[4,3,2304,360]{3,2,0,1:T(8,128)(2,1)} %all-gather.2.cloned.1.call-done, f32[256]{0:T(256)S(1)} %bitcast.136, bf16[2304,256]{1,0:T(8,128)(2,1)S(1)} %bitcast.115, f32[360,256]{1,0:T(8,128)} %fusion.9), kind=kOutput, calls=%fused_computation.8 | convolution fusion | flops 851079168 | bytes 9806848 | tf_op jit(solution)/shard_map/dot_general | solution.py:132
  260.9 6.5 %fusion.1 = f32[2304,256]{1,0:T(8,128)} fusion(f32[2304,256]{1,0:T(8,128)} %fusion.2, bf16[4,3,2304,360]{3,2,0,1:T(8,128)(2,1)} %all-gather.2.cloned.1.call-done, f32[256]{0:T(256)S(1)} %bitcast.135, bf16[2304,256]{1,0:T(8,128)(2,1)S(1)} %bitcast.116, f32[360,256]{1,0:T(8,128)} %fusion.7), kind=kOutput, calls=%fused_computation.6 | convolution fusion | flops 851079168 | bytes 9806848 | tf_op jit(solution)/shard_map/dot_general | solution.py:132
  267.4 6.0 %fusion.3 = bf16[2304,256]{1,0:T(8,128)(2,1)} fusion(f32[2304,256]{1,0:T(8,128)} %fusion.1, bf16[4,3,2304,360]{3,2,0,1:T(8,128)(2,1)} %all-gather.2.cloned.1.call-done, f32[256]{0:T(256)S(1)} %bitcast.134, bf16[2304,256]{1,0:T(8,128)(2,1)S(1)} %bitcast.117, f32[360,256]{1,0:T(8,128)} %fusion.5), kind=kOutput, calls=%fused_computation.10 | convolution fusion | flops 851668992 | bytes 8627200 | tf_op jit(solution)/shard_map/dot_general | solution.py:132
  273.4 1.7 copy.75
  275.2 0.0 copy-start.6
  275.2 1.4 gather_fusion
  276.6 16.3 %shard_map.124 = (bf16[16,4,2304]{2,1,0:T(4,128)(2,1)}, f32[16,4,144]{2,1,0:T(4,128)}) custom-call(bf16[4,2304]{1,0:T(4,128)(2,1)} %gather_fusion, f32[4,144]{1,0:T(4,128)} %gather_fusion.1), custom_call_target="tpu_custom_call" | custom-call | tf_op jit(solution)/shard_map/pallas_call | solution.py:55
  293.0 1.1 convert_reduce_fusion.1
  294.1 0.1 mul.151
  294.2 1.0 fusion.46
  295.2 0.9 copy.77
  296.1 0.1 reshape.198
  296.2 0.7 multiply_convert_fusion.1.refs_1_
  296.9 38.2 %shard_map.125 = (bf16[16,144,256]{2,1,0:T(8,128)(2,1)}, bf16[16,4,2304]{2,1,0:T(4,128)(2,1)}) custom-call(bf16[16,144,256]{2,1,0:T(8,128)(2,1)} %bitcast.118, bf16[4,2304]{1,0:T(4,128)(2,1)} %multiply_convert_fusion.1.refs_1_), custom_call_target="tpu_custom_call" | custom-call | tf_op jit(solution)/shard_map/pallas_call | solution.py:55
  335.1 1.0 reshape.199
  336.1 0.0 copy-done
  336.1 0.0 copy-done.11
  336.1 0.0 copy-start.3
  336.1 0.6 fusion.61
  336.7 0.2 exponential_reduce_fusion
  336.9 0.6 pad_maximum_fusion.1.refs_0_
  337.5 9.7 %shard_map.126 = f32[16,2,64]{2,1,0:T(2,128)} custom-call(f32[2,64]{1,0:T(2,128)} %pad_maximum_fusion.1.refs_0_), custom_call_target="tpu_custom_call" | custom-call | tf_op jit(solution)/shard_map/pallas_call | solution.py:55
  347.2 0.8 fusion.60
  348.1 0.6 pad_maximum_fusion.2.refs_0_
  348.7 12.0 %shard_map.127 = f32[16,2,64]{2,1,0:T(2,128)} custom-call(f32[2,64]{1,0:T(2,128)} %pad_maximum_fusion.2.refs_0_), custom_call_target="tpu_custom_call" | custom-call | tf_op jit(solution)/shard_map/pallas_call | solution.py:55
  360.7 0.8 fusion.59
  361.6 0.8 subtract_subtract_fusion
  362.3 1.4 convert_reduce_fusion
  363.8 0.7 bitcast_add_fusion
  (24 shorter events, 0.2 us)
Async XLA Ops:
  7.2 328.9 %copy-start = (bf16[2304,512]{1,0:T(8,128)(2,1)S(1)}, bf16[2304,512]{1,0:T(8,128)(2,1)}, u32[]{:S(2)}) copy-start(bf16[2304,512]{1,0:T(8,128)(2,1)} %param.20) | copy-start | bytes 7077892
  7.2 230.1 %all-gather.2.cloned.1.call-start = ((), (), s32[]{:S(2)}) async-start(), calls=%async_computation | async-start | bytes 22560768 | tf_op jit(solution)/shard_map/all_gather | solution.py:109
  7.2 2.9 copy-start.2
  7.2 16.6 %copy-start.8 = (f32[144]{0:T(256)S(1)}, f32[144]{0:T(256)}, u32[]{:S(2)}) copy-start(f32[144]{0:T(256)} %param.14) | copy-start | bytes 1732
  10.1 74.3 %copy-start.4 = (s32[256,2]{0,1:T(2,128)S(1)}, s32[256,2]{0,1:T(2,128)}, u32[]{:S(2)}) copy-start(s32[256,2]{0,1:T(2,128)} %param.12) | copy-start | bytes 6148
  10.1 74.6 %copy-start.5 = (bf16[2304,4]{0,1:T(4,128)(2,1)S(1)}, bf16[2304,4]{0,1:T(4,128)(2,1)}, u32[]{:S(2)}) copy-start(bf16[2304,4]{0,1:T(4,128)(2,1)} %param.15) | copy-start | bytes 55300
  86.2 151.1 %copy-start.1 = (bf16[16,144,256]{2,1,0:T(8,128)(2,1)S(1)}, bf16[16,144,256]{2,1,0:T(8,128)(2,1)}, u32[]{:S(2)}) copy-start(bf16[16,144,256]{2,1,0:T(8,128)(2,1)} %shard_map.123) | copy-start | bytes 3538948
  93.7 0.6 copy-start.7
  245.9 2.9 copy-start.10
  248.8 5.7 %copy-start.9 = (f32[256,1]{0,1:T(1,128)S(1)}, f32[256,1]{0,1:T(1,128)}, u32[]{:S(2)}) copy-start(f32[256,1]{0,1:T(1,128)} %get-tuple-element.19) | copy-start | bytes 3076
  275.2 21.0 %copy-start.6 = (f32[2304]{0:T(1024)S(1)}, f32[2304]{0:T(1024)}, u32[]{:S(2)}) copy-start(f32[2304]{0:T(1024)} %param.19) | copy-start | bytes 27652
  276.6 59.5 %copy-start.11 = (f32[64]{0:T(128)S(1)}, f32[64]{0:T(128)}, u32[]{:S(2)}) copy-start(f32[64]{0:T(128)} %broadcast_multiply_fusion.1) | copy-start | bytes 772
  336.1 27.6 %copy-start.3 = (f32[256,144]{0,1:T(8,128)S(1)}, f32[256,144]{0,1:T(8,128)}, u32[]{:S(2)}) copy-start(f32[256,144]{0,1:T(8,128)} %param.11) | copy-start | bytes 442372
Sparse Core Ops, SparseCore 0:
  10.7 226.5 all-gather.1

commit v5 on v4

--- a/solution.py
+++ b/solution.py
@@ -148,12 +148,19 @@
     end_normed = (
         end_rows * lax.rsqrt(end_squares / EMBED_DIMENSION + epsilon)[:, None] * terminal_rmsnorm_gain
     ).astype(jnp.bfloat16)
-    swapped, head_rows = mesh_share(
-        [(column_blocks, "mp", True), (end_normed, "dp", False)],
-        {"mp": columns_count, "dp": groups},
-        7,
-    )
-    branch = jnp.sum(swapped.astype(jnp.float32), axis=0).T
+    head_rows = axis_gather(end_normed, "dp", groups, 7)
+    me = lax.axis_index("mp")
+    own = lax.dynamic_index_in_dim(column_blocks, me, 0, keepdims=False)
+    branch_t = own.astype(jnp.float32)
+    for shift in range(1, columns_count):
+        outgoing = lax.dynamic_index_in_dim(
+            column_blocks, lax.rem(me + shift, columns_count), 0, keepdims=False
+        )
+        incoming = lax.ppermute(
+            outgoing, "mp", [(i, (i + shift) % columns_count) for i in range(columns_count)]
+        )
+        branch_t = branch_t + incoming.astype(jnp.float32)
+    branch = branch_t.T
     new_hidden = skip_stream_arriving + branch_scale * branch
     lexicon_projector_feed = head_rows.reshape(groups * end_normed.shape[0], EMBED_DIMENSION)
     lexicon_logit_values = jnp.dot(

time: 374 us -> 388 us (1.037)
  starting transfers between devices: 0.04 us -> 25.2 us
  Pallas kernels: 148 us -> 124 us
  waiting for transfers between devices: 139 us -> 146 us
    ppermute x0 -> x15, starting transfers between devices: none -> 25.2 us  [body(): lax.ppermute(outgoing, 'mp', [(i, (i + shift) % columns_count) for i in r...]
    pallas_call x6, Pallas kernels: 148 us -> 124 us  [mesh_share(): pl.pallas_call(kernel, out_shape=[jax.ShapeDtypeStruct(array.shape if spl...]
    ppermute x0 -> x15, waiting for transfers between devices: none -> 5.83 us  [body(): lax.ppermute(outgoing, 'mp', [(i, (i + shift) % columns_count) for i in r...]
  transfers between devices with their start and end apart: 1 -> 16, of which waited for: 1 -> 5; matrix products, arithmetic and copies ran while one was open for 4% -> 5% of each run, Pallas kernels for 19% -> 18%
where the time goes in v5:
time: 388 us; the launch traced here: 385 us
  waiting for transfers between devices  146 us (38%)
  Pallas kernels  124 us (32%)
  matrix products  39.2 us (10%)
  starting transfers between devices  25.2 us (6%)
  local copies, waits for them, and re-layouts  18.6 us (5%)
  other arithmetic  18.3 us (5%)
  between operations  14.4 us (4%)
    all_gather x1, waiting for transfers between devices, body(): lax.all_gather(jnp.stack([specialist_switch_weights, specialist_expand_we...  140 us
    pallas_call x6, Pallas kernels, mesh_share(): pl.pallas_call(kernel, out_shape=[jax.ShapeDtypeStruct(array.shape if spl...  124 us
    ppermute x15, starting transfers between devices, body(): lax.ppermute(outgoing, 'mp', [(i, (i + shift) % columns_count) for i in r...  25.2 us
    dot_general x4, matrix products, body(): jnp.dot(all_weights[expert, 2], act_t, preferred_element_type=jnp.float32)  24.6 us
    dot_general x4, matrix products, body(): lax.dot_general(all_weights[expert, 0], features_t, by_rows, preferred_el...  11.5 us
  transfers between devices with their start and end apart: 16, of which 5 were waited for; matrix products, arithmetic and copies ran while one was open for 5% of the time, Pallas kernels for 18%

profile of v5, /device:TPU:8, one launch (start us, length us, event | category | flops | bytes accessed | tf_op | source)
XLA Modules:
  0.0 385.5 jit_solution(7442138159763798414)
XLA Ops:
  7.2 2.8 pad_maximum_fusion
  10.2 0.8 copy.76
  11.0 0.6 multiply_reduce_fusion
  11.6 11.5 %shard_map.122 = f32[16,1,256]{2,1,0:T(1,128)} custom-call(f32[1,256]{1,0:T(1,128)} %bitcast.167), custom_call_target="tpu_custom_call" | custom-call | tf_op jit(solution)/shard_map/pallas_call | solution.py:55
  23.1 0.8 reduce_sum.73
  23.9 0.7 fusion.61.refs_0_
  24.6 59.7 %shard_map.123 = bf16[16,144,256]{2,1,0:T(8,128)(2,1)} custom-call(bf16[144,256]{1,0:T(8,128)(2,1)} %fusion.61.refs_0_), custom_call_target="tpu_custom_call" | custom-call | tf_op jit(solution)/shard_map/pallas_call | solution.py:55
  84.7 1.5 fusion.79
  86.2 4.9 %gather_fusion.2 = f32[512]{0:T(512)S(1)} fusion(f32[256,4]{0,1:T(4,128)S(1)} %fusion.79, s32[512]{0:T(512)S(1)} %reshape.219), kind=kCustom, calls=%fused_computation.2 | custom fusion | bytes 8192 | tf_op jit(solution)/shard_map/jit(take_along_axis)/gather | solution.py:108
  91.1 0.8 reshape.222
  91.9 1.0 copy.74
  92.8 0.8 reduce-window.4
  93.7 2.2 gather_fusion.1
  95.9 1.2 broadcast_multiply_fusion.1
  97.1 0.6 fusion.69
  97.7 139.7 %all-gather.2.cloned.1.call-done = bf16[4,3,2304,360]{3,2,0,1:T(8,128)(2,1)} async-done(((bf16[4,3,144,360]{3,2,0,1:T(8,128)(2,1)}), bf16[4,3,2304,360]{3,2,0,1:T(8,128)(2,1)}) %all-gather.2.cloned.1.call-update) | async-done | bytes 19906576 | tf_op jit(solution)/shard_map/all_gather | solution.py:109
  237.5 2.8 fusion.11
  240.3 2.9 fusion.9
  243.2 2.9 fusion.7
  246.1 2.9 fusion.5
  249.0 5.7 %convolution_multiply_fusion.3 = f32[2304,256]{1,0:T(8,128)} fusion(bf16[4,3,2304,360]{3,2,0,1:T(8,128)(2,1)} %all-gather.2.cloned.1.call-done, f32[256]{0:T(256)S(1)} %bitcast.173, bf16[2304,256]{1,0:T(8,128)(2,1)S(1)} %bitcast.149, f32[360,256]{1,0:T(8,128)} %fusion.11), kind=kOutput, calls=%fused_computation.9 | convolution fusion | flops 850489344 | bytes 7447552 | tf_op jit(solution)/shard_map/dot_general | solution.py:132
  254.6 6.5 %fusion.2 = f32[2304,256]{1,0:T(8,128)} fusion(f32[2304,256]{1,0:T(8,128)} %convolution_multiply_fusion.3, bf16[4,3,2304,360]{3,2,0,1:T(8,128)(2,1)} %all-gather.2.cloned.1.call-done, f32[256]{0:T(256)S(1)} %bitcast.172, bf16[2304,256]{1,0:T(8,128)(2,1)S(1)} %bitcast.150, f32[360,256]{1,0:T(8,128)} %fusion.9), kind=kOutput, calls=%fused_computation.8 | convolution fusion | flops 851079168 | bytes 9806848 | tf_op jit(solution)/shard_map/dot_general | solution.py:132
  261.1 6.5 %fusion.1 = f32[2304,256]{1,0:T(8,128)} fusion(f32[2304,256]{1,0:T(8,128)} %fusion.2, bf16[4,3,2304,360]{3,2,0,1:T(8,128)(2,1)} %all-gather.2.cloned.1.call-done, f32[256]{0:T(256)S(1)} %bitcast.171, bf16[2304,256]{1,0:T(8,128)(2,1)S(1)} %bitcast.151, f32[360,256]{1,0:T(8,128)} %fusion.7), kind=kOutput, calls=%fused_computation.6 | convolution fusion | flops 851079168 | bytes 9806848 | tf_op jit(solution)/shard_map/dot_general | solution.py:132
  267.6 6.0 %fusion.3 = bf16[2304,256]{1,0:T(8,128)(2,1)} fusion(f32[2304,256]{1,0:T(8,128)} %fusion.1, bf16[4,3,2304,360]{3,2,0,1:T(8,128)(2,1)} %all-gather.2.cloned.1.call-done, f32[256]{0:T(256)S(1)} %bitcast.170, bf16[2304,256]{1,0:T(8,128)(2,1)S(1)} %bitcast.152, f32[360,256]{1,0:T(8,128)} %fusion.5), kind=kOutput, calls=%fused_computation.10 | convolution fusion | flops 851668992 | bytes 8627200 | tf_op jit(solution)/shard_map/dot_general | solution.py:132
  273.6 1.7 copy.75
  275.4 1.4 gather_fusion
  276.8 16.3 %shard_map.124 = (bf16[16,4,2304]{2,1,0:T(4,128)(2,1)}, f32[16,4,144]{2,1,0:T(4,128)}) custom-call(bf16[4,2304]{1,0:T(4,128)(2,1)} %gather_fusion, f32[4,144]{1,0:T(4,128)} %gather_fusion.1), custom_call_target="tpu_custom_call" | custom-call | tf_op jit(solution)/shard_map/pallas_call | solution.py:55
  293.1 1.1 convert_reduce_fusion
  294.4 1.0 fusion.63
  295.4 0.9 copy.77
  296.4 0.7 multiply_convert_fusion.1.refs_0_
  297.0 13.4 %shard_map.125 = bf16[16,4,2304]{2,1,0:T(4,128)(2,1)} custom-call(bf16[4,2304]{1,0:T(4,128)(2,1)} %multiply_convert_fusion.1.refs_0_), custom_call_target="tpu_custom_call" | custom-call | tf_op jit(solution)/shard_map/pallas_call | solution.py:55
  310.5 1.8 reshape.201
  312.3 1.6 fusion.78
  313.9 0.7 copy-done.4
  314.8 0.6 pad_maximum_fusion.1.refs_0_
  315.4 11.7 %shard_map.126 = f32[16,2,64]{2,1,0:T(2,128)} custom-call(f32[2,64]{1,0:T(2,128)} %pad_maximum_fusion.1.refs_0_), custom_call_target="tpu_custom_call" | custom-call | tf_op jit(solution)/shard_map/pallas_call | solution.py:55
  327.1 0.8 fusion.77
  327.9 0.5 reduce_max.38
  328.4 0.6 multiply_reduce_fusion.2
  329.1 1.2 pad_maximum_fusion.2.refs_0_
  330.2 11.5 %shard_map.127 = f32[16,2,64]{2,1,0:T(2,128)} custom-call(f32[2,64]{1,0:T(2,128)} %pad_maximum_fusion.2.refs_0_), custom_call_target="tpu_custom_call" | custom-call | tf_op jit(solution)/shard_map/pallas_call | solution.py:55
  341.7 1.0 dynamic-slice_bitcast_fusion.14
  342.8 0.6 collective-permute-start
  343.4 1.5 collective-permute-start.1
  344.9 4.1 %collective-permute-start.10 = (bf16[144,256]{1,0:T(8,128)(2,1)}, bf16[144,256]{1,0:T(8,128)(2,1)}, u32[]{:S(2)}, u32[]{:S(2)}) collective-permute-start(bf16[144,256]{1,0:T(8,128)(2,1)} %get-tuple-element.13), channel_id=1, source_target_pairs={{0,11},{1,12},{2,13},{3,14},{4,15},{5,0},{6,1},{7,2},{8,3},{9,4},{... | collective-permute-start | bytes 221192 | tf_op jit(solution)/shard_map/ppermute | solution.py:159
  349.0 1.4 collective-permute-start.11
  350.4 0.6 reduce_max.39
  351.0 1.2 collective-permute-done
  352.4 2.5 collective-permute-done.1
  354.9 0.5 collective-permute-start.14
  355.4 1.2 collective-permute-start.2
  356.6 1.8 collective-permute-start.3
  358.4 2.4 collective-permute-start.4
  360.7 0.7 multiply_reduce_fusion.1
  361.4 1.1 collective-permute-start.5
  362.5 5.8 %collective-permute-start.6 = (bf16[144,256]{1,0:T(8,128)(2,1)}, bf16[144,256]{1,0:T(8,128)(2,1)S(1)}, u32[]{:S(2)}, u32[]{:S(2)}) collective-permute-start(bf16[144,256]{1,0:T(8,128)(2,1)} %get-tuple-element.17), channel_id=1, source_target_pairs={{0,7},{1,8},{2,9},{3,10},{4,11},{5,12},{6,13},{7,14},{8,15},{9,0},... | collective-permute-start | bytes 221192 | tf_op jit(solution)/shard_map/ppermute | solution.py:159
  368.3 0.3 collective-permute-start.7
  368.6 0.9 collective-permute-start.8
  369.6 3.4 collective-permute-start.9
  372.9 1.6 subtract_subtract_fusion
  374.6 1.4 collective-permute-done.8
  376.0 0.7 collective-permute-done.9
  376.7 2.0 fusion.60
  (58 shorter events, 1.2 us)
Async XLA Ops:
  7.2 305.2 %copy-start = (bf16[2304,512]{1,0:T(8,128)(2,1)S(1)}, bf16[2304,512]{1,0:T(8,128)(2,1)}, u32[]{:S(2)}) copy-start(bf16[2304,512]{1,0:T(8,128)(2,1)} %param.20) | copy-start | bytes 7077892
  7.2 230.3 %all-gather.2.cloned.1.call-start = ((), (), s32[]{:S(2)}) async-start(), calls=%async_computation | async-start | bytes 22560768 | tf_op jit(solution)/shard_map/all_gather | solution.py:109
  7.2 2.9 copy-start.3
  7.2 16.7 %copy-start.10 = (f32[144]{0:T(256)S(1)}, f32[144]{0:T(256)}, u32[]{:S(2)}) copy-start(f32[144]{0:T(256)} %param.14) | copy-start | bytes 1732
  10.1 74.3 %copy-start.6 = (s32[256,2]{0,1:T(2,128)S(1)}, s32[256,2]{0,1:T(2,128)}, u32[]{:S(2)}) copy-start(s32[256,2]{0,1:T(2,128)} %param.12) | copy-start | bytes 6148
  10.1 74.6 %copy-start.7 = (bf16[2304,4]{0,1:T(4,128)(2,1)S(1)}, bf16[2304,4]{0,1:T(4,128)(2,1)}, u32[]{:S(2)}) copy-start(bf16[2304,4]{0,1:T(4,128)(2,1)} %param.15) | copy-start | bytes 55300
  86.2 151.3 %copy-start.1 = (bf16[16,144,256]{2,1,0:T(8,128)(2,1)S(1)}, bf16[16,144,256]{2,1,0:T(8,128)(2,1)}, u32[]{:S(2)}) copy-start(bf16[16,144,256]{2,1,0:T(8,128)(2,1)} %shard_map.123) | copy-start | bytes 3538948
  93.7 2.2 copy-start.9
  246.1 2.9 copy-start.12
  249.0 5.7 %copy-start.11 = (f32[256,1]{0,1:T(1,128)S(1)}, f32[256,1]{0,1:T(1,128)}, u32[]{:S(2)}) copy-start(f32[256,1]{0,1:T(1,128)} %get-tuple-element.30) | copy-start | bytes 3076
  275.4 21.0 %copy-start.8 = (f32[2304]{0:T(1024)S(1)}, f32[2304]{0:T(1024)}, u32[]{:S(2)}) copy-start(f32[2304]{0:T(1024)} %param.19) | copy-start | bytes 27652
  276.8 35.5 %copy-start.13 = (f32[64]{0:T(128)S(1)}, f32[64]{0:T(128)}, u32[]{:S(2)}) copy-start(f32[64]{0:T(128)} %broadcast_multiply_fusion.1) | copy-start | bytes 772
  310.5 31.3 %copy-start.2 = (bf16[2304,256]{1,0:T(8,128)(2,1)S(1)}, bf16[2304,256]{1,0:T(8,128)(2,1)}, u32[]{:S(2)}) copy-start(bf16[2304,256]{1,0:T(8,128)(2,1)} %fusion.3) | copy-start | bytes 3538948
  313.9 0.7 copy-start.4
  341.7 8.7 %copy-start.5 = (f32[16,2,64]{2,1,0:T(2,128)S(1)}, f32[16,2,64]{2,1,0:T(2,128)}, u32[]{:S(2)}) copy-start(f32[16,2,64]{2,1,0:T(2,128)} %shard_map.127) | copy-start | bytes 24580
  342.8 9.4 %collective-permute-start = (bf16[144,256]{1,0:T(8,128)(2,1)}, bf16[144,256]{1,0:T(8,128)(2,1)}, u32[]{:S(2)}, u32[]{:S(2)}) collective-permute-start(bf16[144,256]{1,0:T(8,128)(2,1)} %get-tuple-element.8), channel_id=1, source_target_pairs={{0,1},{1,2},{2,3},{3,4},{4,5},{5,6},{6,7},{7,8},{8,9},{9,10},{10,1... | collective-permute-start | bytes 221192 | tf_op jit(solution)/shard_map/ppermute | solution.py:159
  343.4 11.5 %collective-permute-start.1 = (bf16[144,256]{1,0:T(8,128)(2,1)}, bf16[144,256]{1,0:T(8,128)(2,1)}, u32[]{:S(2)}, u32[]{:S(2)}) collective-permute-start(bf16[144,256]{1,0:T(8,128)(2,1)} %get-tuple-element.22), channel_id=1, source_target_pairs={{0,2},{1,3},{2,4},{3,5},{4,6},{5,7},{6,8},{7,9},{8,10},{9,11},{10,... | collective-permute-start | bytes 221192 | tf_op jit(solution)/shard_map/ppermute | solution.py:159
  344.9 10.5 %collective-permute-start.10 = (bf16[144,256]{1,0:T(8,128)(2,1)}, bf16[144,256]{1,0:T(8,128)(2,1)}, u32[]{:S(2)}, u32[]{:S(2)}) collective-permute-start(bf16[144,256]{1,0:T(8,128)(2,1)} %get-tuple-element.13), channel_id=1, source_target_pairs={{0,11},{1,12},{2,13},{3,14},{4,15},{5,0},{6,1},{7,2},{8,3},{9,4},{... | collective-permute-start | bytes 221192 | tf_op jit(solution)/shard_map/ppermute | solution.py:159
  349.0 7.6 %collective-permute-start.11 = (bf16[144,256]{1,0:T(8,128)(2,1)}, bf16[144,256]{1,0:T(8,128)(2,1)}, u32[]{:S(2)}, u32[]{:S(2)}) collective-permute-start(bf16[144,256]{1,0:T(8,128)(2,1)} %get-tuple-element.12), channel_id=1, source_target_pairs={{0,12},{1,13},{2,14},{3,15},{4,0},{5,1},{6,2},{7,3},{8,4},{9,5},{1... | collective-permute-start | bytes 221192 | tf_op jit(solution)/shard_map/ppermute | solution.py:159
  350.4 8.0 %collective-permute-start.12 = (bf16[144,256]{1,0:T(8,128)(2,1)}, bf16[144,256]{1,0:T(8,128)(2,1)}, u32[]{:S(2)}, u32[]{:S(2)}) collective-permute-start(bf16[144,256]{1,0:T(8,128)(2,1)} %get-tuple-element.11), channel_id=1, source_target_pairs={{0,13},{1,14},{2,15},{3,0},{4,1},{5,2},{6,3},{7,4},{8,5},{9,6},{10... | collective-permute-start | bytes 221192 | tf_op jit(solution)/shard_map/ppermute | solution.py:159
  352.2 9.2 %collective-permute-start.13 = (bf16[144,256]{1,0:T(8,128)(2,1)}, bf16[144,256]{1,0:T(8,128)(2,1)S(1)}, u32[]{:S(2)}, u32[]{:S(2)}) collective-permute-start(bf16[144,256]{1,0:T(8,128)(2,1)} %get-tuple-element.10), channel_id=1, source_target_pairs={{0,14},{1,15},{2,0},{3,1},{4,2},{5,3},{6,4},{7,5},{8,6},{9,7},{10,... | collective-permute-start | bytes 221192 | tf_op jit(solution)/shard_map/ppermute | solution.py:159
  354.9 7.6 %collective-permute-start.14 = (bf16[144,256]{1,0:T(8,128)(2,1)}, bf16[144,256]{1,0:T(8,128)(2,1)S(1)}, u32[]{:S(2)}, u32[]{:S(2)}) collective-permute-start(bf16[144,256]{1,0:T(8,128)(2,1)} %get-tuple-element.9), channel_id=1, source_target_pairs={{0,15},{1,0},{2,1},{3,2},{4,3},{5,4},{6,5},{7,6},{8,7},{9,8},{10,9... | collective-permute-start | bytes 221192 | tf_op jit(solution)/shard_map/ppermute | solution.py:159
  355.4 12.9 %collective-permute-start.2 = (bf16[144,256]{1,0:T(8,128)(2,1)}, bf16[144,256]{1,0:T(8,128)(2,1)S(1)}, u32[]{:S(2)}, u32[]{:S(2)}) collective-permute-start(bf16[144,256]{1,0:T(8,128)(2,1)} %get-tuple-element.21), channel_id=1, source_target_pairs={{0,3},{1,4},{2,5},{3,6},{4,7},{5,8},{6,9},{7,10},{8,11},{9,12},{10... | collective-permute-start | bytes 221192 | tf_op jit(solution)/shard_map/ppermute | solution.py:159
  356.6 12.0 %collective-permute-start.3 = (bf16[144,256]{1,0:T(8,128)(2,1)}, bf16[144,256]{1,0:T(8,128)(2,1)S(1)}, u32[]{:S(2)}, u32[]{:S(2)}) collective-permute-start(bf16[144,256]{1,0:T(8,128)(2,1)} %get-tuple-element.20), channel_id=1, source_target_pairs={{0,4},{1,5},{2,6},{3,7},{4,8},{5,9},{6,10},{7,11},{8,12},{9,13},{1... | collective-permute-start | bytes 221192 | tf_op jit(solution)/shard_map/ppermute | solution.py:159
  358.4 11.2 %collective-permute-start.4 = (bf16[144,256]{1,0:T(8,128)(2,1)}, bf16[144,256]{1,0:T(8,128)(2,1)S(1)}, u32[]{:S(2)}, u32[]{:S(2)}) collective-permute-start(bf16[144,256]{1,0:T(8,128)(2,1)} %get-tuple-element.19), channel_id=1, source_target_pairs={{0,5},{1,6},{2,7},{3,8},{4,9},{5,10},{6,11},{7,12},{8,13},{9,14},{... | collective-permute-start | bytes 221192 | tf_op jit(solution)/shard_map/ppermute | solution.py:159
  361.4 13.2 %collective-permute-start.5 = (bf16[144,256]{1,0:T(8,128)(2,1)}, bf16[144,256]{1,0:T(8,128)(2,1)S(1)}, u32[]{:S(2)}, u32[]{:S(2)}) collective-permute-start(bf16[144,256]{1,0:T(8,128)(2,1)} %get-tuple-element.18), channel_id=1, source_target_pairs={{0,6},{1,7},{2,8},{3,9},{4,10},{5,11},{6,12},{7,13},{8,14},{9,15},... | collective-permute-start | bytes 221192 | tf_op jit(solution)/shard_map/ppermute | solution.py:159
  362.5 12.1 %collective-permute-start.6 = (bf16[144,256]{1,0:T(8,128)(2,1)}, bf16[144,256]{1,0:T(8,128)(2,1)S(1)}, u32[]{:S(2)}, u32[]{:S(2)}) collective-permute-start(bf16[144,256]{1,0:T(8,128)(2,1)} %get-tuple-element.17), channel_id=1, source_target_pairs={{0,7},{1,8},{2,9},{3,10},{4,11},{5,12},{6,13},{7,14},{8,15},{9,0},... | collective-permute-start | bytes 221192 | tf_op jit(solution)/shard_map/ppermute | solution.py:159
  368.3 6.3 %collective-permute-start.7 = (bf16[144,256]{1,0:T(8,128)(2,1)}, bf16[144,256]{1,0:T(8,128)(2,1)S(1)}, u32[]{:S(2)}, u32[]{:S(2)}) collective-permute-start(bf16[144,256]{1,0:T(8,128)(2,1)} %get-tuple-element.16), channel_id=1, source_target_pairs={{0,8},{1,9},{2,10},{3,11},{4,12},{5,13},{6,14},{7,15},{8,0},{9,1},... | collective-permute-start | bytes 221192 | tf_op jit(solution)/shard_map/ppermute | solution.py:159
  368.6 7.3 %collective-permute-start.8 = (bf16[144,256]{1,0:T(8,128)(2,1)}, bf16[144,256]{1,0:T(8,128)(2,1)S(1)}, u32[]{:S(2)}, u32[]{:S(2)}) collective-permute-start(bf16[144,256]{1,0:T(8,128)(2,1)} %get-tuple-element.15), channel_id=1, source_target_pairs={{0,9},{1,10},{2,11},{3,12},{4,13},{5,14},{6,15},{7,0},{8,1},{9,2},... | collective-permute-start | bytes 221192 | tf_op jit(solution)/shard_map/ppermute | solution.py:159
  369.6 7.1 %collective-permute-start.9 = (bf16[144,256]{1,0:T(8,128)(2,1)}, bf16[144,256]{1,0:T(8,128)(2,1)S(1)}, u32[]{:S(2)}, u32[]{:S(2)}) collective-permute-start(bf16[144,256]{1,0:T(8,128)(2,1)} %get-tuple-element.14), channel_id=1, source_target_pairs={{0,10},{1,11},{2,12},{3,13},{4,14},{5,15},{6,0},{7,1},{8,2},{9,3},... | collective-permute-start | bytes 221192 | tf_op jit(solution)/shard_map/ppermute | solution.py:159
Sparse Core Ops, SparseCore 0:
  10.7 226.7 all-gather.1

commit v6 on v3

--- a/solution.py
+++ b/solution.py
@@ -69,6 +69,63 @@
     return axis_share([(block, False)], axis, count, tag)[0]
 
 
+def stats_combine(tile, counts, tag):
+    axes = ("mp", "dp")
+
+    def merge(buffer):
+        top = jnp.max(buffer[:, 0, :], axis=0, keepdims=True)
+        total = jnp.sum(buffer[:, 1, :] * jnp.exp(buffer[:, 0, :] - top), axis=0, keepdims=True)
+        return top, total
+
+    def kernel(x_ref, out_ref, first, second, middle, send_sem, recv_sem):
+        barrier = pltpu.get_barrier_semaphore()
+        for axis in axes:
+            me = lax.axis_index(axis)
+            for step in range(1, counts[axis]):
+                peer = lax.rem(me + step, counts[axis])
+                pl.semaphore_signal(barrier, 1, device_id={axis: peer},
+                                    device_id_type=pl.DeviceIdType.MESH)
+        pl.semaphore_wait(barrier, sum(counts[axis] - 1 for axis in axes))
+        stages = ((x_ref, first), (middle, second))
+        for index, axis in enumerate(axes):
+            source, target = stages[index]
+            me = lax.axis_index(axis)
+            copies = []
+            for step in range(1, counts[axis]):
+                peer = lax.rem(me + step, counts[axis])
+                copy = pltpu.make_async_remote_copy(
+                    src_ref=source, dst_ref=target.at[me],
+                    send_sem=send_sem.at[index, step], recv_sem=recv_sem.at[index, step],
+                    device_id={axis: peer}, device_id_type=pl.DeviceIdType.MESH)
+                copy.start()
+                copies.append(copy)
+            target[me] = source[...]
+            for copy in copies:
+                copy.wait_send()
+                copy.wait_recv()
+            top, total = merge(target[...])
+            result = out_ref if index == 1 else middle
+            result[...] = jnp.zeros(result.shape, result.dtype)
+            result[0:1, :] = top
+            result[1:2, :] = total
+
+    count = max(counts.values())
+    return pl.pallas_call(
+        kernel,
+        out_shape=jax.ShapeDtypeStruct(tile.shape, tile.dtype),
+        in_specs=[pl.BlockSpec(memory_space=pltpu.VMEM)],
+        out_specs=pl.BlockSpec(memory_space=pltpu.VMEM),
+        scratch_shapes=[
+            pltpu.VMEM((counts["mp"],) + tile.shape, tile.dtype),
+            pltpu.VMEM((counts["dp"],) + tile.shape, tile.dtype),
+            pltpu.VMEM(tile.shape, tile.dtype),
+            pltpu.SemaphoreType.DMA((2, count)),
+            pltpu.SemaphoreType.DMA((2, count)),
+        ],
+        compiler_params=pltpu.CompilerParams(collective_id=tag, has_side_effects=True),
+    )(tile)
+
+
 def body(
     skip_stream_arriving,
     chosen_specialists,
@@ -152,12 +209,11 @@
     ) / (EMBED_DIMENSION / 256.0 * softness_per_sequence[:, None])
     local_max = jnp.max(lexicon_logit_values, axis=1)
     local_sum = jnp.sum(jnp.exp(lexicon_logit_values - local_max[:, None]), axis=1)
-    stats = jnp.stack([local_max, local_sum])
-    for axis, count, tag in (("mp", columns_count, 3), ("dp", groups, 4)):
-        held = axis_gather(stats, axis, count, tag)
-        top = jnp.max(held[:, 0], axis=0)
-        stats = jnp.stack([top, jnp.sum(held[:, 1] * jnp.exp(held[:, 0] - top[None]), axis=0)])
-    largest, total_exp = stats[0], stats[1]
+    requests = local_max.shape[0]
+    tile = jnp.zeros((8, 128), jnp.float32)
+    tile = tile.at[0, :requests].set(local_max).at[1, :requests].set(local_sum)
+    merged = stats_combine(tile, {"mp": columns_count, "dp": groups}, 3)
+    largest, total_exp = merged[0, :requests], merged[1, :requests]
     logprobs = lexicon_logit_values - largest[:, None] - jnp.log(total_exp)[:, None]
     return (new_hidden, logprobs)
 

time: 374 us -> 368 us (0.984)
  Pallas kernels: 269 us -> 265 us
    pallas_call x7 -> x5, Pallas kernels: 269 us -> 247 us  [axis_share(): pl.pallas_call(kernel, out_shape=[jax.ShapeDtypeStruct(array.shape if spl...]
    pallas_call x0 -> x1, Pallas kernels: none -> 17.8 us  [stats_combine(): pl.pallas_call(kernel, out_shape=jax.ShapeDtypeStruct(tile.shape, tile.dt...]
where the time goes in v6:
time: 368 us; the launch traced here: 366 us
  Pallas kernels  265 us (72%)
  matrix products  38.2 us (10%)
  local copies, waits for them, and re-layouts  18.6 us (5%)
  waiting for transfers between devices  16 us (4%)
  between operations  14.3 us (4%)
  other arithmetic  13.4 us (4%)
    pallas_call x5, Pallas kernels, axis_share(): pl.pallas_call(kernel, out_shape=[jax.ShapeDtypeStruct(array.shape if spl...  247 us
    dot_general x4, matrix products, body(): jnp.dot(all_weights[expert, 2], act_t, preferred_element_type=jnp.float32)  24.6 us
    pallas_call x1, Pallas kernels, stats_combine(): pl.pallas_call(kernel, out_shape=jax.ShapeDtypeStruct(tile.shape, tile.dt...  17.8 us
    all_gather x1, waiting for transfers between devices, body(): lax.all_gather(jnp.stack([specialist_switch_weights, specialist_expand_we...  16 us
    dot_general x4, matrix products, body(): lax.dot_general(all_weights[expert, 0], features_t, by_rows, preferred_el...  11.5 us
  transfers between devices with their start and end apart: 1, of which 1 were waited for; matrix products, arithmetic and copies ran while one was open for 5% of the time, Pallas kernels for 52%

profile of v6, /device:TPU:8, one launch (start us, length us, event | category | flops | bytes accessed | tf_op | source)
XLA Modules:
  0.0 365.7 jit_solution(10764925769851985142)
XLA Ops:
  7.2 0.0 copy-start
  7.2 0.0 all-gather.2.cloned.1.call-start
  7.2 0.0 copy-start.2
  7.2 0.0 copy-start.9
  7.2 2.8 pad_maximum_fusion
  10.1 0.0 all-gather.2.cloned.1.call-update
  10.1 0.0 copy-done.2
  10.1 0.8 copy.70
  10.9 0.6 multiply_reduce_fusion
  11.5 11.5 %shard_map.122 = f32[16,1,256]{2,1,0:T(1,128)} custom-call(f32[1,256]{1,0:T(1,128)} %bitcast.118), custom_call_target="tpu_custom_call" | custom-call | tf_op jit(solution)/shard_map/pallas_call | solution.py:52
  23.0 0.8 reduce_sum.64
  23.8 0.0 copy-done.9
  23.8 0.7 fusion.44.refs_0_
  24.5 59.8 %shard_map.123 = bf16[16,144,256]{2,1,0:T(8,128)(2,1)} custom-call(bf16[144,256]{1,0:T(8,128)(2,1)} %fusion.44.refs_0_), custom_call_target="tpu_custom_call" | custom-call | tf_op jit(solution)/shard_map/pallas_call | solution.py:52
  84.3 0.0 copy-done.5
  84.4 0.1 copy.67
  84.5 0.1 reshape.278
  84.7 0.0 copy-done.6
  84.7 1.5 fusion.60
  86.2 4.9 %gather_fusion.2 = f32[512]{0:T(512)S(1)} fusion(f32[256,4]{0,1:T(4,128)S(1)} %fusion.60, s32[512]{0:T(512)S(1)} %reshape.278), kind=kCustom, calls=%fused_computation.2 | custom fusion | bytes 8192 | tf_op jit(solution)/shard_map/jit(take_along_axis)/gather | solution.py:160
  91.1 0.8 reshape.281
  91.9 1.0 copy.68
  92.8 0.8 reduce-window.4
  93.7 2.2 gather_fusion.1
  95.9 120.4 %shard_map.125 = f32[16,4,144]{2,1,0:T(4,128)} custom-call(f32[4,144]{1,0:T(4,128)} %gather_fusion.1), custom_call_target="tpu_custom_call" | custom-call | tf_op jit(solution)/shard_map/pallas_call | solution.py:52
  216.2 1.5 copy.71
  217.7 1.6 reshape.258
  219.3 1.2 broadcast_multiply_fusion.1
  220.5 0.6 fusion.52
  221.1 16.0 %all-gather.2.cloned.1.call-done = bf16[4,3,2304,360]{3,2,0,1:T(8,128)(2,1)} async-done(((bf16[4,3,144,360]{3,2,0,1:T(8,128)(2,1)}), bf16[4,3,2304,360]{3,2,0,1:T(8,128)(2,1)}) %all-gather.2.cloned.1.call-update) | async-done | bytes 19906576 | tf_op jit(solution)/shard_map/all_gather | solution.py:161
  237.1 0.0 copy-done.1
  237.1 2.9 fusion.11
  239.9 2.9 fusion.9
  242.8 2.9 fusion.7
  245.7 2.9 fusion.5
  248.6 0.0 copy-done.12
  248.6 5.7 %convolution_multiply_fusion.3 = f32[2304,256]{1,0:T(8,128)} fusion(bf16[4,3,2304,360]{3,2,0,1:T(8,128)(2,1)} %all-gather.2.cloned.1.call-done, f32[256]{0:T(256)S(1)} %bitcast.123, bf16[2304,256]{1,0:T(8,128)(2,1)S(1)} %bitcast.108, f32[360,256]{1,0:T(8,128)} %fusion.11), kind=kOutput, calls=%fused_computation.9 | convolution fusion | flops 850489344 | bytes 7447552 | tf_op jit(solution)/shard_map/dot_general | solution.py:184
  254.3 0.0 copy-done.11
  254.3 6.5 %fusion.2 = f32[2304,256]{1,0:T(8,128)} fusion(f32[2304,256]{1,0:T(8,128)} %convolution_multiply_fusion.3, bf16[4,3,2304,360]{3,2,0,1:T(8,128)(2,1)} %all-gather.2.cloned.1.call-done, f32[256]{0:T(256)S(1)} %bitcast.122, bf16[2304,256]{1,0:T(8,128)(2,1)S(1)} %bitcast.109, f32[360,256]{1,0:T(8,128)} %fusion.9), kind=kOutput, calls=%fused_computation.8 | convolution fusion | flops 851079168 | bytes 9806848 | tf_op jit(solution)/shard_map/dot_general | solution.py:184
  260.7 0.0 copy-done.10
  260.7 6.5 %fusion.1 = f32[2304,256]{1,0:T(8,128)} fusion(f32[2304,256]{1,0:T(8,128)} %fusion.2, bf16[4,3,2304,360]{3,2,0,1:T(8,128)(2,1)} %all-gather.2.cloned.1.call-done, f32[256]{0:T(256)S(1)} %bitcast.121, bf16[2304,256]{1,0:T(8,128)(2,1)S(1)} %bitcast.110, f32[360,256]{1,0:T(8,128)} %fusion.7), kind=kOutput, calls=%fused_computation.6 | convolution fusion | flops 851079168 | bytes 9806848 | tf_op jit(solution)/shard_map/dot_general | solution.py:184
  267.2 6.0 %fusion.3 = bf16[2304,256]{1,0:T(8,128)(2,1)} fusion(f32[2304,256]{1,0:T(8,128)} %fusion.1, bf16[4,3,2304,360]{3,2,0,1:T(8,128)(2,1)} %all-gather.2.cloned.1.call-done, f32[256]{0:T(256)S(1)} %bitcast.120, bf16[2304,256]{1,0:T(8,128)(2,1)S(1)} %bitcast.111, f32[360,256]{1,0:T(8,128)} %fusion.5), kind=kOutput, calls=%fused_computation.10 | convolution fusion | flops 851668992 | bytes 8627200 | tf_op jit(solution)/shard_map/dot_general | solution.py:184
  273.2 1.7 copy.69
  275.0 1.2 gather_fusion
  276.2 39.6 %shard_map.124 = (bf16[16,144,256]{2,1,0:T(8,128)(2,1)}, bf16[16,4,2304]{2,1,0:T(4,128)(2,1)}) custom-call(bf16[16,144,256]{2,1,0:T(8,128)(2,1)} %bitcast.112, bf16[4,2304]{1,0:T(4,128)(2,1)} %gather_fusion), custom_call_target="tpu_custom_call" | custom-call | tf_op jit(solution)/shard_map/pallas_call | solution.py:52
  315.7 1.1 convert_reduce_fusion.1
  316.8 0.1 mul.148
  316.9 1.0 fusion.46
  318.0 0.0 copy-done.4
  318.0 0.0 copy-done.8
  318.0 0.7 multiply_convert_fusion.1.refs_0_
  318.7 16.0 %shard_map.126 = bf16[16,4,2304]{2,1,0:T(4,128)(2,1)} custom-call(bf16[4,2304]{1,0:T(4,128)(2,1)} %multiply_convert_fusion.1.refs_0_), custom_call_target="tpu_custom_call" | custom-call | tf_op jit(solution)/shard_map/pallas_call | solution.py:52
  334.6 1.0 reshape.259
  335.7 0.0 copy-start.3
  335.7 0.6 fusion.59
  336.3 0.2 exponential_reduce_fusion
  336.5 0.2 scatter.9.x_ref
  336.7 0.0 copy-start.7
  336.8 0.6 copy-done.7
  337.3 17.8 %shard_map.127 = f32[8,128]{1,0:T(8,128)} custom-call(f32[8,128]{1,0:T(8,128)} %copy-done.7), custom_call_target="tpu_custom_call" | custom-call | tf_op jit(solution)/shard_map/pallas_call | solution.py:113
  355.2 0.8 slice_bitcast_fusion.48
  355.9 1.4 convert_reduce_fusion
  357.4 0.7 bitcast_add_fusion
  358.1 0.7 subtract_subtract_fusion
  (22 shorter events, 0.1 us)
Async XLA Ops:
  7.2 328.5 %copy-start = (bf16[2304,512]{1,0:T(8,128)(2,1)S(1)}, bf16[2304,512]{1,0:T(8,128)(2,1)}, u32[]{:S(2)}) copy-start(bf16[2304,512]{1,0:T(8,128)(2,1)} %param.24) | copy-start | bytes 7077892
  7.2 229.9 %all-gather.2.cloned.1.call-start = ((), (), s32[]{:S(2)}) async-start(), calls=%async_computation | async-start | bytes 22560768 | tf_op jit(solution)/shard_map/all_gather | solution.py:161
  7.2 2.9 copy-start.2
  7.2 16.6 %copy-start.9 = (f32[144]{0:T(256)S(1)}, f32[144]{0:T(256)}, u32[]{:S(2)}) copy-start(f32[144]{0:T(256)} %param.18) | copy-start | bytes 1732
  10.1 74.3 %copy-start.5 = (s32[256,2]{0,1:T(2,128)S(1)}, s32[256,2]{0,1:T(2,128)}, u32[]{:S(2)}) copy-start(s32[256,2]{0,1:T(2,128)} %param.16) | copy-start | bytes 6148
  10.1 74.6 %copy-start.6 = (bf16[2304,4]{0,1:T(4,128)(2,1)S(1)}, bf16[2304,4]{0,1:T(4,128)(2,1)}, u32[]{:S(2)}) copy-start(bf16[2304,4]{0,1:T(4,128)(2,1)} %param.19) | copy-start | bytes 55300
  86.2 150.9 %copy-start.1 = (bf16[16,144,256]{2,1,0:T(8,128)(2,1)S(1)}, bf16[16,144,256]{2,1,0:T(8,128)(2,1)}, u32[]{:S(2)}) copy-start(bf16[16,144,256]{2,1,0:T(8,128)(2,1)} %shard_map.123) | copy-start | bytes 3538948
  245.7 2.9 copy-start.12
  248.6 5.7 %copy-start.11 = (f32[256,1]{0,1:T(1,128)S(1)}, f32[256,1]{0,1:T(1,128)}, u32[]{:S(2)}) copy-start(f32[256,1]{0,1:T(1,128)} %get-tuple-element.37) | copy-start | bytes 3076
  254.3 6.5 %copy-start.10 = (f32[256,1]{0,1:T(1,128)S(1)}, f32[256,1]{0,1:T(1,128)}, u32[]{:S(2)}) copy-start(f32[256,1]{0,1:T(1,128)} %get-tuple-element.35) | copy-start | bytes 3076
  276.2 41.8 %copy-start.4 = (f32[4,2304]{1,0:T(4,128)S(1)}, f32[4,2304]{1,0:T(4,128)}, u32[]{:S(2)}) copy-start(f32[4,2304]{1,0:T(4,128)} %reshape.258) | copy-start | bytes 110596
  276.2 41.8 %copy-start.8 = (f32[2304]{0:T(1024)S(1)}, f32[2304]{0:T(1024)}, u32[]{:S(2)}) copy-start(f32[2304]{0:T(1024)} %param.23) | copy-start | bytes 27652
  276.2 59.5 %copy-start.13 = (f32[64]{0:T(128)S(1)}, f32[64]{0:T(128)}, u32[]{:S(2)}) copy-start(f32[64]{0:T(128)} %broadcast_multiply_fusion.1) | copy-start | bytes 772
  335.7 21.7 %copy-start.3 = (f32[256,144]{0,1:T(8,128)S(1)}, f32[256,144]{0,1:T(8,128)}, u32[]{:S(2)}) copy-start(f32[256,144]{0,1:T(8,128)} %param.15) | copy-start | bytes 442372
  336.7 0.6 copy-start.7
Sparse Core Ops, SparseCore 0:
  10.7 226.3 all-gather.1

commit v7 on v6

--- a/solution.py
+++ b/solution.py
@@ -126,6 +126,82 @@
     )(tile)
 
 
+def tail_exchange(blocks, end_parts, skip_ends, gain, counts, tag):
+    rows = end_parts.shape[0]
+
+    def kernel(blocks_ref, parts_ref, skip_ref, gain_ref, swapped_ref, head_ref,
+               parts_held, normed, send_sem, recv_sem):
+        barrier = pltpu.get_barrier_semaphore()
+        for axis in ("mp", "dp"):
+            me = lax.axis_index(axis)
+            for step in range(1, counts[axis]):
+                peer = lax.rem(me + step, counts[axis])
+                pl.semaphore_signal(barrier, 1, device_id={axis: peer},
+                                    device_id_type=pl.DeviceIdType.MESH)
+        pl.semaphore_wait(barrier, counts["mp"] + counts["dp"] - 2)
+        me = lax.axis_index("mp")
+        block_copies, part_copies = [], []
+        for step in range(1, counts["mp"]):
+            peer = lax.rem(me + step, counts["mp"])
+            copy = pltpu.make_async_remote_copy(
+                src_ref=parts_ref, dst_ref=parts_held.at[me],
+                send_sem=send_sem.at[0, step], recv_sem=recv_sem.at[0, step],
+                device_id={"mp": peer}, device_id_type=pl.DeviceIdType.MESH)
+            copy.start()
+            part_copies.append(copy)
+        for step in range(1, counts["mp"]):
+            peer = lax.rem(me + step, counts["mp"])
+            copy = pltpu.make_async_remote_copy(
+                src_ref=blocks_ref.at[peer], dst_ref=swapped_ref.at[me],
+                send_sem=send_sem.at[1, step], recv_sem=recv_sem.at[1, step],
+                device_id={"mp": peer}, device_id_type=pl.DeviceIdType.MESH)
+            copy.start()
+            block_copies.append(copy)
+        parts_held[me] = parts_ref[...]
+        swapped_ref[me] = blocks_ref[me]
+        for copy in part_copies:
+            copy.wait_send()
+            copy.wait_recv()
+        total = jnp.sum(parts_held[...].astype(jnp.float32), axis=0)
+        end_rows = skip_ref[...] + branch_scale * total
+        squares = jnp.sum(end_rows * end_rows, axis=1, keepdims=True)
+        normed[...] = (
+            end_rows * lax.rsqrt(squares / EMBED_DIMENSION + epsilon) * gain_ref[...]
+        ).astype(normed.dtype)
+        group = lax.axis_index("dp")
+        head_copies = []
+        for step in range(1, counts["dp"]):
+            peer = lax.rem(group + step, counts["dp"])
+            copy = pltpu.make_async_remote_copy(
+                src_ref=normed, dst_ref=head_ref.at[group],
+                send_sem=send_sem.at[2, step], recv_sem=recv_sem.at[2, step],
+                device_id={"dp": peer}, device_id_type=pl.DeviceIdType.MESH)
+            copy.start()
+            head_copies.append(copy)
+        head_ref[group] = normed[...]
+        for copy in block_copies + head_copies:
+            copy.wait_send()
+            copy.wait_recv()
+
+    count = max(counts.values())
+    return pl.pallas_call(
+        kernel,
+        out_shape=[
+            jax.ShapeDtypeStruct(blocks.shape, blocks.dtype),
+            jax.ShapeDtypeStruct((counts["dp"], rows, EMBED_DIMENSION), jnp.bfloat16),
+        ],
+        in_specs=[pl.BlockSpec(memory_space=pltpu.VMEM)] * 4,
+        out_specs=[pl.BlockSpec(memory_space=pltpu.VMEM)] * 2,
+        scratch_shapes=[
+            pltpu.VMEM((counts["mp"],) + end_parts.shape, end_parts.dtype),
+            pltpu.VMEM((rows, EMBED_DIMENSION), jnp.bfloat16),
+            pltpu.SemaphoreType.DMA((3, count)),
+            pltpu.SemaphoreType.DMA((3, count)),
+        ],
+        compiler_params=pltpu.CompilerParams(collective_id=tag, has_side_effects=True),
+    )(blocks, end_parts, skip_ends, gain)
+
+
 def body(
     skip_stream_arriving,
     chosen_specialists,
@@ -191,19 +267,17 @@
         .transpose(1, 0, 2)
         .reshape(ends_index.shape[0], EMBED_DIMENSION)
     )
-    swapped, end_partials = axis_share(
-        [(column_blocks, True), (partial_t[:, ends_index].T, False)], "mp", columns_count, 7
+    swapped, head_rows = tail_exchange(
+        column_blocks,
+        partial_t[:, ends_index].T,
+        skip_ends,
+        terminal_rmsnorm_gain[None],
+        {"mp": columns_count, "dp": groups},
+        7,
     )
     branch = jnp.sum(swapped.astype(jnp.float32), axis=0).T
     new_hidden = skip_stream_arriving + branch_scale * branch
-    end_rows = skip_ends + branch_scale * jnp.sum(end_partials.astype(jnp.float32), axis=0)
-    end_squares = jnp.sum(end_rows * end_rows, axis=1)
-    end_normed = (
-        end_rows * lax.rsqrt(end_squares / EMBED_DIMENSION + epsilon)[:, None] * terminal_rmsnorm_gain
-    ).astype(jnp.bfloat16)
-    lexicon_projector_feed = axis_gather(end_normed, "dp", groups, 2).reshape(
-        groups * end_normed.shape[0], EMBED_DIMENSION
-    )
+    lexicon_projector_feed = head_rows.reshape(groups * ends_index.shape[0], EMBED_DIMENSION)
     lexicon_logit_values = jnp.dot(
         lexicon_projector_feed, lexicon_projector_weights, preferred_element_type=jnp.float32
     ) / (EMBED_DIMENSION / 256.0 * softness_per_sequence[:, None])

time: 368 us -> 357 us (0.970)
  Pallas kernels: 265 us -> 257 us
    pallas_call x5 -> x3, Pallas kernels: 247 us -> 192 us  [axis_share(): pl.pallas_call(kernel, out_shape=[jax.ShapeDtypeStruct(array.shape if spl...]
    pallas_call x0 -> x1, Pallas kernels: none -> 46.5 us  [tail_exchange(): pl.pallas_call(kernel, out_shape=[jax.ShapeDtypeStruct(blocks.shape, bloc...]
  transfers between devices with their start and end apart: 1 -> 1, of which waited for: 1 -> 1; matrix products, arithmetic and copies ran while one was open for 5% -> 6% of each run, Pallas kernels for 52% -> 54%
where the time goes in v7:
time: 357 us; the launch traced here: 355 us
  Pallas kernels  257 us (72%)
  matrix products  38.2 us (11%)
  local copies, waits for them, and re-layouts  19.8 us (6%)
  waiting for transfers between devices  14.7 us (4%)
  between operations  14.2 us (4%)
  other arithmetic  10.6 us (3%)
    pallas_call x3, Pallas kernels, axis_share(): pl.pallas_call(kernel, out_shape=[jax.ShapeDtypeStruct(array.shape if spl...  192 us
    pallas_call x1, Pallas kernels, tail_exchange(): pl.pallas_call(kernel, out_shape=[jax.ShapeDtypeStruct(blocks.shape, bloc...  46.5 us
    dot_general x4, matrix products, body(): jnp.dot(all_weights[expert, 2], act_t, preferred_element_type=jnp.float32)  24.6 us
    pallas_call x1, Pallas kernels, stats_combine(): pl.pallas_call(kernel, out_shape=jax.ShapeDtypeStruct(tile.shape, tile.dt...  18.7 us
    all_gather x1, waiting for transfers between devices, body(): lax.all_gather(jnp.stack([specialist_switch_weights, specialist_expand_we...  14.7 us
    dot_general x4, matrix products, body(): lax.dot_general(all_weights[expert, 0], features_t, by_rows, preferred_el...  11.5 us
  transfers between devices with their start and end apart: 1, of which 1 were waited for; matrix products, arithmetic and copies ran while one was open for 6% of the time, Pallas kernels for 54%

profile of v7, /device:TPU:8, one launch (start us, length us, event | category | flops | bytes accessed | tf_op | source)
XLA Modules:
  0.0 354.5 jit_solution(9109175381314808104)
XLA Ops:
  7.2 0.0 copy-start
  7.2 0.0 all-gather.2.cloned.1.call-start
  7.2 0.0 copy-start.2
  7.2 0.0 copy-start.7
  7.2 2.8 pad_maximum_fusion
  10.1 0.0 copy-start.4
  10.1 0.0 copy-start.5
  10.1 0.0 all-gather.2.cloned.1.call-update
  10.1 0.0 copy-done.2
  10.1 0.8 copy.67
  10.9 0.6 multiply_reduce_fusion
  11.5 11.5 %shard_map.122 = f32[16,1,256]{2,1,0:T(1,128)} custom-call(f32[1,256]{1,0:T(1,128)} %bitcast.117), custom_call_target="tpu_custom_call" | custom-call | tf_op jit(solution)/shard_map/pallas_call | solution.py:52
  23.0 0.8 reduce_sum.46
  23.8 0.0 copy-done.7
  23.8 0.7 fusion.44.refs_0_
  24.5 59.8 %shard_map.123 = bf16[16,144,256]{2,1,0:T(8,128)(2,1)} custom-call(bf16[144,256]{1,0:T(8,128)(2,1)} %fusion.44.refs_0_), custom_call_target="tpu_custom_call" | custom-call | tf_op jit(solution)/shard_map/pallas_call | solution.py:52
  84.3 0.0 copy-done.4
  84.4 0.1 copy.64
  84.5 0.1 reshape.269
  84.7 0.0 copy-done.5
  84.7 1.5 fusion.58
  86.2 0.0 copy-start.1
  86.2 4.9 %gather_fusion.2 = f32[512]{0:T(512)S(1)} fusion(f32[256,4]{0,1:T(4,128)S(1)} %fusion.58, s32[512]{0:T(512)S(1)} %reshape.269), kind=kCustom, calls=%fused_computation.2 | custom fusion | bytes 8192 | tf_op jit(solution)/shard_map/jit(take_along_axis)/gather | solution.py:236
  91.1 0.8 reshape.272
  91.9 1.0 copy.65
  92.8 0.8 reduce-window.4
  93.7 2.2 gather_fusion.1
  95.9 120.4 %shard_map.124 = f32[16,4,144]{2,1,0:T(4,128)} custom-call(f32[4,144]{1,0:T(4,128)} %gather_fusion.1), custom_call_target="tpu_custom_call" | custom-call | tf_op jit(solution)/shard_map/pallas_call | solution.py:52
  216.2 1.5 copy.68
  217.7 1.6 reshape.249.skip_ref
  219.3 1.3 broadcast_in_dim.38.gain_ref
  220.6 1.2 broadcast_multiply_fusion
  221.8 0.6 fusion.50
  222.4 14.7 %all-gather.2.cloned.1.call-done = bf16[4,3,2304,360]{3,2,0,1:T(8,128)(2,1)} async-done(((bf16[4,3,144,360]{3,2,0,1:T(8,128)(2,1)}), bf16[4,3,2304,360]{3,2,0,1:T(8,128)(2,1)}) %all-gather.2.cloned.1.call-update) | async-done | bytes 19906576 | tf_op jit(solution)/shard_map/all_gather | solution.py:237
  237.1 0.0 copy-done.1
  237.1 2.9 fusion.11
  239.9 2.9 fusion.9
  242.8 2.9 fusion.7
  245.7 2.9 fusion.5
  248.6 0.0 copy-done.10
  248.6 5.7 %convolution_multiply_fusion.3 = f32[2304,256]{1,0:T(8,128)} fusion(bf16[4,3,2304,360]{3,2,0,1:T(8,128)(2,1)} %all-gather.2.cloned.1.call-done, f32[256]{0:T(256)S(1)} %bitcast.122, bf16[2304,256]{1,0:T(8,128)(2,1)S(1)} %bitcast.107, f32[360,256]{1,0:T(8,128)} %fusion.11), kind=kOutput, calls=%fused_computation.9 | convolution fusion | flops 850489344 | bytes 7447552 | tf_op jit(solution)/shard_map/dot_general | solution.py:260
  254.3 0.0 copy-done.9
  254.3 6.5 %fusion.2 = f32[2304,256]{1,0:T(8,128)} fusion(f32[2304,256]{1,0:T(8,128)} %convolution_multiply_fusion.3, bf16[4,3,2304,360]{3,2,0,1:T(8,128)(2,1)} %all-gather.2.cloned.1.call-done, f32[256]{0:T(256)S(1)} %bitcast.121, bf16[2304,256]{1,0:T(8,128)(2,1)S(1)} %bitcast.108, f32[360,256]{1,0:T(8,128)} %fusion.9), kind=kOutput, calls=%fused_computation.8 | convolution fusion | flops 851079168 | bytes 9806848 | tf_op jit(solution)/shard_map/dot_general | solution.py:260
  260.7 0.0 copy-done.8
  260.7 6.5 %fusion.1 = f32[2304,256]{1,0:T(8,128)} fusion(f32[2304,256]{1,0:T(8,128)} %fusion.2, bf16[4,3,2304,360]{3,2,0,1:T(8,128)(2,1)} %all-gather.2.cloned.1.call-done, f32[256]{0:T(256)S(1)} %bitcast.120, bf16[2304,256]{1,0:T(8,128)(2,1)S(1)} %bitcast.109, f32[360,256]{1,0:T(8,128)} %fusion.7), kind=kOutput, calls=%fused_computation.6 | convolution fusion | flops 851079168 | bytes 9806848 | tf_op jit(solution)/shard_map/dot_general | solution.py:260
  267.2 6.0 %fusion.3 = bf16[2304,256]{1,0:T(8,128)(2,1)} fusion(f32[2304,256]{1,0:T(8,128)} %fusion.1, bf16[4,3,2304,360]{3,2,0,1:T(8,128)(2,1)} %all-gather.2.cloned.1.call-done, f32[256]{0:T(256)S(1)} %bitcast.119, bf16[2304,256]{1,0:T(8,128)(2,1)S(1)} %bitcast.110, f32[360,256]{1,0:T(8,128)} %fusion.5), kind=kOutput, calls=%fused_computation.10 | convolution fusion | flops 851668992 | bytes 8627200 | tf_op jit(solution)/shard_map/dot_general | solution.py:260
  273.2 1.7 copy.66
  275.0 1.2 gather_fusion
  276.2 46.5 %shard_map.125 = (bf16[16,144,256]{2,1,0:T(8,128)(2,1)}, bf16[16,4,2304]{2,1,0:T(4,128)(2,1)}) custom-call(bf16[16,144,256]{2,1,0:T(8,128)(2,1)} %bitcast.111, bf16[4,2304]{1,0:T(4,128)(2,1)} %gather_fusion, f32[4,2304]{1,0:T(4,128)} %reshape.249.skip_ref, f32[1,2304]{1,0:T(1,128)} %broadcast_in_dim.38.gain_ref), custom_call_target="tpu_custom_call" | custom-call | tf_op jit(solution)/shard_map/pallas_call | solution.py:187
  322.7 1.0 reshape.250
  323.7 0.0 copy-done
  323.7 0.0 copy-done.11
  323.7 0.0 copy-start.3
  323.7 0.6 fusion.57
  324.4 0.2 exponential_reduce_fusion
  324.6 0.2 scatter.9.x_ref
  324.8 0.0 copy-start.6
  324.8 0.6 copy-done.6
  325.4 18.7 %shard_map.126 = f32[8,128]{1,0:T(8,128)} custom-call(f32[8,128]{1,0:T(8,128)} %copy-done.6), custom_call_target="tpu_custom_call" | custom-call | tf_op jit(solution)/shard_map/pallas_call | solution.py:113
  344.0 0.8 slice_bitcast_fusion.48
  344.8 1.4 convert_reduce_fusion
  346.2 0.0 copy-done.3
  346.2 0.7 bitcast_add_fusion
  346.9 0.7 subtract_subtract_fusion
  (12 shorter events, 0.1 us)
Async XLA Ops:
  7.2 316.5 %copy-start = (bf16[2304,512]{1,0:T(8,128)(2,1)S(1)}, bf16[2304,512]{1,0:T(8,128)(2,1)}, u32[]{:S(2)}) copy-start(bf16[2304,512]{1,0:T(8,128)(2,1)} %param.24) | copy-start | bytes 7077892
  7.2 229.9 %all-gather.2.cloned.1.call-start = ((), (), s32[]{:S(2)}) async-start(), calls=%async_computation | async-start | bytes 22560768 | tf_op jit(solution)/shard_map/all_gather | solution.py:237
  7.2 2.9 copy-start.2
  7.2 16.6 %copy-start.7 = (f32[144]{0:T(256)S(1)}, f32[144]{0:T(256)}, u32[]{:S(2)}) copy-start(f32[144]{0:T(256)} %param.18) | copy-start | bytes 1732
  10.1 74.3 %copy-start.4 = (s32[256,2]{0,1:T(2,128)S(1)}, s32[256,2]{0,1:T(2,128)}, u32[]{:S(2)}) copy-start(s32[256,2]{0,1:T(2,128)} %param.16) | copy-start | bytes 6148
  10.1 74.6 %copy-start.5 = (bf16[2304,4]{0,1:T(4,128)(2,1)S(1)}, bf16[2304,4]{0,1:T(4,128)(2,1)}, u32[]{:S(2)}) copy-start(bf16[2304,4]{0,1:T(4,128)(2,1)} %param.19) | copy-start | bytes 55300
  86.2 150.9 %copy-start.1 = (bf16[16,144,256]{2,1,0:T(8,128)(2,1)S(1)}, bf16[16,144,256]{2,1,0:T(8,128)(2,1)}, u32[]{:S(2)}) copy-start(bf16[16,144,256]{2,1,0:T(8,128)(2,1)} %shard_map.123) | copy-start | bytes 3538948
  245.7 2.9 copy-start.10
  248.6 5.7 %copy-start.9 = (f32[256,1]{0,1:T(1,128)S(1)}, f32[256,1]{0,1:T(1,128)}, u32[]{:S(2)}) copy-start(f32[256,1]{0,1:T(1,128)} %get-tuple-element.37) | copy-start | bytes 3076
  254.3 6.5 %copy-start.8 = (f32[256,1]{0,1:T(1,128)S(1)}, f32[256,1]{0,1:T(1,128)}, u32[]{:S(2)}) copy-start(f32[256,1]{0,1:T(1,128)} %get-tuple-element.35) | copy-start | bytes 3076
  276.2 47.6 %copy-start.11 = (f32[64]{0:T(128)S(1)}, f32[64]{0:T(128)}, u32[]{:S(2)}) copy-start(f32[64]{0:T(128)} %broadcast_multiply_fusion) | copy-start | bytes 772
  323.7 22.5 %copy-start.3 = (f32[256,144]{0,1:T(8,128)S(1)}, f32[256,144]{0,1:T(8,128)}, u32[]{:S(2)}) copy-start(f32[256,144]{0,1:T(8,128)} %param.15) | copy-start | bytes 442372
  324.8 0.6 copy-start.6
Sparse Core Ops, SparseCore 0:
  10.7 226.3 all-gather.1

commit v8 on v7

--- a/solution.py
+++ b/solution.py
@@ -69,7 +69,7 @@
     return axis_share([(block, False)], axis, count, tag)[0]
 
 
-def stats_combine(tile, counts, tag):
+def stats_combine(tile, blocks, counts, tag):
     axes = ("mp", "dp")
 
     def merge(buffer):
@@ -77,7 +77,7 @@
         total = jnp.sum(buffer[:, 1, :] * jnp.exp(buffer[:, 0, :] - top), axis=0, keepdims=True)
         return top, total
 
-    def kernel(x_ref, out_ref, first, second, middle, send_sem, recv_sem):
+    def kernel(x_ref, blocks_ref, out_ref, swapped_ref, first, second, middle, send_sem, recv_sem):
         barrier = pltpu.get_barrier_semaphore()
         for axis in axes:
             me = lax.axis_index(axis)
@@ -86,6 +86,17 @@
                 pl.semaphore_signal(barrier, 1, device_id={axis: peer},
                                     device_id_type=pl.DeviceIdType.MESH)
         pl.semaphore_wait(barrier, sum(counts[axis] - 1 for axis in axes))
+        column = lax.axis_index("mp")
+        block_copies = []
+        for step in range(1, counts["mp"]):
+            peer = lax.rem(column + step, counts["mp"])
+            copy = pltpu.make_async_remote_copy(
+                src_ref=blocks_ref.at[peer], dst_ref=swapped_ref.at[column],
+                send_sem=send_sem.at[2, step], recv_sem=recv_sem.at[2, step],
+                device_id={"mp": peer}, device_id_type=pl.DeviceIdType.MESH)
+            copy.start()
+            block_copies.append(copy)
+        swapped_ref[column] = blocks_ref[column]
         stages = ((x_ref, first), (middle, second))
         for index, axis in enumerate(axes):
             source, target = stages[index]
@@ -108,29 +119,34 @@
             result[...] = jnp.zeros(result.shape, result.dtype)
             result[0:1, :] = top
             result[1:2, :] = total
+        for copy in block_copies:
+            copy.wait_send()
+            copy.wait_recv()
 
     count = max(counts.values())
     return pl.pallas_call(
         kernel,
-        out_shape=jax.ShapeDtypeStruct(tile.shape, tile.dtype),
-        in_specs=[pl.BlockSpec(memory_space=pltpu.VMEM)],
-        out_specs=pl.BlockSpec(memory_space=pltpu.VMEM),
+        out_shape=[
+            jax.ShapeDtypeStruct(tile.shape, tile.dtype),
+            jax.ShapeDtypeStruct(blocks.shape, blocks.dtype),
+        ],
+        in_specs=[pl.BlockSpec(memory_space=pltpu.VMEM)] * 2,
+        out_specs=[pl.BlockSpec(memory_space=pltpu.VMEM)] * 2,
         scratch_shapes=[
             pltpu.VMEM((counts["mp"],) + tile.shape, tile.dtype),
             pltpu.VMEM((counts["dp"],) + tile.shape, tile.dtype),
             pltpu.VMEM(tile.shape, tile.dtype),
-            pltpu.SemaphoreType.DMA((2, count)),
-            pltpu.SemaphoreType.DMA((2, count)),
+            pltpu.SemaphoreType.DMA((3, count)),
+            pltpu.SemaphoreType.DMA((3, count)),
         ],
         compiler_params=pltpu.CompilerParams(collective_id=tag, has_side_effects=True),
-    )(tile)
-
-
-def tail_exchange(blocks, end_parts, skip_ends, gain, counts, tag):
+    )(tile, blocks)
+
+
+def tail_exchange(end_parts, skip_ends, gain, counts, tag):
     rows = end_parts.shape[0]
 
-    def kernel(blocks_ref, parts_ref, skip_ref, gain_ref, swapped_ref, head_ref,
-               parts_held, normed, send_sem, recv_sem):
+    def kernel(parts_ref, skip_ref, gain_ref, head_ref, parts_held, normed, send_sem, recv_sem):
         barrier = pltpu.get_barrier_semaphore()
         for axis in ("mp", "dp"):
             me = lax.axis_index(axis)
@@ -140,7 +156,7 @@
                                     device_id_type=pl.DeviceIdType.MESH)
         pl.semaphore_wait(barrier, counts["mp"] + counts["dp"] - 2)
         me = lax.axis_index("mp")
-        block_copies, part_copies = [], []
+        part_copies = []
         for step in range(1, counts["mp"]):
             peer = lax.rem(me + step, counts["mp"])
             copy = pltpu.make_async_remote_copy(
@@ -149,16 +165,7 @@
                 device_id={"mp": peer}, device_id_type=pl.DeviceIdType.MESH)
             copy.start()
             part_copies.append(copy)
-        for step in range(1, counts["mp"]):
-            peer = lax.rem(me + step, counts["mp"])
-            copy = pltpu.make_async_remote_copy(
-                src_ref=blocks_ref.at[peer], dst_ref=swapped_ref.at[me],
-                send_sem=send_sem.at[1, step], recv_sem=recv_sem.at[1, step],
-                device_id={"mp": peer}, device_id_type=pl.DeviceIdType.MESH)
-            copy.start()
-            block_copies.append(copy)
         parts_held[me] = parts_ref[...]
-        swapped_ref[me] = blocks_ref[me]
         for copy in part_copies:
             copy.wait_send()
             copy.wait_recv()
@@ -179,19 +186,16 @@
             copy.start()
             head_copies.append(copy)
         head_ref[group] = normed[...]
-        for copy in block_copies + head_copies:
+        for copy in head_copies:
             copy.wait_send()
             copy.wait_recv()
 
     count = max(counts.values())
     return pl.pallas_call(
         kernel,
-        out_shape=[
-            jax.ShapeDtypeStruct(blocks.shape, blocks.dtype),
-            jax.ShapeDtypeStruct((counts["dp"], rows, EMBED_DIMENSION), jnp.bfloat16),
-        ],
-        in_specs=[pl.BlockSpec(memory_space=pltpu.VMEM)] * 4,
-        out_specs=[pl.BlockSpec(memory_space=pltpu.VMEM)] * 2,
+        out_shape=jax.ShapeDtypeStruct((counts["dp"], rows, EMBED_DIMENSION), jnp.bfloat16),
+        in_specs=[pl.BlockSpec(memory_space=pltpu.VMEM)] * 3,
+        out_specs=pl.BlockSpec(memory_space=pltpu.VMEM),
         scratch_shapes=[
             pltpu.VMEM((counts["mp"],) + end_parts.shape, end_parts.dtype),
             pltpu.VMEM((rows, EMBED_DIMENSION), jnp.bfloat16),
@@ -199,7 +203,7 @@
             pltpu.SemaphoreType.DMA((3, count)),
         ],
         compiler_params=pltpu.CompilerParams(collective_id=tag, has_side_effects=True),
-    )(blocks, end_parts, skip_ends, gain)
+    )(end_parts, skip_ends, gain)
 
 
 def body(
@@ -267,16 +271,13 @@
         .transpose(1, 0, 2)
         .reshape(ends_index.shape[0], EMBED_DIMENSION)
     )
-    swapped, head_rows = tail_exchange(
-        column_blocks,
+    head_rows = tail_exchange(
         partial_t[:, ends_index].T,
         skip_ends,
         terminal_rmsnorm_gain[None],
         {"mp": columns_count, "dp": groups},
         7,
     )
-    branch = jnp.sum(swapped.astype(jnp.float32), axis=0).T
-    new_hidden = skip_stream_arriving + branch_scale * branch
     lexicon_projector_feed = head_rows.reshape(groups * ends_index.shape[0], EMBED_DIMENSION)
     lexicon_logit_values = jnp.dot(
         lexicon_projector_feed, lexicon_projector_weights, preferred_element_type=jnp.float32
@@ -286,7 +287,9 @@
     requests = local_max.shape[0]
     tile = jnp.zeros((8, 128), jnp.float32)
     tile = tile.at[0, :requests].set(local_max).at[1, :requests].set(local_sum)
-    merged = stats_combine(tile, {"mp": columns_count, "dp": groups}, 3)
+    merged, swapped = stats_combine(tile, column_blocks, {"mp": columns_count, "dp": groups}, 3)
+    branch = jnp.sum(swapped.astype(jnp.float32), axis=0).T
+    new_hidden = skip_stream_arriving + branch_scale * branch
     largest, total_exp = merged[0, :requests], merged[1, :requests]
     logprobs = lexicon_logit_values - largest[:, None] - jnp.log(total_exp)[:, None]
     return (new_hidden, logprobs)

time: 357 us -> 361 us (1.011)
  no operation moved by 1% of the time
where the time goes in v8:
time: 361 us; the launch traced here: 358 us
  Pallas kernels  260 us (72%)
  matrix products  38.2 us (11%)
  local copies, waits for them, and re-layouts  19.8 us (5%)
  waiting for transfers between devices  14.7 us (4%)
  between operations  14.3 us (4%)
  other arithmetic  10.6 us (3%)
    pallas_call x3, Pallas kernels, axis_share(): pl.pallas_call(kernel, out_shape=[jax.ShapeDtypeStruct(array.shape if spl...  192 us
    pallas_call x1, Pallas kernels, stats_combine(): pl.pallas_call(kernel, out_shape=[jax.ShapeDtypeStruct(tile.shape, tile.d...  46 us
    dot_general x4, matrix products, body(): jnp.dot(all_weights[expert, 2], act_t, preferred_element_type=jnp.float32)  24.6 us
    pallas_call x1, Pallas kernels, tail_exchange(): pl.pallas_call(kernel, out_shape=jax.ShapeDtypeStruct((counts['dp'], rows...  22.8 us
    all_gather x1, waiting for transfers between devices, body(): lax.all_gather(jnp.stack([specialist_switch_weights, specialist_expand_we...  14.7 us
    dot_general x4, matrix products, body(): lax.dot_general(all_weights[expert, 0], features_t, by_rows, preferred_el...  11.5 us
  transfers between devices with their start and end apart: 1, of which 1 were waited for; matrix products, arithmetic and copies ran while one was open for 6% of the time, Pallas kernels for 54%

profile of v8, /device:TPU:8, one launch (start us, length us, event | category | flops | bytes accessed | tf_op | source)
XLA Modules:
  0.0 358.1 jit_solution(14447455524674860176)
XLA Ops:
  7.2 0.0 copy-start
  7.2 0.0 all-gather.2.cloned.1.call-start
  7.2 0.0 copy-start.2
  7.2 0.0 copy-start.7
  7.2 2.8 pad_maximum_fusion
  10.1 0.0 copy-start.4
  10.1 0.0 copy-start.5
  10.1 0.0 all-gather.2.cloned.1.call-update
  10.1 0.0 copy-done.2
  10.1 0.8 copy.67
  10.9 0.6 multiply_reduce_fusion
  11.5 11.5 %shard_map.122 = f32[16,1,256]{2,1,0:T(1,128)} custom-call(f32[1,256]{1,0:T(1,128)} %bitcast.117), custom_call_target="tpu_custom_call" | custom-call | tf_op jit(solution)/shard_map/pallas_call | solution.py:52
  23.0 0.8 reduce_sum.46
  23.8 0.0 copy-done.7
  23.8 0.7 fusion.44.refs_0_
  24.5 59.8 %shard_map.123 = bf16[16,144,256]{2,1,0:T(8,128)(2,1)} custom-call(bf16[144,256]{1,0:T(8,128)(2,1)} %fusion.44.refs_0_), custom_call_target="tpu_custom_call" | custom-call | tf_op jit(solution)/shard_map/pallas_call | solution.py:52
  84.3 0.0 copy-done.4
  84.4 0.1 copy.64
  84.5 0.1 reshape.269
  84.7 0.0 copy-done.5
  84.7 1.5 fusion.58
  86.2 4.9 %gather_fusion.2 = f32[512]{0:T(512)S(1)} fusion(f32[256,4]{0,1:T(4,128)S(1)} %fusion.58, s32[512]{0:T(512)S(1)} %reshape.269), kind=kCustom, calls=%fused_computation.2 | custom fusion | bytes 8192 | tf_op jit(solution)/shard_map/jit(take_along_axis)/gather | solution.py:240
  91.1 0.8 reshape.272
  91.9 1.0 copy.65
  92.8 0.8 reduce-window.4
  93.7 2.2 gather_fusion.1
  95.9 120.4 %shard_map.124 = f32[16,4,144]{2,1,0:T(4,128)} custom-call(f32[4,144]{1,0:T(4,128)} %gather_fusion.1), custom_call_target="tpu_custom_call" | custom-call | tf_op jit(solution)/shard_map/pallas_call | solution.py:52
  216.2 1.5 copy.68
  217.7 1.6 reshape.248.skip_ref
  219.3 1.3 broadcast_in_dim.38.gain_ref
  220.6 1.2 broadcast_multiply_fusion
  221.8 0.6 fusion.50
  222.4 14.7 %all-gather.2.cloned.1.call-done = bf16[4,3,2304,360]{3,2,0,1:T(8,128)(2,1)} async-done(((bf16[4,3,144,360]{3,2,0,1:T(8,128)(2,1)}), bf16[4,3,2304,360]{3,2,0,1:T(8,128)(2,1)}) %all-gather.2.cloned.1.call-update) | async-done | bytes 19906576 | tf_op jit(solution)/shard_map/all_gather | solution.py:241
  237.1 0.0 copy-done.1
  237.1 2.9 fusion.11
  239.9 2.9 fusion.9
  242.8 2.9 fusion.7
  245.7 2.9 fusion.5
  248.6 0.0 copy-done.10
  248.6 5.7 %convolution_multiply_fusion.3 = f32[2304,256]{1,0:T(8,128)} fusion(bf16[4,3,2304,360]{3,2,0,1:T(8,128)(2,1)} %all-gather.2.cloned.1.call-done, f32[256]{0:T(256)S(1)} %bitcast.122, bf16[2304,256]{1,0:T(8,128)(2,1)S(1)} %bitcast.107, f32[360,256]{1,0:T(8,128)} %fusion.11), kind=kOutput, calls=%fused_computation.9 | convolution fusion | flops 850489344 | bytes 7447552 | tf_op jit(solution)/shard_map/dot_general | solution.py:264
  254.3 0.0 copy-done.9
  254.3 6.5 %fusion.2 = f32[2304,256]{1,0:T(8,128)} fusion(f32[2304,256]{1,0:T(8,128)} %convolution_multiply_fusion.3, bf16[4,3,2304,360]{3,2,0,1:T(8,128)(2,1)} %all-gather.2.cloned.1.call-done, f32[256]{0:T(256)S(1)} %bitcast.121, bf16[2304,256]{1,0:T(8,128)(2,1)S(1)} %bitcast.108, f32[360,256]{1,0:T(8,128)} %fusion.9), kind=kOutput, calls=%fused_computation.8 | convolution fusion | flops 851079168 | bytes 9806848 | tf_op jit(solution)/shard_map/dot_general | solution.py:264
  260.7 0.0 copy-done.8
  260.7 6.5 %fusion.1 = f32[2304,256]{1,0:T(8,128)} fusion(f32[2304,256]{1,0:T(8,128)} %fusion.2, bf16[4,3,2304,360]{3,2,0,1:T(8,128)(2,1)} %all-gather.2.cloned.1.call-done, f32[256]{0:T(256)S(1)} %bitcast.120, bf16[2304,256]{1,0:T(8,128)(2,1)S(1)} %bitcast.109, f32[360,256]{1,0:T(8,128)} %fusion.7), kind=kOutput, calls=%fused_computation.6 | convolution fusion | flops 851079168 | bytes 9806848 | tf_op jit(solution)/shard_map/dot_general | solution.py:264
  267.2 6.0 %fusion.3 = bf16[2304,256]{1,0:T(8,128)(2,1)} fusion(f32[2304,256]{1,0:T(8,128)} %fusion.1, bf16[4,3,2304,360]{3,2,0,1:T(8,128)(2,1)} %all-gather.2.cloned.1.call-done, f32[256]{0:T(256)S(1)} %bitcast.119, bf16[2304,256]{1,0:T(8,128)(2,1)S(1)} %bitcast.110, f32[360,256]{1,0:T(8,128)} %fusion.5), kind=kOutput, calls=%fused_computation.10 | convolution fusion | flops 851668992 | bytes 8627200 | tf_op jit(solution)/shard_map/dot_general | solution.py:264
  273.2 1.7 copy.66
  275.0 0.0 copy-start.11
  275.0 1.2 gather_fusion
  276.2 22.8 %shard_map.125 = bf16[16,4,2304]{2,1,0:T(4,128)(2,1)} custom-call(bf16[4,2304]{1,0:T(4,128)(2,1)} %gather_fusion, f32[4,2304]{1,0:T(4,128)} %reshape.248.skip_ref, f32[1,2304]{1,0:T(1,128)} %broadcast_in_dim.38.gain_ref), custom_call_target="tpu_custom_call" | custom-call | tf_op jit(solution)/shard_map/pallas_call | solution.py:194
  299.0 1.0 reshape.249
  300.0 0.0 copy-done
  300.0 0.0 copy-done.11
  300.0 0.6 fusion.57
  300.6 0.0 copy-start.3
  300.7 0.2 exponential_reduce_fusion
  300.9 0.2 scatter.9.x_ref
  301.1 0.0 copy-start.6
  301.1 0.6 copy-done.6
  301.6 46.0 %shard_map.126 = (f32[8,128]{1,0:T(8,128)}, bf16[16,144,256]{2,1,0:T(8,128)(2,1)}) custom-call(f32[8,128]{1,0:T(8,128)} %copy-done.6, bf16[16,144,256]{2,1,0:T(8,128)(2,1)} %bitcast.111), custom_call_target="tpu_custom_call" | custom-call | tf_op jit(solution)/shard_map/pallas_call | solution.py:127
  347.6 0.8 slice_bitcast_fusion.48
  348.4 1.4 convert_reduce_fusion
  349.8 0.0 copy-done.3
  349.8 0.7 bitcast_add_fusion
  350.5 0.7 subtract_subtract_fusion
  (12 shorter events, 0.1 us)
Async XLA Ops:
  7.2 292.8 %copy-start = (bf16[2304,512]{1,0:T(8,128)(2,1)S(1)}, bf16[2304,512]{1,0:T(8,128)(2,1)}, u32[]{:S(2)}) copy-start(bf16[2304,512]{1,0:T(8,128)(2,1)} %param.24) | copy-start | bytes 7077892
  7.2 229.9 %all-gather.2.cloned.1.call-start = ((), (), s32[]{:S(2)}) async-start(), calls=%async_computation | async-start | bytes 22560768 | tf_op jit(solution)/shard_map/all_gather | solution.py:241
  7.2 2.9 copy-start.2
  7.2 16.6 %copy-start.7 = (f32[144]{0:T(256)S(1)}, f32[144]{0:T(256)}, u32[]{:S(2)}) copy-start(f32[144]{0:T(256)} %param.18) | copy-start | bytes 1732
  10.1 74.3 %copy-start.4 = (s32[256,2]{0,1:T(2,128)S(1)}, s32[256,2]{0,1:T(2,128)}, u32[]{:S(2)}) copy-start(s32[256,2]{0,1:T(2,128)} %param.16) | copy-start | bytes 6148
  10.1 74.6 %copy-start.5 = (bf16[2304,4]{0,1:T(4,128)(2,1)S(1)}, bf16[2304,4]{0,1:T(4,128)(2,1)}, u32[]{:S(2)}) copy-start(bf16[2304,4]{0,1:T(4,128)(2,1)} %param.19) | copy-start | bytes 55300
  86.2 150.9 %copy-start.1 = (bf16[16,144,256]{2,1,0:T(8,128)(2,1)S(1)}, bf16[16,144,256]{2,1,0:T(8,128)(2,1)}, u32[]{:S(2)}) copy-start(bf16[16,144,256]{2,1,0:T(8,128)(2,1)} %shard_map.123) | copy-start | bytes 3538948
  245.7 2.9 copy-start.10
  248.6 5.7 %copy-start.9 = (f32[256,1]{0,1:T(1,128)S(1)}, f32[256,1]{0,1:T(1,128)}, u32[]{:S(2)}) copy-start(f32[256,1]{0,1:T(1,128)} %get-tuple-element.37) | copy-start | bytes 3076
  254.3 6.5 %copy-start.8 = (f32[256,1]{0,1:T(1,128)S(1)}, f32[256,1]{0,1:T(1,128)}, u32[]{:S(2)}) copy-start(f32[256,1]{0,1:T(1,128)} %get-tuple-element.35) | copy-start | bytes 3076
  275.0 25.0 %copy-start.11 = (f32[64]{0:T(128)S(1)}, f32[64]{0:T(128)}, u32[]{:S(2)}) copy-start(f32[64]{0:T(128)} %broadcast_multiply_fusion) | copy-start | bytes 772
  300.6 49.2 %copy-start.3 = (f32[256,144]{0,1:T(8,128)S(1)}, f32[256,144]{0,1:T(8,128)}, u32[]{:S(2)}) copy-start(f32[256,144]{0,1:T(8,128)} %param.15) | copy-start | bytes 442372
  301.1 0.6 copy-start.6
Sparse Core Ops, SparseCore 0:
  10.7 226.3 all-gather.1

commit v9 on v7

--- a/solution.py
+++ b/solution.py
@@ -149,16 +149,7 @@
                 device_id={"mp": peer}, device_id_type=pl.DeviceIdType.MESH)
             copy.start()
             part_copies.append(copy)
-        for step in range(1, counts["mp"]):
-            peer = lax.rem(me + step, counts["mp"])
-            copy = pltpu.make_async_remote_copy(
-                src_ref=blocks_ref.at[peer], dst_ref=swapped_ref.at[me],
-                send_sem=send_sem.at[1, step], recv_sem=recv_sem.at[1, step],
-                device_id={"mp": peer}, device_id_type=pl.DeviceIdType.MESH)
-            copy.start()
-            block_copies.append(copy)
         parts_held[me] = parts_ref[...]
-        swapped_ref[me] = blocks_ref[me]
         for copy in part_copies:
             copy.wait_send()
             copy.wait_recv()
@@ -178,7 +169,16 @@
                 device_id={"dp": peer}, device_id_type=pl.DeviceIdType.MESH)
             copy.start()
             head_copies.append(copy)
+        for step in range(1, counts["mp"]):
+            peer = lax.rem(me + step, counts["mp"])
+            copy = pltpu.make_async_remote_copy(
+                src_ref=blocks_ref.at[peer], dst_ref=swapped_ref.at[me],
+                send_sem=send_sem.at[1, step], recv_sem=recv_sem.at[1, step],
+                device_id={"mp": peer}, device_id_type=pl.DeviceIdType.MESH)
+            copy.start()
+            block_copies.append(copy)
         head_ref[group] = normed[...]
+        swapped_ref[me] = blocks_ref[me]
         for copy in block_copies + head_copies:
             copy.wait_send()
             copy.wait_recv()

time: 357 us -> 360 us (level)
  no operation moved by 1% of the time
where the time goes in v9:
time: 360 us; the launch traced here: 357 us
  Pallas kernels  259 us (72%)
  matrix products  38.2 us (11%)
  local copies, waits for them, and re-layouts  19.8 us (6%)
  waiting for transfers between devices  14.7 us (4%)
  between operations  14.2 us (4%)
  other arithmetic  10.6 us (3%)
    pallas_call x3, Pallas kernels, axis_share(): pl.pallas_call(kernel, out_shape=[jax.ShapeDtypeStruct(array.shape if spl...  192 us
    pallas_call x1, Pallas kernels, tail_exchange(): pl.pallas_call(kernel, out_shape=[jax.ShapeDtypeStruct(blocks.shape, bloc...  47.5 us
    dot_general x4, matrix products, body(): jnp.dot(all_weights[expert, 2], act_t, preferred_element_type=jnp.float32)  24.6 us
    pallas_call x1, Pallas kernels, stats_combine(): pl.pallas_call(kernel, out_shape=jax.ShapeDtypeStruct(tile.shape, tile.dt...  20 us
    all_gather x1, waiting for transfers between devices, body(): lax.all_gather(jnp.stack([specialist_switch_weights, specialist_expand_we...  14.7 us
    dot_general x4, matrix products, body(): lax.dot_general(all_weights[expert, 0], features_t, by_rows, preferred_el...  11.5 us
  transfers between devices with their start and end apart: 1, of which 1 were waited for; matrix products, arithmetic and copies ran while one was open for 6% of the time, Pallas kernels for 54%

profile of v9, /device:TPU:8, one launch (start us, length us, event | category | flops | bytes accessed | tf_op | source)
XLA Modules:
  0.0 356.9 jit_solution(4562968862162446793)
XLA Ops:
  7.2 0.0 copy-start
  7.2 0.0 all-gather.2.cloned.1.call-start
  7.2 0.0 copy-start.2
  7.2 0.0 copy-start.7
  7.2 2.8 pad_maximum_fusion
  10.1 0.0 copy-start.4
  10.1 0.0 copy-start.5
  10.1 0.0 all-gather.2.cloned.1.call-update
  10.1 0.0 copy-done.2
  10.1 0.8 copy.67
  10.9 0.6 multiply_reduce_fusion
  11.5 11.5 %shard_map.122 = f32[16,1,256]{2,1,0:T(1,128)} custom-call(f32[1,256]{1,0:T(1,128)} %bitcast.117), custom_call_target="tpu_custom_call" | custom-call | tf_op jit(solution)/shard_map/pallas_call | solution.py:52
  23.0 0.8 reduce_sum.46
  23.8 0.0 copy-done.7
  23.8 0.7 fusion.44.refs_0_
  24.5 59.8 %shard_map.123 = bf16[16,144,256]{2,1,0:T(8,128)(2,1)} custom-call(bf16[144,256]{1,0:T(8,128)(2,1)} %fusion.44.refs_0_), custom_call_target="tpu_custom_call" | custom-call | tf_op jit(solution)/shard_map/pallas_call | solution.py:52
  84.3 0.0 copy-done.4
  84.4 0.1 copy.64
  84.5 0.1 reshape.269
  84.7 0.0 copy-done.5
  84.7 1.5 fusion.58
  86.2 4.9 %gather_fusion.2 = f32[512]{0:T(512)S(1)} fusion(f32[256,4]{0,1:T(4,128)S(1)} %fusion.58, s32[512]{0:T(512)S(1)} %reshape.269), kind=kCustom, calls=%fused_computation.2 | custom fusion | bytes 8192 | tf_op jit(solution)/shard_map/jit(take_along_axis)/gather | solution.py:236
  91.1 0.8 reshape.272
  91.9 1.0 copy.65
  92.8 0.8 reduce-window.4
  93.7 2.2 gather_fusion.1
  95.9 120.4 %shard_map.124 = f32[16,4,144]{2,1,0:T(4,128)} custom-call(f32[4,144]{1,0:T(4,128)} %gather_fusion.1), custom_call_target="tpu_custom_call" | custom-call | tf_op jit(solution)/shard_map/pallas_call | solution.py:52
  216.2 1.5 copy.68
  217.7 1.6 reshape.249.skip_ref
  219.3 1.3 broadcast_in_dim.38.gain_ref
  220.6 1.2 broadcast_multiply_fusion
  221.8 0.6 fusion.50
  222.4 14.7 %all-gather.2.cloned.1.call-done = bf16[4,3,2304,360]{3,2,0,1:T(8,128)(2,1)} async-done(((bf16[4,3,144,360]{3,2,0,1:T(8,128)(2,1)}), bf16[4,3,2304,360]{3,2,0,1:T(8,128)(2,1)}) %all-gather.2.cloned.1.call-update) | async-done | bytes 19906576 | tf_op jit(solution)/shard_map/all_gather | solution.py:237
  237.1 0.0 copy-done.1
  237.1 2.9 fusion.11
  239.9 2.9 fusion.9
  242.8 2.9 fusion.7
  245.7 0.0 copy-start.10
  245.7 2.9 fusion.5
  248.6 0.0 copy-done.10
  248.6 5.7 %convolution_multiply_fusion.3 = f32[2304,256]{1,0:T(8,128)} fusion(bf16[4,3,2304,360]{3,2,0,1:T(8,128)(2,1)} %all-gather.2.cloned.1.call-done, f32[256]{0:T(256)S(1)} %bitcast.122, bf16[2304,256]{1,0:T(8,128)(2,1)S(1)} %bitcast.107, f32[360,256]{1,0:T(8,128)} %fusion.11), kind=kOutput, calls=%fused_computation.9 | convolution fusion | flops 850489344 | bytes 7447552 | tf_op jit(solution)/shard_map/dot_general | solution.py:260
  254.3 0.0 copy-done.9
  254.3 6.5 %fusion.2 = f32[2304,256]{1,0:T(8,128)} fusion(f32[2304,256]{1,0:T(8,128)} %convolution_multiply_fusion.3, bf16[4,3,2304,360]{3,2,0,1:T(8,128)(2,1)} %all-gather.2.cloned.1.call-done, f32[256]{0:T(256)S(1)} %bitcast.121, bf16[2304,256]{1,0:T(8,128)(2,1)S(1)} %bitcast.108, f32[360,256]{1,0:T(8,128)} %fusion.9), kind=kOutput, calls=%fused_computation.8 | convolution fusion | flops 851079168 | bytes 9806848 | tf_op jit(solution)/shard_map/dot_general | solution.py:260
  260.7 0.0 copy-done.8
  260.7 6.5 %fusion.1 = f32[2304,256]{1,0:T(8,128)} fusion(f32[2304,256]{1,0:T(8,128)} %fusion.2, bf16[4,3,2304,360]{3,2,0,1:T(8,128)(2,1)} %all-gather.2.cloned.1.call-done, f32[256]{0:T(256)S(1)} %bitcast.120, bf16[2304,256]{1,0:T(8,128)(2,1)S(1)} %bitcast.109, f32[360,256]{1,0:T(8,128)} %fusion.7), kind=kOutput, calls=%fused_computation.6 | convolution fusion | flops 851079168 | bytes 9806848 | tf_op jit(solution)/shard_map/dot_general | solution.py:260
  267.2 6.0 %fusion.3 = bf16[2304,256]{1,0:T(8,128)(2,1)} fusion(f32[2304,256]{1,0:T(8,128)} %fusion.1, bf16[4,3,2304,360]{3,2,0,1:T(8,128)(2,1)} %all-gather.2.cloned.1.call-done, f32[256]{0:T(256)S(1)} %bitcast.119, bf16[2304,256]{1,0:T(8,128)(2,1)S(1)} %bitcast.110, f32[360,256]{1,0:T(8,128)} %fusion.5), kind=kOutput, calls=%fused_computation.10 | convolution fusion | flops 851668992 | bytes 8627200 | tf_op jit(solution)/shard_map/dot_general | solution.py:260
  273.2 1.7 copy.66
  275.0 1.2 gather_fusion
  276.2 47.5 %shard_map.125 = (bf16[16,144,256]{2,1,0:T(8,128)(2,1)}, bf16[16,4,2304]{2,1,0:T(4,128)(2,1)}) custom-call(bf16[16,144,256]{2,1,0:T(8,128)(2,1)} %bitcast.111, bf16[4,2304]{1,0:T(4,128)(2,1)} %gather_fusion, f32[4,2304]{1,0:T(4,128)} %reshape.249.skip_ref, f32[1,2304]{1,0:T(1,128)} %broadcast_in_dim.38.gain_ref), custom_call_target="tpu_custom_call" | custom-call | tf_op jit(solution)/shard_map/pallas_call | solution.py:187
  323.7 1.0 reshape.250
  324.7 0.0 copy-done
  324.7 0.0 copy-done.11
  324.8 0.0 copy-start.3
  324.8 0.6 fusion.57
  325.4 0.2 exponential_reduce_fusion
  325.6 0.2 scatter.9.x_ref
  325.8 0.0 copy-start.6
  325.8 0.6 copy-done.6
  326.4 20.0 %shard_map.126 = f32[8,128]{1,0:T(8,128)} custom-call(f32[8,128]{1,0:T(8,128)} %copy-done.6), custom_call_target="tpu_custom_call" | custom-call | tf_op jit(solution)/shard_map/pallas_call | solution.py:113
  346.4 0.8 slice_bitcast_fusion.48
  347.1 1.4 convert_reduce_fusion
  348.6 0.0 copy-done.3
  348.6 0.7 bitcast_add_fusion
  349.3 0.7 subtract_subtract_fusion
  (12 shorter events, 0.1 us)
Async XLA Ops:
  7.2 317.6 %copy-start = (bf16[2304,512]{1,0:T(8,128)(2,1)S(1)}, bf16[2304,512]{1,0:T(8,128)(2,1)}, u32[]{:S(2)}) copy-start(bf16[2304,512]{1,0:T(8,128)(2,1)} %param.24) | copy-start | bytes 7077892
  7.2 229.9 %all-gather.2.cloned.1.call-start = ((), (), s32[]{:S(2)}) async-start(), calls=%async_computation | async-start | bytes 22560768 | tf_op jit(solution)/shard_map/all_gather | solution.py:237
  7.2 2.9 copy-start.2
  7.2 16.6 %copy-start.7 = (f32[144]{0:T(256)S(1)}, f32[144]{0:T(256)}, u32[]{:S(2)}) copy-start(f32[144]{0:T(256)} %param.18) | copy-start | bytes 1732
  10.1 74.3 %copy-start.4 = (s32[256,2]{0,1:T(2,128)S(1)}, s32[256,2]{0,1:T(2,128)}, u32[]{:S(2)}) copy-start(s32[256,2]{0,1:T(2,128)} %param.16) | copy-start | bytes 6148
  10.1 74.6 %copy-start.5 = (bf16[2304,4]{0,1:T(4,128)(2,1)S(1)}, bf16[2304,4]{0,1:T(4,128)(2,1)}, u32[]{:S(2)}) copy-start(bf16[2304,4]{0,1:T(4,128)(2,1)} %param.19) | copy-start | bytes 55300
  86.2 150.9 %copy-start.1 = (bf16[16,144,256]{2,1,0:T(8,128)(2,1)S(1)}, bf16[16,144,256]{2,1,0:T(8,128)(2,1)}, u32[]{:S(2)}) copy-start(bf16[16,144,256]{2,1,0:T(8,128)(2,1)} %shard_map.123) | copy-start | bytes 3538948
  245.7 2.9 copy-start.10
  248.6 5.7 %copy-start.9 = (f32[256,1]{0,1:T(1,128)S(1)}, f32[256,1]{0,1:T(1,128)}, u32[]{:S(2)}) copy-start(f32[256,1]{0,1:T(1,128)} %get-tuple-element.37) | copy-start | bytes 3076
  254.3 6.5 %copy-start.8 = (f32[256,1]{0,1:T(1,128)S(1)}, f32[256,1]{0,1:T(1,128)}, u32[]{:S(2)}) copy-start(f32[256,1]{0,1:T(1,128)} %get-tuple-element.35) | copy-start | bytes 3076
  276.2 48.6 %copy-start.11 = (f32[64]{0:T(128)S(1)}, f32[64]{0:T(128)}, u32[]{:S(2)}) copy-start(f32[64]{0:T(128)} %broadcast_multiply_fusion) | copy-start | bytes 772
  324.8 23.8 %copy-start.3 = (f32[256,144]{0,1:T(8,128)S(1)}, f32[256,144]{0,1:T(8,128)}, u32[]{:S(2)}) copy-start(f32[256,144]{0,1:T(8,128)} %param.15) | copy-start | bytes 442372
  325.8 0.6 copy-start.6
Sparse Core Ops, SparseCore 0:
  10.7 226.3 all-gather.1

commit v10 on v7

--- a/solution.py
+++ b/solution.py
@@ -220,7 +220,13 @@
     columns_count = lax.axis_size("mp")
     groups = lax.axis_size("dp")
     local_squares = jnp.sum(skip_stream_arriving * skip_stream_arriving, axis=1)
-    squares = jnp.sum(axis_gather(local_squares[None], "mp", columns_count, 0), axis=(0, 1))
+    ends_index = jnp.cumsum(sequence_piece_tallies[0], dtype=jnp.int32) - 1
+    held_squares, skip_ends = axis_share(
+        [(local_squares[None], False), (skip_stream_arriving[ends_index], False)],
+        "mp", columns_count, 0,
+    )
+    squares = jnp.sum(held_squares, axis=(0, 1))
+    skip_ends = skip_ends.transpose(1, 0, 2).reshape(ends_index.shape[0], EMBED_DIMENSION)
     normed_local = (
         skip_stream_arriving
         * lax.rsqrt(squares / EMBED_DIMENSION + epsilon)[:, None]
@@ -259,14 +265,8 @@
         act_t = (jax.nn.silu(gate_t) * up_t).astype(jnp.bfloat16)
         down_t = jnp.dot(all_weights[expert, 2], act_t, preferred_element_type=jnp.float32)
         combined_t = combined_t + down_t * weight[None, :]
-    ends_index = jnp.cumsum(sequence_piece_tallies[0], dtype=jnp.int32) - 1
     partial_t = combined_t.astype(jnp.bfloat16)
     column_blocks = partial_t.reshape(columns_count, -1, tok_rows)
-    skip_ends = (
-        axis_gather(skip_stream_arriving[ends_index], "mp", columns_count, 6)
-        .transpose(1, 0, 2)
-        .reshape(ends_index.shape[0], EMBED_DIMENSION)
-    )
     swapped, head_rows = tail_exchange(
         column_blocks,
         partial_t[:, ends_index].T,

time: 357 us -> 358 us (level)
  waiting for transfers between devices: 14.7 us -> 143 us
  Pallas kernels: 257 us -> 135 us
  local copies, waits for them, and re-layouts: 19.8 us -> 15 us
    all_gather x1, waiting for transfers between devices: 14.7 us -> 143 us  [body(): lax.all_gather(jnp.stack([specialist_switch_weights, specialist_expand_we...]
    pallas_call x3 -> x2, Pallas kernels: 192 us -> 69.5 us  [axis_share(): pl.pallas_call(kernel, out_shape=[jax.ShapeDtypeStruct(array.shape if spl...]
  transfers between devices with their start and end apart: 1 -> 1, of which waited for: 1 -> 1; matrix products, arithmetic and copies ran while one was open for 6% -> 5% of each run, Pallas kernels for 54% -> 20%
where the time goes in v10:
time: 358 us; the launch traced here: 355 us
  waiting for transfers between devices  143 us (40%)
  Pallas kernels  135 us (38%)
  matrix products  38.3 us (11%)
  local copies, waits for them, and re-layouts  15 us (4%)
  between operations  14.3 us (4%)
  other arithmetic  9.99 us (3%)
    all_gather x1, waiting for transfers between devices, body(): lax.all_gather(jnp.stack([specialist_switch_weights, specialist_expand_we...  143 us
    pallas_call x2, Pallas kernels, axis_share(): pl.pallas_call(kernel, out_shape=[jax.ShapeDtypeStruct(array.shape if spl...  69.5 us
    pallas_call x1, Pallas kernels, tail_exchange(): pl.pallas_call(kernel, out_shape=[jax.ShapeDtypeStruct(blocks.shape, bloc...  46.5 us
    dot_general x4, matrix products, body(): jnp.dot(all_weights[expert, 2], act_t, preferred_element_type=jnp.float32)  24.6 us
    pallas_call x1, Pallas kernels, stats_combine(): pl.pallas_call(kernel, out_shape=jax.ShapeDtypeStruct(tile.shape, tile.dt...  18.7 us
    dot_general x4, matrix products, body(): lax.dot_general(all_weights[expert, 0], features_t, by_rows, preferred_el...  11.6 us
  transfers between devices with their start and end apart: 1, of which 1 were waited for; matrix products, arithmetic and copies ran while one was open for 5% of the time, Pallas kernels for 20%

profile of v10, /device:TPU:8, one launch (start us, length us, event | category | flops | bytes accessed | tf_op | source)
XLA Modules:
  0.0 354.9 jit_solution(17068856176677795673)
XLA Ops:
  7.2 0.0 copy-start
  7.2 0.0 all-gather.2.cloned.1.call-start
  7.2 0.0 copy-start.8
  7.2 0.0 copy-start.5
  7.2 0.0 copy-start.2
  7.3 0.0 copy-start.13
  7.3 2.8 pad_maximum_fusion
  10.1 0.0 all-gather.2.cloned.1.call-update
  10.1 0.0 copy-done.8
  10.1 0.6 broadcast_in_dim.38.gain_ref
  10.7 0.0 copy-done.5
  10.7 0.1 copy.65
  10.9 0.1 reshape.269
  11.0 0.0 copy-done.2
  11.0 0.1 copy.64
  11.2 0.0 copy-done.13
  11.2 0.2 reduce-window.4
  11.4 1.1 gather_fusion
  12.5 0.6 multiply_reduce_fusion
  13.1 12.3 %shard_map.122 = (f32[16,1,256]{2,1,0:T(1,128)}, f32[16,4,144]{2,1,0:T(4,128)}) custom-call(f32[1,256]{1,0:T(1,128)} %bitcast.117, f32[4,144]{1,0:T(4,128)} %gather_fusion), custom_call_target="tpu_custom_call" | custom-call | tf_op jit(solution)/shard_map/pallas_call | solution.py:52
  25.4 0.9 copy.68
  26.3 0.7 reshape.249.skip_ref
  27.0 0.8 reduce_sum.46
  27.8 0.0 copy-done.10
  27.8 0.7 fusion.44.refs_0_
  28.5 57.2 %shard_map.123 = bf16[16,144,256]{2,1,0:T(8,128)(2,1)} custom-call(bf16[144,256]{1,0:T(8,128)(2,1)} %fusion.44.refs_0_), custom_call_target="tpu_custom_call" | custom-call | tf_op jit(solution)/shard_map/pallas_call | solution.py:52
  85.7 0.0 copy-done.9
  85.7 0.0 copy-done.6
  85.7 1.5 fusion.58
  87.2 5.0 %gather_fusion.2 = f32[512]{0:T(512)S(1)} fusion(f32[256,4]{0,1:T(4,128)S(1)} %fusion.58, s32[512]{0:T(512)S(1)} %reshape.269), kind=kCustom, calls=%fused_computation.2 | custom fusion | bytes 8192 | tf_op jit(solution)/shard_map/jit(take_along_axis)/gather | solution.py:242
  92.2 0.8 reshape.272
  93.0 1.0 copy.66
  94.0 1.2 broadcast_multiply_fusion
  95.2 0.6 fusion.50
  95.8 142.5 %all-gather.2.cloned.1.call-done = bf16[4,3,2304,360]{3,2,0,1:T(8,128)(2,1)} async-done(((bf16[4,3,144,360]{3,2,0,1:T(8,128)(2,1)}), bf16[4,3,2304,360]{3,2,0,1:T(8,128)(2,1)}) %all-gather.2.cloned.1.call-update) | async-done | bytes 19906576 | tf_op jit(solution)/shard_map/all_gather | solution.py:243
  238.3 0.0 copy-done.1
  238.3 2.9 fusion.7
  241.2 2.9 fusion.9
  244.1 2.9 fusion.5
  247.0 2.9 fusion.11
  249.9 0.0 copy-done.11
  249.9 5.7 %convolution_multiply_fusion.3 = f32[2304,256]{1,0:T(8,128)} fusion(bf16[4,3,2304,360]{3,2,0,1:T(8,128)(2,1)} %all-gather.2.cloned.1.call-done, f32[256]{0:T(256)S(1)} %bitcast.122, bf16[2304,256]{1,0:T(8,128)(2,1)S(1)} %bitcast.107, f32[360,256]{1,0:T(8,128)} %fusion.11), kind=kOutput, calls=%fused_computation.9 | convolution fusion | flops 850489344 | bytes 7447552 | tf_op jit(solution)/shard_map/dot_general | solution.py:266
  255.6 6.5 %fusion.2 = f32[2304,256]{1,0:T(8,128)} fusion(f32[2304,256]{1,0:T(8,128)} %convolution_multiply_fusion.3, bf16[4,3,2304,360]{3,2,0,1:T(8,128)(2,1)} %all-gather.2.cloned.1.call-done, f32[256]{0:T(256)S(1)} %bitcast.121, bf16[2304,256]{1,0:T(8,128)(2,1)S(1)} %bitcast.108, f32[360,256]{1,0:T(8,128)} %fusion.9), kind=kOutput, calls=%fused_computation.8 | convolution fusion | flops 851079168 | bytes 9806848 | tf_op jit(solution)/shard_map/dot_general | solution.py:266
  262.0 6.5 %fusion.1 = f32[2304,256]{1,0:T(8,128)} fusion(f32[2304,256]{1,0:T(8,128)} %fusion.2, bf16[4,3,2304,360]{3,2,0,1:T(8,128)(2,1)} %all-gather.2.cloned.1.call-done, f32[256]{0:T(256)S(1)} %bitcast.120, bf16[2304,256]{1,0:T(8,128)(2,1)S(1)} %bitcast.109, f32[360,256]{1,0:T(8,128)} %fusion.7), kind=kOutput, calls=%fused_computation.6 | convolution fusion | flops 851079168 | bytes 9806848 | tf_op jit(solution)/shard_map/dot_general | solution.py:266
  268.5 6.0 %fusion.3 = bf16[2304,256]{1,0:T(8,128)(2,1)} fusion(f32[2304,256]{1,0:T(8,128)} %fusion.1, bf16[4,3,2304,360]{3,2,0,1:T(8,128)(2,1)} %all-gather.2.cloned.1.call-done, f32[256]{0:T(256)S(1)} %bitcast.119, bf16[2304,256]{1,0:T(8,128)(2,1)S(1)} %bitcast.110, f32[360,256]{1,0:T(8,128)} %fusion.5), kind=kOutput, calls=%fused_computation.10 | convolution fusion | flops 851668992 | bytes 8627200 | tf_op jit(solution)/shard_map/dot_general | solution.py:266
  274.5 1.6 copy.67
  276.1 1.3 gather_fusion.1
  277.4 46.5 %shard_map.124 = (bf16[16,144,256]{2,1,0:T(8,128)(2,1)}, bf16[16,4,2304]{2,1,0:T(4,128)(2,1)}) custom-call(bf16[16,144,256]{2,1,0:T(8,128)(2,1)} %bitcast.111, bf16[4,2304]{1,0:T(4,128)(2,1)} %gather_fusion.1, f32[4,2304]{1,0:T(4,128)} %reshape.249.skip_ref, f32[1,2304]{1,0:T(1,128)} %broadcast_in_dim.38.gain_ref), custom_call_target="tpu_custom_call" | custom-call | tf_op jit(solution)/shard_map/pallas_call | solution.py:187
  324.0 0.0 copy-start.4
  324.0 1.5 convert_reduce_fusion
  325.5 0.0 copy-done.3
  325.5 0.7 bitcast_add_fusion
  326.1 0.0 copy-done.4
  326.1 0.1 reshape.250
  326.2 0.0 copy-done
  326.2 0.0 copy-done.12
  326.2 0.6 fusion.57
  326.9 0.2 exponential_reduce_fusion
  327.1 0.2 scatter.9.x_ref
  327.3 0.0 copy-start.7
  327.3 0.6 copy-done.7
  327.9 18.7 %shard_map.125 = f32[8,128]{1,0:T(8,128)} custom-call(f32[8,128]{1,0:T(8,128)} %copy-done.7), custom_call_target="tpu_custom_call" | custom-call | tf_op jit(solution)/shard_map/pallas_call | solution.py:113
  346.5 0.8 slice_bitcast_fusion.48
  347.3 0.7 subtract_subtract_fusion
  (15 shorter events, 0.1 us)
Async XLA Ops:
  7.2 319.1 %copy-start = (bf16[2304,512]{1,0:T(8,128)(2,1)S(1)}, bf16[2304,512]{1,0:T(8,128)(2,1)}, u32[]{:S(2)}) copy-start(bf16[2304,512]{1,0:T(8,128)(2,1)} %param.24) | copy-start | bytes 7077892
  7.2 231.1 %all-gather.2.cloned.1.call-start = ((), (), s32[]{:S(2)}) async-start(), calls=%async_computation | async-start | bytes 22560768 | tf_op jit(solution)/shard_map/all_gather | solution.py:243
  7.2 2.9 copy-start.8
  7.2 3.5 copy-start.5
  7.2 3.8 %copy-start.2 = (f32[256,144]{0,1:T(8,128)S(1)}, f32[256,144]{0,1:T(8,128)}, u32[]{:S(2)}) copy-start(f32[256,144]{0,1:T(8,128)} %param.15) | copy-start | bytes 442372
  7.3 3.9 %copy-start.13 = (s32[1,4]{1,0:T(1,128)S(1)}, s32[1,4]{1,0:T(1,128)}, u32[]{:S(2)}) copy-start(s32[1,4]{1,0:T(1,128)} %param.17) | copy-start | bytes 52
  10.1 17.7 %copy-start.10 = (f32[144]{0:T(256)S(1)}, f32[144]{0:T(256)}, u32[]{:S(2)}) copy-start(f32[144]{0:T(256)} %param.18) | copy-start | bytes 1732
  10.1 75.6 %copy-start.6 = (bf16[2304,4]{0,1:T(4,128)(2,1)S(1)}, bf16[2304,4]{0,1:T(4,128)(2,1)}, u32[]{:S(2)}) copy-start(bf16[2304,4]{0,1:T(4,128)(2,1)} %param.19) | copy-start | bytes 55300
  11.4 74.3 %copy-start.9 = (s32[1024]{0:T(1024)}, s32[1024]{0:T(1024)S(1)}, u32[]{:S(2)}) copy-start(s32[1024]{0:T(1024)S(1)} %pad_clamp_fusion) | copy-start | bytes 12292
  87.2 151.1 %copy-start.1 = (bf16[16,144,256]{2,1,0:T(8,128)(2,1)S(1)}, bf16[16,144,256]{2,1,0:T(8,128)(2,1)}, u32[]{:S(2)}) copy-start(bf16[16,144,256]{2,1,0:T(8,128)(2,1)} %shard_map.123) | copy-start | bytes 3538948
  247.0 2.9 copy-start.11
  277.4 48.1 %copy-start.3 = (f32[256,144]{0,1:T(8,128)S(1)}, f32[256,144]{0,1:T(8,128)}, u32[]{:S(2)}) copy-start(f32[256,144]{0,1:T(8,128)} %param.15) | copy-start | bytes 442372
  277.4 48.8 %copy-start.12 = (f32[64]{0:T(128)S(1)}, f32[64]{0:T(128)}, u32[]{:S(2)}) copy-start(f32[64]{0:T(128)} %broadcast_multiply_fusion) | copy-start | bytes 772
  324.0 2.2 copy-start.4
  327.3 0.6 copy-start.7
Sparse Core Ops, SparseCore 0:
  10.7 227.5 all-gather.1

commit v11 on v10

--- a/solution.py
+++ b/solution.py
@@ -149,14 +149,20 @@
                 device_id={"mp": peer}, device_id_type=pl.DeviceIdType.MESH)
             copy.start()
             part_copies.append(copy)
-        for step in range(1, counts["mp"]):
-            peer = lax.rem(me + step, counts["mp"])
-            copy = pltpu.make_async_remote_copy(
-                src_ref=blocks_ref.at[peer], dst_ref=swapped_ref.at[me],
-                send_sem=send_sem.at[1, step], recv_sem=recv_sem.at[1, step],
-                device_id={"mp": peer}, device_id_type=pl.DeviceIdType.MESH)
-            copy.start()
-            block_copies.append(copy)
+        width = blocks.shape[2] // 2
+
+        def send_blocks(half, slot):
+            for step in range(1, counts["mp"]):
+                peer = lax.rem(me + step, counts["mp"])
+                lanes = pl.ds(half * width, width)
+                copy = pltpu.make_async_remote_copy(
+                    src_ref=blocks_ref.at[peer, :, lanes], dst_ref=swapped_ref.at[me, :, lanes],
+                    send_sem=send_sem.at[slot, step], recv_sem=recv_sem.at[slot, step],
+                    device_id={"mp": peer}, device_id_type=pl.DeviceIdType.MESH)
+                copy.start()
+                block_copies.append(copy)
+
+        send_blocks(0, 1)
         parts_held[me] = parts_ref[...]
         swapped_ref[me] = blocks_ref[me]
         for copy in part_copies:
@@ -178,6 +184,7 @@
                 device_id={"dp": peer}, device_id_type=pl.DeviceIdType.MESH)
             copy.start()
             head_copies.append(copy)
+        send_blocks(1, 3)
         head_ref[group] = normed[...]
         for copy in block_copies + head_copies:
             copy.wait_send()
@@ -195,8 +202,8 @@
         scratch_shapes=[
             pltpu.VMEM((counts["mp"],) + end_parts.shape, end_parts.dtype),
             pltpu.VMEM((rows, EMBED_DIMENSION), jnp.bfloat16),
-            pltpu.SemaphoreType.DMA((3, count)),
-            pltpu.SemaphoreType.DMA((3, count)),
+            pltpu.SemaphoreType.DMA((4, count)),
+            pltpu.SemaphoreType.DMA((4, count)),
         ],
         compiler_params=pltpu.CompilerParams(collective_id=tag, has_side_effects=True),
     )(blocks, end_parts, skip_ends, gain)

time: 358 us -> 358 us (level)
  no operation moved by 1% of the time
where the time goes in v11:
time: 358 us; the launch traced here: 355 us
  waiting for transfers between devices  143 us (40%)
  Pallas kernels  135 us (38%)
  matrix products  38.3 us (11%)
  local copies, waits for them, and re-layouts  15.2 us (4%)
  between operations  14.3 us (4%)
  other arithmetic  9.99 us (3%)
    all_gather x1, waiting for transfers between devices, body(): lax.all_gather(jnp.stack([specialist_switch_weights, specialist_expand_we...  143 us
    pallas_call x2, Pallas kernels, axis_share(): pl.pallas_call(kernel, out_shape=[jax.ShapeDtypeStruct(array.shape if spl...  69.5 us
    pallas_call x1, Pallas kernels, tail_exchange(): pl.pallas_call(kernel, out_shape=[jax.ShapeDtypeStruct(blocks.shape, bloc...  47.3 us
    dot_general x4, matrix products, body(): jnp.dot(all_weights[expert, 2], act_t, preferred_element_type=jnp.float32)  24.6 us
    pallas_call x1, Pallas kernels, stats_combine(): pl.pallas_call(kernel, out_shape=jax.ShapeDtypeStruct(tile.shape, tile.dt...  18.1 us
    dot_general x4, matrix products, body(): lax.dot_general(all_weights[expert, 0], features_t, by_rows, preferred_el...  11.6 us
  transfers between devices with their start and end apart: 1, of which 1 were waited for; matrix products, arithmetic and copies ran while one was open for 5% of the time, Pallas kernels for 20%

profile of v11, /device:TPU:8, one launch (start us, length us, event | category | flops | bytes accessed | tf_op | source)
XLA Modules:
  0.0 355.4 jit_solution(6121204773693092703)
XLA Ops:
  7.2 0.0 copy-start
  7.2 0.0 all-gather.2.cloned.1.call-start
  7.2 0.0 copy-start.8
  7.2 0.0 copy-start.5
  7.2 0.0 copy-start.2
  7.3 0.0 copy-start.13
  7.3 2.8 pad_maximum_fusion
  10.1 0.0 all-gather.2.cloned.1.call-update
  10.1 0.0 copy-done.8
  10.1 0.6 broadcast_in_dim.38.gain_ref
  10.7 0.0 copy-done.5
  10.7 0.1 copy.65
  10.9 0.1 reshape.269
  11.0 0.0 copy-done.2
  11.0 0.1 copy.64
  11.2 0.0 copy-done.13
  11.2 0.2 reduce-window.4
  11.4 1.1 gather_fusion
  12.5 0.6 multiply_reduce_fusion
  13.1 12.3 %shard_map.122 = (f32[16,1,256]{2,1,0:T(1,128)}, f32[16,4,144]{2,1,0:T(4,128)}) custom-call(f32[1,256]{1,0:T(1,128)} %bitcast.117, f32[4,144]{1,0:T(4,128)} %gather_fusion), custom_call_target="tpu_custom_call" | custom-call | tf_op jit(solution)/shard_map/pallas_call | solution.py:52
  25.4 0.9 copy.68
  26.3 0.7 reshape.249.skip_ref
  27.0 0.8 reduce_sum.46
  27.8 0.0 copy-done.10
  27.8 0.7 fusion.44.refs_0_
  28.5 57.2 %shard_map.123 = bf16[16,144,256]{2,1,0:T(8,128)(2,1)} custom-call(bf16[144,256]{1,0:T(8,128)(2,1)} %fusion.44.refs_0_), custom_call_target="tpu_custom_call" | custom-call | tf_op jit(solution)/shard_map/pallas_call | solution.py:52
  85.7 0.0 copy-done.9
  85.7 0.0 copy-done.6
  85.7 1.5 fusion.58
  87.2 5.0 %gather_fusion.2 = f32[512]{0:T(512)S(1)} fusion(f32[256,4]{0,1:T(4,128)S(1)} %fusion.58, s32[512]{0:T(512)S(1)} %reshape.269), kind=kCustom, calls=%fused_computation.2 | custom fusion | bytes 8192 | tf_op jit(solution)/shard_map/jit(take_along_axis)/gather | solution.py:249
  92.2 0.8 reshape.272
  93.0 1.0 copy.66
  94.0 1.2 broadcast_multiply_fusion
  95.2 0.6 fusion.50
  95.8 142.5 %all-gather.2.cloned.1.call-done = bf16[4,3,2304,360]{3,2,0,1:T(8,128)(2,1)} async-done(((bf16[4,3,144,360]{3,2,0,1:T(8,128)(2,1)}), bf16[4,3,2304,360]{3,2,0,1:T(8,128)(2,1)}) %all-gather.2.cloned.1.call-update) | async-done | bytes 19906576 | tf_op jit(solution)/shard_map/all_gather | solution.py:250
  238.3 0.0 copy-done.1
  238.3 2.9 fusion.7
  241.2 2.9 fusion.9
  244.1 2.9 fusion.5
  247.0 2.9 fusion.11
  249.9 0.0 copy-done.11
  249.9 5.7 %convolution_multiply_fusion.3 = f32[2304,256]{1,0:T(8,128)} fusion(bf16[4,3,2304,360]{3,2,0,1:T(8,128)(2,1)} %all-gather.2.cloned.1.call-done, f32[256]{0:T(256)S(1)} %bitcast.122, bf16[2304,256]{1,0:T(8,128)(2,1)S(1)} %bitcast.107, f32[360,256]{1,0:T(8,128)} %fusion.11), kind=kOutput, calls=%fused_computation.9 | convolution fusion | flops 850489344 | bytes 7447552 | tf_op jit(solution)/shard_map/dot_general | solution.py:273
  255.6 6.5 %fusion.2 = f32[2304,256]{1,0:T(8,128)} fusion(f32[2304,256]{1,0:T(8,128)} %convolution_multiply_fusion.3, bf16[4,3,2304,360]{3,2,0,1:T(8,128)(2,1)} %all-gather.2.cloned.1.call-done, f32[256]{0:T(256)S(1)} %bitcast.121, bf16[2304,256]{1,0:T(8,128)(2,1)S(1)} %bitcast.108, f32[360,256]{1,0:T(8,128)} %fusion.9), kind=kOutput, calls=%fused_computation.8 | convolution fusion | flops 851079168 | bytes 9806848 | tf_op jit(solution)/shard_map/dot_general | solution.py:273
  262.0 6.5 %fusion.1 = f32[2304,256]{1,0:T(8,128)} fusion(f32[2304,256]{1,0:T(8,128)} %fusion.2, bf16[4,3,2304,360]{3,2,0,1:T(8,128)(2,1)} %all-gather.2.cloned.1.call-done, f32[256]{0:T(256)S(1)} %bitcast.120, bf16[2304,256]{1,0:T(8,128)(2,1)S(1)} %bitcast.109, f32[360,256]{1,0:T(8,128)} %fusion.7), kind=kOutput, calls=%fused_computation.6 | convolution fusion | flops 851079168 | bytes 9806848 | tf_op jit(solution)/shard_map/dot_general | solution.py:273
  268.5 6.0 %fusion.3 = bf16[2304,256]{1,0:T(8,128)(2,1)} fusion(f32[2304,256]{1,0:T(8,128)} %fusion.1, bf16[4,3,2304,360]{3,2,0,1:T(8,128)(2,1)} %all-gather.2.cloned.1.call-done, f32[256]{0:T(256)S(1)} %bitcast.119, bf16[2304,256]{1,0:T(8,128)(2,1)S(1)} %bitcast.110, f32[360,256]{1,0:T(8,128)} %fusion.5), kind=kOutput, calls=%fused_computation.10 | convolution fusion | flops 851668992 | bytes 8627200 | tf_op jit(solution)/shard_map/dot_general | solution.py:273
  274.5 1.8 copy.67
  276.3 1.3 gather_fusion.1
  277.6 47.3 %shard_map.124 = (bf16[16,144,256]{2,1,0:T(8,128)(2,1)}, bf16[16,4,2304]{2,1,0:T(4,128)(2,1)}) custom-call(bf16[16,144,256]{2,1,0:T(8,128)(2,1)} %bitcast.111, bf16[4,2304]{1,0:T(4,128)(2,1)} %gather_fusion.1, f32[4,2304]{1,0:T(4,128)} %reshape.249.skip_ref, f32[1,2304]{1,0:T(1,128)} %broadcast_in_dim.38.gain_ref), custom_call_target="tpu_custom_call" | custom-call | tf_op jit(solution)/shard_map/pallas_call | solution.py:194
  325.0 0.0 copy-start.4
  325.0 1.5 convert_reduce_fusion
  326.5 0.0 copy-done.3
  326.5 0.7 bitcast_add_fusion
  327.2 0.0 copy-done.4
  327.2 0.1 reshape.250
  327.2 0.0 copy-done
  327.3 0.0 copy-done.12
  327.3 0.6 fusion.57
  327.9 0.2 exponential_reduce_fusion
  328.1 0.2 scatter.9.x_ref
  328.3 0.0 copy-start.7
  328.3 0.6 copy-done.7
  328.9 18.1 %shard_map.125 = f32[8,128]{1,0:T(8,128)} custom-call(f32[8,128]{1,0:T(8,128)} %copy-done.7), custom_call_target="tpu_custom_call" | custom-call | tf_op jit(solution)/shard_map/pallas_call | solution.py:113
  347.0 0.8 slice_bitcast_fusion.48
  347.8 0.7 subtract_subtract_fusion
  (15 shorter events, 0.1 us)
Async XLA Ops:
  7.2 320.1 %copy-start = (bf16[2304,512]{1,0:T(8,128)(2,1)S(1)}, bf16[2304,512]{1,0:T(8,128)(2,1)}, u32[]{:S(2)}) copy-start(bf16[2304,512]{1,0:T(8,128)(2,1)} %param.24) | copy-start | bytes 7077892
  7.2 231.1 %all-gather.2.cloned.1.call-start = ((), (), s32[]{:S(2)}) async-start(), calls=%async_computation | async-start | bytes 22560768 | tf_op jit(solution)/shard_map/all_gather | solution.py:250
  7.2 2.9 copy-start.8
  7.2 3.5 copy-start.5
  7.2 3.8 %copy-start.2 = (f32[256,144]{0,1:T(8,128)S(1)}, f32[256,144]{0,1:T(8,128)}, u32[]{:S(2)}) copy-start(f32[256,144]{0,1:T(8,128)} %param.15) | copy-start | bytes 442372
  7.3 3.9 %copy-start.13 = (s32[1,4]{1,0:T(1,128)S(1)}, s32[1,4]{1,0:T(1,128)}, u32[]{:S(2)}) copy-start(s32[1,4]{1,0:T(1,128)} %param.17) | copy-start | bytes 52
  10.1 17.7 %copy-start.10 = (f32[144]{0:T(256)S(1)}, f32[144]{0:T(256)}, u32[]{:S(2)}) copy-start(f32[144]{0:T(256)} %param.18) | copy-start | bytes 1732
  10.1 75.6 %copy-start.6 = (bf16[2304,4]{0,1:T(4,128)(2,1)S(1)}, bf16[2304,4]{0,1:T(4,128)(2,1)}, u32[]{:S(2)}) copy-start(bf16[2304,4]{0,1:T(4,128)(2,1)} %param.19) | copy-start | bytes 55300
  11.4 74.3 %copy-start.9 = (s32[1024]{0:T(1024)}, s32[1024]{0:T(1024)S(1)}, u32[]{:S(2)}) copy-start(s32[1024]{0:T(1024)S(1)} %pad_clamp_fusion) | copy-start | bytes 12292
  87.2 151.1 %copy-start.1 = (bf16[16,144,256]{2,1,0:T(8,128)(2,1)S(1)}, bf16[16,144,256]{2,1,0:T(8,128)(2,1)}, u32[]{:S(2)}) copy-start(bf16[16,144,256]{2,1,0:T(8,128)(2,1)} %shard_map.123) | copy-start | bytes 3538948
  247.0 2.9 copy-start.11
  277.6 48.9 %copy-start.3 = (f32[256,144]{0,1:T(8,128)S(1)}, f32[256,144]{0,1:T(8,128)}, u32[]{:S(2)}) copy-start(f32[256,144]{0,1:T(8,128)} %param.15) | copy-start | bytes 442372
  277.6 49.6 %copy-start.12 = (f32[64]{0:T(128)S(1)}, f32[64]{0:T(128)}, u32[]{:S(2)}) copy-start(f32[64]{0:T(128)} %broadcast_multiply_fusion) | copy-start | bytes 772
  325.0 2.2 copy-start.4
  328.3 0.6 copy-start.7
Sparse Core Ops, SparseCore 0:
  10.7 227.5 all-gather.1
